TPU v7x, 32 devices: a whole 2x2x4 slice. The times are simulated.
32 devices in a mesh: rep: 8 (over z, x), exp: 4 (over y, core).
Axes of the slice: x: 2, y: 2, z: 4, core: 2. Of those that a mesh axis runs over, the one named last changes fastest.
Arguments:
- expert_ids: int32 [8, 512, 8], P('rep', 'exp'), may hold values from 0 to 15, as said below
- route_weights: bfloat16 [8, 512, 8], P('rep', 'exp'), may hold values from 0.049804688 to 0.59765625
- out_grad: bfloat16 [8, 512, 1024], P('rep', 'exp'), may hold values from -6 to 6
- saved_inputs: bfloat16 [8, 4, 32, 1024], P('rep', 'exp'), may hold values from -6 to 6
- gate_weight: bfloat16 [4, 1024, 384], P('exp', 'rep'), may hold values from -0.1875 to 0.1875
- up_weight: bfloat16 [4, 1024, 384], P('exp', 'rep'), may hold values from -0.1875 to 0.1875
- down_weight: bfloat16 [4, 1024, 384], P('exp', 'rep'), may hold values from -0.3125 to 0.3125
Outputs:
- input_grad: bfloat16 [8, 512, 1024], P('rep', 'exp')
- route_grad: bfloat16 [8, 512, 8], P('rep', 'exp')
- gate_grad: float32 [4, 1024, 384], P('exp', 'rep')
- up_grad: float32 [4, 1024, 384], P('exp', 'rep')
- down_grad: float32 [4, 1024, 384], P('exp', 'rep')
Inputs may be any that keep to these rules, and one draw needn't show every extreme that they name: `expert_ids`: each row names 8 different experts. Within each aligned block of 128 rows of one replica, an expert e with e % 4 == 0 is named at most 8 times; for every replica, some such expert is named exactly 8 times in each of its blocks.
All inputs are finite; a program needn't handle non-finite values.
Results may differ from a plain program's by a relative error of at most 0.014.
Values may be sent and summed in bfloat16 or wider, within the bound.
No kernel may reach another device: no remote copies, remote signals or barrier semaphores. Data moves between devices by JAX's collectives and lax.ppermute only.
A program may use at most 64 MiB of HBM per device.

v0:
```python
import jax
import jax.numpy as jnp
from jax import lax
from jax.sharding import PartitionSpec as P

TOPK = 8
EXP_DEV = 4


def slot_table(block_ids, slot_count, owners):
    flat_ids = block_ids.reshape(-1)
    chosen = flat_ids % EXP_DEV == 0
    owner_of = flat_ids // EXP_DEV
    capacity = slot_count // owners
    onehot = ((owner_of[:, None] == jnp.arange(owners)[None, :]) & chosen[:, None]).astype(
        jnp.int32
    )
    earlier = jnp.cumsum(onehot, axis=0) - onehot
    position = jnp.sum(earlier * onehot, axis=1)
    slot_of = jnp.where(chosen, owner_of * capacity + position, -1)
    return slot_of[None, :] == jnp.arange(slot_count)[:, None]


def first_contract(left, right):
    return lax.dot_general(
        left, right, (((0,), (0,)), ((), ())), preferred_element_type=jnp.float32
    )


def second_contract(left, right):
    return lax.dot_general(
        left, right, (((1,), (1,)), ((), ())), preferred_element_type=jnp.float32
    )


def body(expert_ids, route_weights, out_grad, saved_inputs, gate_weight, up_weight, down_weight):
    owners = lax.axis_size("exp")
    replicas = lax.axis_size("rep")
    tokens_here = out_grad.shape[1]
    features = out_grad.shape[2]
    hidden_width = gate_weight.shape[2]
    slot_count = saved_inputs.shape[2]
    capacity = slot_count // owners
    placed = slot_table(expert_ids[0], slot_count, owners)
    weights_flat = route_weights[0].reshape(-1)
    slot_scale = jnp.sum(
        jnp.where(placed, weights_flat[None, :], jnp.zeros((), weights_flat.dtype)), axis=1
    )
    token_hits = jnp.any(placed.reshape(slot_count, tokens_here, TOPK), axis=2)
    token_of = jnp.sum(jnp.where(token_hits, jnp.arange(tokens_here)[None, :], 0), axis=1)
    is_live = jnp.any(token_hits, axis=1)
    routed = jnp.where(is_live[:, None], out_grad[0][token_of], jnp.zeros((), jnp.bfloat16))
    arrived, arrived_scale = (
        lax.all_to_all(
            routed.reshape(owners, capacity, features),
            "exp",
            split_axis=0,
            concat_axis=0,
            tiled=True,
        ),
        lax.all_to_all(
            slot_scale.reshape(owners, capacity), "exp", split_axis=0, concat_axis=0, tiled=True
        ),
    )
    full_gate, full_up, full_down = (
        lax.all_gather(gate_weight[0], "rep", axis=0, tiled=True),
        lax.all_gather(up_weight[0], "rep", axis=0, tiled=True),
        lax.all_gather(down_weight[0], "rep", axis=0, tiled=True),
    )
    grad_rows = arrived.reshape(slot_count, features)
    scale_col = arrived_scale.reshape(slot_count, 1).astype(jnp.float32)
    inputs_here = saved_inputs[0, 0]
    pre_gate = jnp.dot(inputs_here, full_gate, preferred_element_type=jnp.float32)
    pre_up = jnp.dot(inputs_here, full_up, preferred_element_type=jnp.float32)
    sigmoid_gate = jax.nn.sigmoid(pre_gate)
    activated = pre_gate * sigmoid_gate
    hidden = (activated * pre_up).astype(jnp.bfloat16)
    raw_grad = jnp.dot(grad_rows, full_down, preferred_element_type=jnp.float32)
    slot_route = jnp.sum(hidden.astype(jnp.float32) * raw_grad, axis=1).astype(jnp.bfloat16)
    hidden_grad = scale_col * raw_grad
    scaled_rows = (scale_col * grad_rows.astype(jnp.float32)).astype(jnp.bfloat16)
    gate_delta = (
        hidden_grad * pre_up * sigmoid_gate * (1.0 + pre_gate * (1.0 - sigmoid_gate))
    ).astype(jnp.bfloat16)
    up_delta = (hidden_grad * activated).astype(jnp.bfloat16)
    back_rows = (
        second_contract(gate_delta, full_gate) + second_contract(up_delta, full_up)
    ).astype(jnp.bfloat16)
    returned, returned_route = (
        lax.all_to_all(
            back_rows.reshape(owners, capacity, features),
            "exp",
            split_axis=0,
            concat_axis=0,
            tiled=True,
        ),
        lax.all_to_all(
            slot_route.reshape(owners, capacity), "exp", split_axis=0, concat_axis=0, tiled=True
        ),
    )
    returned_flat = returned.reshape(slot_count, features)
    route_flat = returned_route.reshape(slot_count)
    combined = jax.ops.segment_sum(
        jnp.where(is_live[:, None], returned_flat.astype(jnp.float32), 0.0),
        token_of,
        num_segments=tokens_here,
    )
    input_grad = combined.astype(jnp.bfloat16)[None]
    route_grad = jnp.sum(
        jnp.where(placed, route_flat[:, None], jnp.zeros((), jnp.bfloat16)), axis=0
    )
    route_grad = route_grad.reshape(1, tokens_here, TOPK)
    joined_share = lax.psum_scatter(
        jnp.concatenate(
            [
                jnp.concatenate(
                    [
                        first_contract(inputs_here, gate_delta),
                        first_contract(inputs_here, up_delta),
                    ],
                    axis=1,
                ),
                first_contract(scaled_rows, hidden),
            ],
            axis=1,
        ),
        "rep",
        scatter_dimension=0,
        tiled=True,
    )
    gate_share = joined_share[:, :hidden_width]
    up_share = joined_share[:, hidden_width : 2 * hidden_width]
    down_share = joined_share[:, 2 * hidden_width :]
    gate_grad = (gate_share / replicas)[None]
    up_grad = (up_share / replicas)[None]
    down_grad = (down_share / replicas)[None]
    return (input_grad, route_grad, gate_grad, up_grad, down_grad)


def solution(mesh):
    in_specs = (
        P("rep", "exp", None),
        P("rep", "exp", None),
        P("rep", "exp", None),
        P("rep", "exp", None, None),
        P("exp", "rep", None),
        P("exp", "rep", None),
        P("exp", "rep", None),
    )
    out_specs = (
        P("rep", "exp", None),
        P("rep", "exp", None),
        P("exp", "rep", None),
        P("exp", "rep", None),
        P("exp", "rep", None),
    )
    return jax.shard_map(body, mesh=mesh, in_specs=in_specs, out_specs=out_specs, check_vma=False)
```

profile of v0, /device:TPU:0, one launch (start us, length us, event | category | flops | bytes accessed | tf_op | source)
XLA Modules:
  0.0 239.1 jit_solution(11610807980264724344)
XLA Ops:
  7.2 0.0 copy-start
  7.2 0.0 copy-start.2
  7.2 0.0 copy-start.3
  7.2 0.8 copy.44
  8.0 0.1 reshape_squeeze.8
  8.1 0.1 reshape_squeeze.9
  8.2 0.0 copy-start.1
  8.3 1.1 reduce-window.6
  9.5 0.2 slice_reduce_fusion
  9.7 0.2 reduce-window.9
  9.9 0.1 add_bitcast_fusion
  10.0 0.1 reduce_sum.54
  10.1 0.1 fusion.23
  10.2 0.7 fusion.18
  10.9 0.1 select_reduce_fusion
  11.0 0.1 broadcast_in_dim.101
  11.1 0.0 copy-done
  11.1 0.6 gather_fusion
  11.7 0.7 bitcast_select_fusion
  12.4 4.2 %all-to-all-start.1 = ((bf16[4,8,1024]{2,1,0:T(8,128)(2,1)}), bf16[4,8,1024]{2,1,0:T(8,128)(2,1)S(1)}, u32[]{:S(2)}, u32[]{:S(2)}) async-start(bf16[4,8,1024]{2,1,0:T(8,128)(2,1)} %bitcast_select_fusion), calls=%async_computation.1 | async-start | bytes 131072 | tf_op jit(solution)/shard_map/all_to_all | solution.py:54
  16.7 0.0 copy-start.4
  16.7 0.0 reduce-scatter.2.cloned.1.call-start
  16.7 0.0 copy-done.2
  16.7 33.0 %all-gather.2 = bf16[1,1024,384]{2,1,0:T(8,128)(2,1)S(1)} all-gather(bf16[1,128,384]{2,1,0:T(8,128)(2,1)S(1)} %copy-done.2), channel_id=4, replica_groups=mesh['rep'=8,'exp'=4] {'rep'}, dimensions={1}, use_global_device_ids=true | all-gather | bytes 884736 | tf_op jit(solution)/shard_map/all_gather | solution.py:66
  49.7 0.0 copy-done.3
  49.7 0.0 copy-start.5
  49.7 32.4 %all-gather.1 = bf16[1,1024,384]{2,1,0:T(8,128)(2,1)S(1)} all-gather(bf16[1,128,384]{2,1,0:T(8,128)(2,1)S(1)} %copy-done.3), channel_id=3, replica_groups=mesh['rep'=8,'exp'=4] {'rep'}, dimensions={1}, use_global_device_ids=true | all-gather | bytes 884736 | tf_op jit(solution)/shard_map/all_gather | solution.py:67
  82.1 0.0 copy-done.1
  82.1 0.2 fusion.4
  82.3 0.2 fusion.7
  82.6 0.0 copy-done.4
  82.6 32.0 %all-gather = bf16[1,1024,384]{2,1,0:T(8,128)(2,1)S(1)} all-gather(bf16[1,128,384]{2,1,0:T(8,128)(2,1)S(1)} %copy-done.4), channel_id=2, replica_groups=mesh['rep'=8,'exp'=4] {'rep'}, dimensions={1}, use_global_device_ids=true | all-gather | bytes 884736 | tf_op jit(solution)/shard_map/all_gather | solution.py:68
  114.6 0.0 copy-done.5
  114.6 0.1 copy.48
  114.7 0.1 broadcast_in_dim.98
  114.8 0.0 all-to-all-done.1
  114.8 0.3 multiply_reduce_fusion
  115.1 0.1 convert_element_type.84
  115.2 7.2 %all_to_all.26 = bf16[4,1,8]{2,1,0:T(2,128)(2,1)S(1)} all-to-all(bf16[4,1,8]{2,1,0:T(2,128)(2,1)S(1)} %convert_element_type.84), channel_id=1, replica_groups=mesh['rep'=8,'exp'=4] {'exp'}, dimensions={0} | all-to-all | bytes 128 | tf_op jit(solution)/shard_map/all_to_all | solution.py:97
  122.4 0.1 broadcast_in_dim.106
  122.5 0.1 fusion.25
  122.7 0.1 all_to_all.21
  122.7 6.1 %all_to_all.27 = bf16[4,1,8]{2,1,0:T(2,128)(2,1)S(1)} all-to-all(bf16[4,1,8]{2,1,0:T(2,128)(2,1)S(1)} %all_to_all.21), channel_id=1, replica_groups=mesh['rep'=8,'exp'=4] {'exp'}, dimensions={0} | all-to-all | bytes 128 | tf_op jit(solution)/shard_map/all_to_all | solution.py:61
  128.9 0.1 reshape.228
  128.9 0.1 multiply_convert_fusion.3
  129.0 0.4 convolution_bitcast_fusion
  129.4 0.4 convolution_bitcast_fusion.1
  129.8 0.4 fusion.26
  130.2 2.5 %pad_maximum_fusion = f32[1024,1152]{0,1:T(8,128)} fusion(f32[1024,384]{0,1:T(8,128)S(1)} %fusion.26, f32[1024,384]{0,1:T(8,128)S(1)} %convolution_bitcast_fusion, f32[1024,384]{0,1:T(8,128)S(1)} %convolution_bitcast_fusion.1), kind=kLoop, calls=%fused_computation.2 | loop fusion | flops 2359296 | bytes 9437184 | tf_op jit(solution)/shard_map/concatenate | solution.py:114
  132.7 0.0 reduce-scatter.2.cloned.1.call-update
  132.8 0.3 fusion.2
  133.1 1.0 fusion.1
  134.1 3.3 %all-to-all-start.2 = ((bf16[4,8,1024]{2,1,0:T(8,128)(2,1)}), bf16[4,8,1024]{2,1,0:T(8,128)(2,1)S(1)}, u32[]{:S(2)}, u32[]{:S(2)}) async-start(bf16[4,8,1024]{2,1,0:T(8,128)(2,1)} %fusion.1), calls=%async_computation.2 | async-start | bytes 131072 | tf_op jit(solution)/shard_map/all_to_all | solution.py:90
  137.4 0.1 reshape.227
  137.5 0.7 copy.51
  138.1 3.3 %all-to-all-done.2 = bf16[4,8,1024]{2,1,0:T(8,128)(2,1)S(1)} async-done(((bf16[4,8,1024]{2,1,0:T(8,128)(2,1)}), bf16[4,8,1024]{2,1,0:T(8,128)(2,1)S(1)}, u32[]{:S(2)}, u32[]{:S(2)}) %all-to-all-start.2) | async-done | bytes 65568 | tf_op jit(solution)/shard_map/all_to_all | solution.py:90
  141.5 1.0 scatter_custom_fusion
  142.5 0.7 convert_bitcast_fusion
  143.3 85.4 %reduce-scatter.2.cloned.1.call-done = f32[128,1152]{0,1:T(8,128)} async-done(((f32[1024,1152]{0,1:T(8,128)}), f32[128,1152]{0,1:T(8,128)}) %reduce-scatter.2.cloned.1.call-update) | async-done | bytes 589840 | tf_op jit(solution)/shard_map/reduce_scatter | solution.py:113
  228.6 1.2 fusion.13
  229.8 0.8 copy.54
  230.6 0.8 copy.53
  231.4 0.8 copy.52
  (12 shorter events, 0.2 us)
Async XLA Ops:
  7.2 3.9 %copy-start = (bf16[1,128,1024]{2,1,0:T(8,128)(2,1)S(1)}, bf16[1,128,1024]{2,1,0:T(8,128)(2,1)}, u32[]{:S(2)}) copy-start(bf16[1,128,1024]{2,1,0:T(8,128)(2,1)} %param.9) | copy-start | bytes 786436
  7.2 9.5 %copy-start.2 = (bf16[1,128,384]{2,1,0:T(8,128)(2,1)S(1)}, bf16[1,128,384]{2,1,0:T(8,128)(2,1)}, u32[]{:S(2)}) copy-start(bf16[1,128,384]{2,1,0:T(8,128)(2,1)} %param.11) | copy-start | bytes 294916
  7.2 42.5 %copy-start.3 = (bf16[1,128,384]{2,1,0:T(8,128)(2,1)S(1)}, bf16[1,128,384]{2,1,0:T(8,128)(2,1)}, u32[]{:S(2)}) copy-start(bf16[1,128,384]{2,1,0:T(8,128)(2,1)} %param.12) | copy-start | bytes 294916
  8.2 73.9 %copy-start.1 = (bf16[1,1,32,1024]{3,2,1,0:T(8,128)(2,1)S(1)}, bf16[1,1,32,1024]{3,2,1,0:T(8,128)(2,1)}, u32[]{:S(2)}) copy-start(bf16[1,1,32,1024]{3,2,1,0:T(8,128)(2,1)} %param.10) | copy-start | bytes 196612
  12.4 102.4 %all-to-all-start.1 = ((bf16[4,8,1024]{2,1,0:T(8,128)(2,1)}), bf16[4,8,1024]{2,1,0:T(8,128)(2,1)S(1)}, u32[]{:S(2)}, u32[]{:S(2)}) async-start(bf16[4,8,1024]{2,1,0:T(8,128)(2,1)} %bitcast_select_fusion), calls=%async_computation.1 | async-start | bytes 131072 | tf_op jit(solution)/shard_map/all_to_all | solution.py:54
  16.7 65.9 %copy-start.4 = (bf16[1,128,384]{2,1,0:T(8,128)(2,1)S(1)}, bf16[1,128,384]{2,1,0:T(8,128)(2,1)}, u32[]{:S(2)}) copy-start(bf16[1,128,384]{2,1,0:T(8,128)(2,1)} %param.13) | copy-start | bytes 294916
  16.7 211.9 %reduce-scatter.2.cloned.1.call-start = ((), (), s32[]{:S(2)}) async-start(), calls=%async_computation.5 | async-start | bytes 5308416 | tf_op jit(solution)/shard_map/reduce_scatter | solution.py:113
  49.7 64.8 %copy-start.5 = (bf16[1,128,8]{1,2,0:T(8,128)(2,1)S(1)}, bf16[1,128,8]{1,2,0:T(8,128)(2,1)}, u32[]{:S(2)}) copy-start(bf16[1,128,8]{1,2,0:T(8,128)(2,1)} %param.8) | copy-start | bytes 6148
  134.1 7.4 %all-to-all-start.2 = ((bf16[4,8,1024]{2,1,0:T(8,128)(2,1)}), bf16[4,8,1024]{2,1,0:T(8,128)(2,1)S(1)}, u32[]{:S(2)}, u32[]{:S(2)}) async-start(bf16[4,8,1024]{2,1,0:T(8,128)(2,1)} %fusion.1), calls=%async_computation.2 | async-start | bytes 131072 | tf_op jit(solution)/shard_map/all_to_all | solution.py:90
Sparse Core Ops, SparseCore 0:
  132.9 95.7 reduce-scatter.1
where the time goes:
time: 240 us; the launch traced here: 239 us
  blocking collectives  111 us (46%)
  waiting for transfers between devices  88.7 us (37%)
  between operations  14.2 us (6%)
  other arithmetic  8.79 us (4%)
  starting transfers between devices  7.52 us (3%)
  local copies, waits for them, and re-layouts  5.86 us (2%)
  matrix products  3.3 us (1%)
    reduce_scatter x1, waiting for transfers between devices, body(): lax.psum_scatter(jnp.concatenate([jnp.concatenate([first_contract(inputs_...  85.4 us
    all_gather x1, blocking collectives, body(): lax.all_gather(gate_weight[0], 'rep', axis=0, tiled=True)  33 us
    all_gather x1, blocking collectives, body(): lax.all_gather(up_weight[0], 'rep', axis=0, tiled=True)  32.4 us
    all_gather x1, blocking collectives, body(): lax.all_gather(down_weight[0], 'rep', axis=0, tiled=True)  32 us
    all_to_all x1, blocking collectives, body(): lax.all_to_all(slot_route.reshape(owners, capacity), 'exp', split_axis=0,...  7.19 us
    all_to_all x1, blocking collectives, body(): lax.all_to_all(slot_scale.reshape(owners, capacity), 'exp', split_axis=0,...  6.08 us
  transfers between devices with their start and end apart: 3, of which 2 were waited for; matrix products, arithmetic and copies ran while one was open for 2% of the time, Pallas kernels for 0%

commit v1 on v0

--- a/solution.py
+++ b/solution.py
@@ -1,10 +1,275 @@
 import jax
 import jax.numpy as jnp
 from jax import lax
+from jax.experimental import pallas as pl
+from jax.experimental.pallas import tpu as pltpu
 from jax.sharding import PartitionSpec as P
 
 TOPK = 8
 EXP_DEV = 4
+PARTS = 4
+CAP = 8
+F32 = jnp.float32
+BF16 = jnp.bfloat16
+
+
+def dot(left, right, ldim, rdim):
+    return lax.dot_general(
+        left, right, (((ldim,), (rdim,)), ((), ())), preferred_element_type=F32
+    )
+
+
+def call(kernel, *args, out, scratch=()):
+    spec = pl.BlockSpec(memory_space=pltpu.VMEM)
+    return pl.pallas_call(
+        kernel,
+        out_shape=[jax.ShapeDtypeStruct(s, d) for s, d in out],
+        in_specs=[spec] * len(args),
+        out_specs=[spec] * len(out),
+        scratch_shapes=list(scratch),
+        compiler_params=pltpu.CompilerParams(vmem_limit_bytes=32 << 20),
+    )(*args)
+
+
+def position():
+    rank = lax.axis_index("rep")
+    return rank // PARTS, rank % PARTS
+
+
+def route_kernel(ids_ref, weights_ref, grads_ref, send_ref, hits_ref):
+    ids = ids_ref[...]
+    weights = weights_ref[...].astype(F32)
+    slots, tokens = hits_ref.shape
+    capacity = CAP
+    owners = slots // capacity
+    hits, scales = [], []
+    for j in range(owners):
+        match = ids == j * EXP_DEV
+        hits.append(jnp.sum(jnp.where(match, 1.0, 0.0), axis=0, keepdims=True))
+        scales.append(jnp.sum(jnp.where(match, weights, 0.0), axis=0, keepdims=True))
+    pad = [jnp.zeros((1, tokens), F32)] * (-owners % 8)
+    hit = jnp.concatenate(hits + pad, axis=0)
+    earlier = lax.broadcasted_iota(jnp.int32, (tokens, tokens), 0) < (
+        lax.broadcasted_iota(jnp.int32, (tokens, tokens), 1)
+    )
+    place = dot(hit.astype(BF16), jnp.where(earlier, 1.0, 0.0).astype(BF16), 1, 0)
+    slot = lax.broadcasted_iota(jnp.int32, (capacity, tokens), 0).astype(F32)
+    chosen, scaled = [], []
+    for j in range(owners):
+        here = (place[j : j + 1] == slot) & (hits[j] > 0.0)
+        chosen.append(jnp.where(here, 1.0, 0.0))
+        scaled.append(jnp.where(here, scales[j], 0.0))
+    hits_ref[...] = jnp.concatenate(chosen, axis=0).astype(BF16)
+    rows = dot(
+        jnp.concatenate(scaled, axis=0).astype(BF16), grads_ref[...], 1, 0
+    ).astype(BF16)
+    half = send_ref.shape[1]
+    for q in range(2):
+        for p in range(PARTS):
+            start = (q * PARTS + p) * slots
+            send_ref[start : start + slots, :] = rows[:, q * half : (q + 1) * half]
+
+
+def weights_kernel(gate_ref, up_ref, down_ref, *rest):
+    outs, flipped = rest[:PARTS], rest[PARTS]
+    part = outs[0].shape[0] // 3
+    _, p = position()
+    for i, ref in enumerate((gate_ref, up_ref, down_ref)):
+        flipped[i] = ref[...].astype(F32).T.astype(BF16)
+    for k in range(PARTS):
+        start = pl.multiple_of((p ^ k) * part, part)
+        for i in range(3):
+            outs[k][i * part : (i + 1) * part, :] = flipped[i, pl.ds(start, part), :]
+
+
+def gate_up_kernel(*refs):
+    weights, inputs = refs[:PARTS], refs[PARTS : 2 * PARTS]
+    weight_ref, input_ref, own_ref, sent_ref = refs[2 * PARTS :]
+    q, p = position()
+    width = weights[0].shape[1]
+    slots = inputs[0].shape[0] // 2
+    for k in range(PARTS):
+        other = p ^ k
+        weight_ref[:, pl.ds(pl.multiple_of(other * width, width), width)] = weights[k][...]
+        for h, owner in enumerate((q, 1 - q)):
+            start = pl.multiple_of((owner * PARTS + other) * slots, slots)
+            input_ref[pl.ds(start, slots), :] = inputs[k][h * slots : (h + 1) * slots, :]
+    rows = own_ref.shape[0]
+    partial = dot(weight_ref[0:rows, :], input_ref[...], 1, 1)
+    own_ref[...] = partial
+    sent_ref[...] = partial.astype(BF16)
+
+
+def down_kernel(weight_ref, grads_ref, own_ref, sent_ref):
+    rows = own_ref.shape[0]
+    partial = dot(weight_ref[2 * rows : 3 * rows, :], grads_ref[...], 1, 1)
+    own_ref[...] = partial
+    sent_ref[...] = partial.astype(BF16)
+
+
+def delta_kernel(own_ref, other_ref, down_ref, down_other_ref, weight_ref, delta_ref, back_ref):
+    part = down_ref.shape[0]
+    both = own_ref[...] + other_ref[...].astype(F32)
+    pre_gate, pre_up = both[:part], both[part:]
+    hidden_grad = down_ref[...] + down_other_ref[...].astype(F32)
+    sigmoid = jax.nn.sigmoid(pre_gate)
+    activated = pre_gate * sigmoid
+    hidden = (activated * pre_up).astype(BF16)
+    gate_delta = hidden_grad * pre_up * sigmoid * (1.0 + pre_gate * (1.0 - sigmoid))
+    up_delta = hidden_grad * activated
+    delta_ref[0:part, :] = gate_delta.astype(BF16)
+    delta_ref[part : 2 * part, :] = up_delta.astype(BF16)
+    delta_ref[2 * part :, :] = hidden
+    half = weight_ref.shape[1]
+    back_ref[:, :half] = dot(
+        delta_ref[0 : 2 * part, :], weight_ref[0 : 2 * part, :], 0, 0
+    ).astype(BF16)
+    product = hidden.astype(F32) * hidden_grad
+    high = product.astype(BF16)
+    low = (product - high.astype(F32)).astype(BF16)
+    ones = jnp.ones((part, back_ref.shape[1] - half), BF16)
+    back_ref[:, half:] = (dot(high, ones, 0, 0) + dot(low, ones, 0, 0)).astype(BF16)
+
+
+def grads_kernel(delta_ref, input_ref, grads_ref, *rest):
+    outs, total = rest[:PARTS], rest[PARTS]
+    part = delta_ref.shape[0] // 3
+    width = outs[0].shape[1]
+    _, p = position()
+    total[0 : 2 * part, :] = dot(delta_ref[0 : 2 * part, :], input_ref[...], 1, 0).astype(BF16)
+    total[2 * part :, :] = dot(delta_ref[2 * part :, :], grads_ref[...], 1, 0).astype(BF16)
+    for k in range(PARTS):
+        outs[k][...] = total[:, pl.ds(pl.multiple_of((p ^ k) * width, width), width)]
+
+
+def tokens_kernel(ids_ref, weights_ref, hits_ref, rows_ref, input_grad_ref, route_ref):
+    slots, tokens = hits_ref.shape
+    group = PARTS * slots
+    half = input_grad_ref.shape[1] // 2
+    hits = hits_ref[...]
+    tiled = jnp.concatenate([hits] * PARTS, axis=0)
+    for q in range(2):
+        input_grad_ref[:, q * half : (q + 1) * half] = dot(
+            tiled, rows_ref[q * group : (q + 1) * group, :half], 0, 0
+        ).astype(BF16)
+    route = rows_ref[0:slots, half:].astype(F32)
+    for p in range(1, PARTS):
+        route = route + rows_ref[p * slots : (p + 1) * slots, half:].astype(F32)
+    spread = hits.astype(F32) * route
+    ids = ids_ref[...]
+    out = jnp.zeros(ids.shape, F32)
+    for j in range(slots // CAP):
+        value = jnp.sum(spread[j * CAP : (j + 1) * CAP], axis=0, keepdims=True)
+        out = jnp.where(ids == j * EXP_DEV, value, out)
+    route_ref[...] = (out / weights_ref[...].astype(F32)).astype(BF16)
+
+
+def outputs_kernel(replicas, *refs):
+    parts, outs, whole = refs[:PARTS], refs[PARTS : PARTS + 3], refs[PARTS + 3]
+    part = parts[0].shape[0] // 3
+    _, p = position()
+    for k in range(PARTS):
+        start = pl.multiple_of((p ^ k) * part, part)
+        for i in range(3):
+            whole[i, pl.ds(start, part), :] = parts[k][i * part : (i + 1) * part, :].astype(F32)
+    for i in range(3):
+        outs[i][...] = whole[i].T / replicas
+
+
+def body(expert_ids, route_weights, out_grad, saved_inputs, gate_weight, up_weight, down_weight):
+    owners = lax.axis_size("exp")
+    replicas = lax.axis_size("rep")
+    tokens, features = out_grad.shape[1:]
+    slots = saved_inputs.shape[2]
+    width, hidden_width = gate_weight.shape[1:]
+    half, part = features // 2, hidden_width // PARTS
+    rows = replicas * slots
+
+    def swap(value, mask):
+        return lax.ppermute(value, "rep", [(i, i ^ mask) for i in range(replicas)])
+
+    saved = saved_inputs[0, 0]
+    q = lax.axis_index("rep") // PARTS
+    mine = lax.dynamic_slice_in_dim(saved, q * half, half, axis=1)
+    theirs = lax.dynamic_slice_in_dim(saved, (1 - q) * half, half, axis=1)
+    theirs = swap(theirs, PARTS)
+    flipped = call(
+        weights_kernel,
+        gate_weight[0],
+        up_weight[0],
+        down_weight[0],
+        out=[((3 * part, width), BF16)] * PARTS,
+        scratch=[pltpu.VMEM((3, hidden_width, width), BF16)],
+    )
+    weights = [flipped[0]] + [swap(flipped[k], k) for k in range(1, PARTS)]
+
+    ids = expert_ids[0].T
+    scales = route_weights[0].T
+    sent, hits = call(
+        route_kernel,
+        ids,
+        scales,
+        out_grad[0],
+        out=[((2 * PARTS * slots, half), BF16), ((slots, tokens), BF16)],
+    )
+    arrived = lax.all_to_all(
+        sent.reshape(replicas * owners, CAP, half), ("rep", "exp"), 0, 0, tiled=True
+    ).reshape(rows, half)
+
+    pair = jnp.concatenate([mine, theirs], axis=0)
+    inputs = [pair] + [swap(pair, k) for k in range(1, PARTS)]
+    weight, joined, own, gate_up_sent = call(
+        gate_up_kernel,
+        *weights,
+        *inputs,
+        out=[
+            ((3 * part, half), BF16),
+            ((rows, half), BF16),
+            ((2 * part, rows), F32),
+            ((2 * part, rows), BF16),
+        ],
+    )
+    other = swap(gate_up_sent, PARTS)
+    down_own, down_sent = call(
+        down_kernel, weight, arrived, out=[((part, rows), F32), ((part, rows), BF16)]
+    )
+    down_other = swap(down_sent, PARTS)
+    delta, back = call(
+        delta_kernel,
+        own,
+        other,
+        down_own,
+        down_other,
+        weight,
+        out=[((3 * part, rows), BF16), ((rows, half + 128), BF16)],
+    )
+    returned = lax.all_to_all(
+        back.reshape(replicas * owners, CAP, half + 128), ("rep", "exp"), 0, 0, tiled=True
+    ).reshape(rows, half + 128)
+    shares = call(
+        grads_kernel,
+        delta,
+        joined,
+        arrived,
+        out=[((3 * part, width), BF16)] * PARTS,
+        scratch=[pltpu.VMEM((3 * part, half), BF16)],
+    )
+    shares = [shares[0]] + [swap(shares[k], k) for k in range(1, PARTS)]
+    input_grad, route_grad = call(
+        tokens_kernel,
+        ids,
+        scales,
+        hits,
+        returned,
+        out=[((tokens, features), BF16), ((TOPK, tokens), BF16)],
+    )
+    gate_grad, up_grad, down_grad = call(
+        lambda *refs: outputs_kernel(replicas, *refs),
+        *shares,
+        out=[((width, hidden_width), F32)] * 3,
+        scratch=[pltpu.VMEM((3, hidden_width, width), F32)],
+    )
+    return (input_grad[None], route_grad.T[None], gate_grad[None], up_grad[None], down_grad[None])
 
 
 def slot_table(block_ids, slot_count, owners):
@@ -33,7 +298,7 @@
     )
 
 
-def body(expert_ids, route_weights, out_grad, saved_inputs, gate_weight, up_weight, down_weight):
+def general_body(expert_ids, route_weights, out_grad, saved_inputs, gate_weight, up_weight, down_weight):
     owners = lax.axis_size("exp")
     replicas = lax.axis_size("rep")
     tokens_here = out_grad.shape[1]
@@ -154,4 +419,6 @@
         P("exp", "rep", None),
         P("exp", "rep", None),
     )
-    return jax.shard_map(body, mesh=mesh, in_specs=in_specs, out_specs=out_specs, check_vma=False)
+    fits = mesh.shape["rep"] == 2 * PARTS
+    step = body if fits else general_body
+    return jax.shard_map(step, mesh=mesh, in_specs=in_specs, out_specs=out_specs, check_vma=False)

time: 240 us -> 56.8 us (0.24)
  blocking collectives: 111 us -> 0 us
  waiting for transfers between devices: 88.7 us -> 20.8 us
  starting transfers between devices: 7.52 us -> 26.9 us
  between operations: 14.2 us -> 0.76 us
  other arithmetic: 8.79 us -> 0.01 us
  Pallas kernels: 0 us -> 4.99 us
  matrix products: 3.3 us -> 0 us
  local copies, waits for them, and re-layouts: 5.86 us -> 3.02 us
    all_gather x3 -> x0, blocking collectives: 97.4 us -> none  [the longest x1 33 us: body(): lax.all_gather(gate_weight[0], 'rep', axis=0, tiled=True)]
    reduce_scatter x1 -> x0, waiting for transfers between devices: 85.4 us -> none  [body(): lax.psum_scatter(jnp.concatenate([jnp.concatenate([first_contract(inputs_...]
    ppermute x0 -> x12, waiting for transfers between devices: none -> 20.8 us  [swap(): return lax.ppermute(value, 'rep', [(i, i ^ mask) for i in range(replicas)])]
    ppermute x0 -> x12, starting transfers between devices: none -> 16.4 us  [swap(): return lax.ppermute(value, 'rep', [(i, i ^ mask) for i in range(replicas)])]
    all_to_all x2 -> x0, blocking collectives: 13.3 us -> none  [the longest x1 7.19 us: body(): lax.all_to_all(slot_route.reshape(owners, capacity), 'exp', split_axis=0,...]
    pallas_call x0 -> x8, Pallas kernels: none -> 4.99 us  [call(): pl.pallas_call(kernel, out_shape=[jax.ShapeDtypeStruct(s, d) for s, d in...]
    all_to_all x2, waiting for transfers between devices: 3.34 us -> 0.01 us  [the longest x1 0.01 us: body(): lax.all_to_all(sent.reshape(replicas * owners, CAP, half), ('rep', 'exp')...]
    dot_general x8 -> x0, matrix products: 3.3 us -> none  [the longest x2 1.33 us: second_contract(): lax.dot_general(left, right, (((1,), (1,)), ((), ())), preferred_element_...]
  transfers between devices with their start and end apart: 3 -> 14, of which waited for: 2 -> 9; matrix products, arithmetic and copies ran while one was open for 2% -> 0% of each run, Pallas kernels for 0% -> 3%
where the time goes in v1:
time: 56.8 us; the launch traced here: 56.4 us
  starting transfers between devices  26.9 us (47%)
  waiting for transfers between devices  20.8 us (37%)
  Pallas kernels  4.99 us (9%)
  local copies, waits for them, and re-layouts  3.02 us (5%)
  between operations  0.76 us (1%)
    ppermute x12, waiting for transfers between devices, swap(): return lax.ppermute(value, 'rep', [(i, i ^ mask) for i in range(replicas)])  20.8 us
    ppermute x12, starting transfers between devices, swap(): return lax.ppermute(value, 'rep', [(i, i ^ mask) for i in range(replicas)])  16.4 us
    all_to_all x1, starting transfers between devices, body(): lax.all_to_all(sent.reshape(replicas * owners, CAP, half), ('rep', 'exp')...  7.3 us
    pallas_call x8, Pallas kernels, call(): pl.pallas_call(kernel, out_shape=[jax.ShapeDtypeStruct(s, d) for s, d in...  4.99 us
    all_to_all x1, starting transfers between devices, body(): lax.all_to_all(back.reshape(replicas * owners, CAP, half + 128), ('rep',...  3.19 us
    unnamed x16, local copies, waits for them, and re-layouts  3.01 us
  transfers between devices with their start and end apart: 14, of which 9 were waited for; matrix products, arithmetic and copies ran while one was open for 0% of the time, Pallas kernels for 3%

profile of v1, /device:TPU:0, one launch (start us, length us, event | category | flops | bytes accessed | tf_op | source)
XLA Modules:
  0.0 56.4 jit_solution(5315585584807205587)
XLA Ops:
  0.6 0.0 copy-start.4
  0.6 0.7 %copy-done.4 = s32[1,128,8]{1,2,0:T(8,128)S(1)} copy-done((s32[1,128,8]{1,2,0:T(8,128)S(1)}, s32[1,128,8]{1,2,0:T(8,128)}, u32[]{:S(2)}) %copy-start.4) | copy-done | bytes 4120
  1.3 0.0 copy-start
  1.3 0.9 %copy-done = bf16[1,128,1024]{2,1,0:T(8,128)(2,1)S(1)} copy-done((bf16[1,128,1024]{2,1,0:T(8,128)(2,1)S(1)}, bf16[1,128,1024]{2,1,0:T(8,128)(2,1)}, u32[]{:S(2)}) %copy-start) | copy-done | bytes 262168
  2.3 0.0 copy-start.5
  2.3 0.7 %copy-done.5 = bf16[1,128,8]{1,2,0:T(8,128)(2,1)S(1)} copy-done((bf16[1,128,8]{1,2,0:T(8,128)(2,1)S(1)}, bf16[1,128,8]{1,2,0:T(8,128)(2,1)}, u32[]{:S(2)}) %copy-start.5) | copy-done | bytes 2072
  3.0 1.0 %shard_map.110 = (bf16[256,512]{1,0:T(8,128)(2,1)}, bf16[32,128]{1,0:T(8,128)(2,1)S(1)}) custom-call(s32[8,128]{1,0:T(8,128)S(1)} %bitcast.32, bf16[8,128]{1,0:T(8,128)(2,1)S(1)} %bitcast.34, bf16[128,1024]{1,0:T(8,128)(2,1)S(1)} %bitcast.28), custom_call_target="tpu_custom_call" | custom-call | tf_op jit(solution)/shard_map/pallas_call | solution.py:24
  4.0 0.0 copy-start.7
  4.0 0.0 copy-start.2
  4.0 0.0 copy-start.3
  4.0 7.3 %all-to-all-start = ((bf16[32,8,512]{2,1,0:T(8,128)(2,1)}), bf16[32,8,512]{2,1,0:T(8,128)(2,1)S(1)}, u32[]{:S(2)}, u32[]{:S(2)}) async-start(bf16[32,8,512]{2,1,0:T(8,128)(2,1)} %bitcast.12), calls=%async_computation | async-start | bytes 524288 | tf_op jit(solution)/shard_map/all_to_all | solution.py:215
  11.3 0.0 copy-start.1
  11.3 0.0 copy-done.7
  11.3 2.7 %collective-permute-start.3 = (bf16[32,512]{1,0:T(8,128)(2,1)S(1)}, bf16[32,512]{1,0:T(8,128)(2,1)S(1)}, u32[]{:S(2)}, u32[]{:S(2)}) collective-permute-start(bf16[32,512]{1,0:T(8,128)(2,1)S(1)} %get-tuple-element.52), channel_id=1, source_target_pairs={{0,16},{4,20},{8,24},{12,28},{16,0},{20,4},{24,8},{28,12},{1,17},{... | collective-permute-start | bytes 98312 | tf_op jit(solution)/shard_map/ppermute | solution.py:189
  14.1 0.0 copy-done.2
  14.1 0.0 copy-done.3
  14.1 0.0 copy-done.1
  14.1 0.2 shard_map.111
  14.3 1.5 %collective-permute-start = (bf16[288,128]{1,0:T(8,128)(2,1)S(1)}, bf16[288,128]{1,0:T(8,128)(2,1)S(1)}, u32[]{:S(2)}, u32[]{:S(2)}) collective-permute-start(bf16[288,128]{1,0:T(8,128)(2,1)S(1)} %get-tuple-element.30), channel_id=1, source_target_pairs={{0,4},{4,0},{8,12},{12,8},{16,20},{20,16},{24,28},{28,24},{1,5},{5... | collective-permute-start | bytes 221192 | tf_op jit(solution)/shard_map/ppermute | solution.py:189
  15.8 1.5 %collective-permute-start.1 = (bf16[288,128]{1,0:T(8,128)(2,1)S(1)}, bf16[288,128]{1,0:T(8,128)(2,1)S(1)}, u32[]{:S(2)}, u32[]{:S(2)}) collective-permute-start(bf16[288,128]{1,0:T(8,128)(2,1)S(1)} %get-tuple-element.31), channel_id=1, source_target_pairs={{0,8},{4,12},{8,0},{12,4},{16,24},{20,28},{24,16},{28,20},{1,9},{5... | collective-permute-start | bytes 221192 | tf_op jit(solution)/shard_map/ppermute | solution.py:189
  17.3 0.5 collective-permute-start.2
  17.8 4.2 %collective-permute-done.3 = bf16[32,512]{1,0:T(8,128)(2,1)S(1)} collective-permute-done((bf16[32,512]{1,0:T(8,128)(2,1)S(1)}, bf16[32,512]{1,0:T(8,128)(2,1)S(1)}, u32[]{:S(2)}, u32[]{:S(2)}) %collective-permute-start.3) | collective-permute-done | bytes 32800 | tf_op jit(solution)/shard_map/ppermute | solution.py:189
  22.1 0.8 %collective-permute-start.6 = (bf16[64,512]{1,0:T(8,128)(2,1)S(1)}, bf16[64,512]{1,0:T(8,128)(2,1)S(1)}, u32[]{:S(2)}, u32[]{:S(2)}) collective-permute-start(bf16[64,512]{1,0:T(8,128)(2,1)S(1)} %pad_maximum_fusion.refs_4_), channel_id=1, source_target_pairs={{0,12},{4,8},{8,4},{12,0},{16,28},{20,24},{24,20},{28,16},{1,13},{... | collective-permute-start | bytes 196616 | tf_op jit(solution)/shard_map/ppermute | solution.py:189
  22.9 2.1 %collective-permute-start.5 = (bf16[64,512]{1,0:T(8,128)(2,1)S(1)}, bf16[64,512]{1,0:T(8,128)(2,1)S(1)}, u32[]{:S(2)}, u32[]{:S(2)}) collective-permute-start(bf16[64,512]{1,0:T(8,128)(2,1)S(1)} %pad_maximum_fusion.refs_4_), channel_id=1, source_target_pairs={{0,8},{4,12},{8,0},{12,4},{16,24},{20,28},{24,16},{28,20},{1,9},{5... | collective-permute-start | bytes 196616 | tf_op jit(solution)/shard_map/ppermute | solution.py:189
  25.0 0.0 collective-permute-done.refs_1_
  25.0 0.6 %collective-permute-start.4 = (bf16[64,512]{1,0:T(8,128)(2,1)S(1)}, bf16[64,512]{1,0:T(8,128)(2,1)S(1)}, u32[]{:S(2)}, u32[]{:S(2)}) collective-permute-start(bf16[64,512]{1,0:T(8,128)(2,1)S(1)} %pad_maximum_fusion.refs_4_), channel_id=1, source_target_pairs={{0,4},{4,0},{8,12},{12,8},{16,20},{20,16},{24,28},{28,24},{1,5},{5... | collective-permute-start | bytes 196616 | tf_op jit(solution)/shard_map/ppermute | solution.py:189
  25.6 0.0 collective-permute-done.1.refs_2_
  25.6 0.0 collective-permute-done.2.refs_3_
  25.6 1.8 %collective-permute-done.6.refs_7_ = bf16[64,512]{1,0:T(8,128)(2,1)S(1)} collective-permute-done((bf16[64,512]{1,0:T(8,128)(2,1)S(1)}, bf16[64,512]{1,0:T(8,128)(2,1)S(1)}, u32[]{:S(2)}, u32[]{:S(2)}) %collective-permute-start.6) | collective-permute-done | bytes 65568 | tf_op jit(solution)/shard_map/ppermute | solution.py:189
  27.4 0.6 %collective-permute-done.5.refs_6_ = bf16[64,512]{1,0:T(8,128)(2,1)S(1)} collective-permute-done((bf16[64,512]{1,0:T(8,128)(2,1)S(1)}, bf16[64,512]{1,0:T(8,128)(2,1)S(1)}, u32[]{:S(2)}, u32[]{:S(2)}) %collective-permute-start.5) | collective-permute-done | bytes 65568 | tf_op jit(solution)/shard_map/ppermute | solution.py:189
  28.0 1.3 %collective-permute-done.4.refs_5_ = bf16[64,512]{1,0:T(8,128)(2,1)S(1)} collective-permute-done((bf16[64,512]{1,0:T(8,128)(2,1)S(1)}, bf16[64,512]{1,0:T(8,128)(2,1)S(1)}, u32[]{:S(2)}, u32[]{:S(2)}) %collective-permute-start.4) | collective-permute-done | bytes 65568 | tf_op jit(solution)/shard_map/ppermute | solution.py:189
  29.3 0.3 shard_map.112
  29.5 0.1 collective-permute-start.7
  29.6 0.0 all-to-all-done
  29.6 0.2 shard_map.113
  29.9 3.0 %collective-permute-start.8 = (bf16[96,256]{1,0:T(8,128)(2,1)S(1)}, bf16[96,256]{1,0:T(8,128)(2,1)S(1)}, u32[]{:S(2)}, u32[]{:S(2)}) collective-permute-start(bf16[96,256]{1,0:T(8,128)(2,1)S(1)} %get-tuple-element.38), channel_id=1, source_target_pairs={{0,16},{4,20},{8,24},{12,28},{16,0},{20,4},{24,8},{28,12},{1,17},{... | collective-permute-start | bytes 147464 | tf_op jit(solution)/shard_map/ppermute | solution.py:189
  32.8 4.0 %collective-permute-done.7.other_ref = bf16[192,256]{1,0:T(8,128)(2,1)S(1)} collective-permute-done((bf16[192,256]{1,0:T(8,128)(2,1)S(1)}, bf16[192,256]{1,0:T(8,128)(2,1)S(1)}, u32[]{:S(2)}, u32[]{:S(2)}) %collective-permute-start.7) | collective-permute-done | bytes 98336 | tf_op jit(solution)/shard_map/ppermute | solution.py:189
  36.8 0.5 collective-permute-done.8.down_other_ref
  37.4 1.1 %shard_map.114 = (bf16[288,256]{1,0:T(8,128)(2,1)S(1)}, bf16[256,640]{1,0:T(8,128)(2,1)}) custom-call(f32[192,256]{1,0:T(8,128)S(1)} %get-tuple-element.33.own_ref, bf16[192,256]{1,0:T(8,128)(2,1)S(1)} %collective-permute-done.7.other_ref, f32[96,256]{1,0:T(8,128)S(1)} %get-tuple-element.37.down_ref, ...), custom_call_target="tpu_custom_call" | custom-call | tf_op jit(solution)/shard_map/pallas_call | solution.py:24
  38.4 3.2 %all-to-all-start.1 = ((bf16[32,8,640]{2,1,0:T(8,128)(2,1)}), bf16[32,8,640]{2,1,0:T(8,128)(2,1)S(1)}, u32[]{:S(2)}, u32[]{:S(2)}) async-start(bf16[32,8,640]{2,1,0:T(8,128)(2,1)} %bitcast.14), calls=%async_computation.1 | async-start | bytes 655360 | tf_op jit(solution)/shard_map/all_to_all | solution.py:246
  41.6 0.3 shard_map.116
  41.9 1.8 %collective-permute-start.9 = (bf16[288,128]{1,0:T(8,128)(2,1)S(1)}, bf16[288,128]{1,0:T(8,128)(2,1)S(1)}, u32[]{:S(2)}, u32[]{:S(2)}) collective-permute-start(bf16[288,128]{1,0:T(8,128)(2,1)S(1)} %get-tuple-element.45), channel_id=1, source_target_pairs={{0,4},{4,0},{8,12},{12,8},{16,20},{20,16},{24,28},{28,24},{1,5},{5... | collective-permute-start | bytes 221192 | tf_op jit(solution)/shard_map/ppermute | solution.py:189
  43.8 1.5 %collective-permute-start.10 = (bf16[288,128]{1,0:T(8,128)(2,1)S(1)}, bf16[288,128]{1,0:T(8,128)(2,1)S(1)}, u32[]{:S(2)}, u32[]{:S(2)}) collective-permute-start(bf16[288,128]{1,0:T(8,128)(2,1)S(1)} %get-tuple-element.46), channel_id=1, source_target_pairs={{0,8},{4,12},{8,0},{12,4},{16,24},{20,28},{24,16},{28,20},{1,9},{5... | collective-permute-start | bytes 221192 | tf_op jit(solution)/shard_map/ppermute | solution.py:189
  45.2 0.3 collective-permute-start.11
  45.5 2.9 %collective-permute-done.9.refs_1_ = bf16[288,128]{1,0:T(8,128)(2,1)S(1)} collective-permute-done((bf16[288,128]{1,0:T(8,128)(2,1)S(1)}, bf16[288,128]{1,0:T(8,128)(2,1)S(1)}, u32[]{:S(2)}, u32[]{:S(2)}) %collective-permute-start.9) | collective-permute-done | bytes 73760 | tf_op jit(solution)/shard_map/ppermute | solution.py:189
  48.4 2.4 %collective-permute-done.10.refs_2_ = bf16[288,128]{1,0:T(8,128)(2,1)S(1)} collective-permute-done((bf16[288,128]{1,0:T(8,128)(2,1)S(1)}, bf16[288,128]{1,0:T(8,128)(2,1)S(1)}, u32[]{:S(2)}, u32[]{:S(2)}) %collective-permute-start.10) | collective-permute-done | bytes 73760 | tf_op jit(solution)/shard_map/ppermute | solution.py:189
  50.8 3.0 %collective-permute-done.11.refs_3_ = bf16[288,128]{1,0:T(8,128)(2,1)S(1)} collective-permute-done((bf16[288,128]{1,0:T(8,128)(2,1)S(1)}, bf16[288,128]{1,0:T(8,128)(2,1)S(1)}, u32[]{:S(2)}, u32[]{:S(2)}) %collective-permute-start.11) | collective-permute-done | bytes 73760 | tf_op jit(solution)/shard_map/ppermute | solution.py:189
  53.8 1.0 %shard_map.117 = (f32[128,384]{1,0:T(8,128)}, f32[128,384]{1,0:T(8,128)}, f32[128,384]{1,0:T(8,128)}) custom-call(bf16[288,128]{1,0:T(8,128)(2,1)S(1)} %get-tuple-element.44.refs_0_, bf16[288,128]{1,0:T(8,128)(2,1)S(1)} %collective-permute-done.9.refs_1_, bf16[288,128]{1,0:T(8,128)(2,1)S(1)} %collective-permute-done.10.refs_2_, ...), custom_call_target="tpu_custom_call" | custom-call | tf_op jit(solution)/shard_map/pallas_call | solution.py:24
  54.8 0.0 copy-start.6
  54.8 0.0 all-to-all-done.1
  54.8 0.7 %copy-done.6 = bf16[1,128,8]{1,2,0:T(8,128)(2,1)S(1)} copy-done((bf16[1,128,8]{1,2,0:T(8,128)(2,1)S(1)}, bf16[1,128,8]{1,2,0:T(8,128)(2,1)}, u32[]{:S(2)}) %copy-start.6) | copy-done | bytes 2072
  55.5 1.0 %shard_map.115 = (bf16[128,1024]{1,0:T(8,128)(2,1)}, bf16[8,128]{1,0:T(8,128)(2,1)}) custom-call(s32[8,128]{1,0:T(8,128)S(1)} %bitcast.33, bf16[8,128]{1,0:T(8,128)(2,1)S(1)} %bitcast.35, bf16[32,128]{1,0:T(8,128)(2,1)S(1)} %get-tuple-element.28.hits_ref, bf16[256,640]{1,0:T(8,128)(2,1)S(1)} %bitcast.27), custom_call_target="tpu_custom_call" | custom-call | tf_op jit(solution)/shard_map/pallas_call | solution.py:24
  (2 shorter events, 0.0 us)
Async XLA Ops:
  0.6 0.7 %copy-start.4 = (s32[1,128,8]{1,2,0:T(8,128)S(1)}, s32[1,128,8]{1,2,0:T(8,128)}, u32[]{:S(2)}) copy-start(s32[1,128,8]{1,2,0:T(8,128)} %param.7) | copy-start | bytes 12292
  1.3 0.9 %copy-start = (bf16[1,128,1024]{2,1,0:T(8,128)(2,1)S(1)}, bf16[1,128,1024]{2,1,0:T(8,128)(2,1)}, u32[]{:S(2)}) copy-start(bf16[1,128,1024]{2,1,0:T(8,128)(2,1)} %param.9) | copy-start | bytes 786436
  2.3 0.7 %copy-start.5 = (bf16[1,128,8]{1,2,0:T(8,128)(2,1)S(1)}, bf16[1,128,8]{1,2,0:T(8,128)(2,1)}, u32[]{:S(2)}) copy-start(bf16[1,128,8]{1,2,0:T(8,128)(2,1)} %param.8) | copy-start | bytes 6148
  4.0 7.3 %copy-start.7 = (bf16[1,1,32,1024]{3,2,1,0:T(8,128)(2,1)S(1)}, bf16[1,1,32,1024]{3,2,1,0:T(8,128)(2,1)}, u32[]{:S(2)}) copy-start(bf16[1,1,32,1024]{3,2,1,0:T(8,128)(2,1)} %param.10) | copy-start | bytes 196612
  4.0 10.1 %copy-start.2 = (bf16[1,128,384]{2,1,0:T(8,128)(2,1)S(1)}, bf16[1,128,384]{2,1,0:T(8,128)(2,1)}, u32[]{:S(2)}) copy-start(bf16[1,128,384]{2,1,0:T(8,128)(2,1)} %param.12) | copy-start | bytes 294916
  4.0 10.1 %copy-start.3 = (bf16[1,128,384]{2,1,0:T(8,128)(2,1)S(1)}, bf16[1,128,384]{2,1,0:T(8,128)(2,1)}, u32[]{:S(2)}) copy-start(bf16[1,128,384]{2,1,0:T(8,128)(2,1)} %param.13) | copy-start | bytes 294916
  4.0 25.7 %all-to-all-start = ((bf16[32,8,512]{2,1,0:T(8,128)(2,1)}), bf16[32,8,512]{2,1,0:T(8,128)(2,1)S(1)}, u32[]{:S(2)}, u32[]{:S(2)}) async-start(bf16[32,8,512]{2,1,0:T(8,128)(2,1)} %bitcast.12), calls=%async_computation | async-start | bytes 524288 | tf_op jit(solution)/shard_map/all_to_all | solution.py:215
  11.3 2.8 %copy-start.1 = (bf16[1,128,384]{2,1,0:T(8,128)(2,1)S(1)}, bf16[1,128,384]{2,1,0:T(8,128)(2,1)}, u32[]{:S(2)}) copy-start(bf16[1,128,384]{2,1,0:T(8,128)(2,1)} %param.11) | copy-start | bytes 294916
  11.3 10.7 %collective-permute-start.3 = (bf16[32,512]{1,0:T(8,128)(2,1)S(1)}, bf16[32,512]{1,0:T(8,128)(2,1)S(1)}, u32[]{:S(2)}, u32[]{:S(2)}) collective-permute-start(bf16[32,512]{1,0:T(8,128)(2,1)S(1)} %get-tuple-element.52), channel_id=1, source_target_pairs={{0,16},{4,20},{8,24},{12,28},{16,0},{20,4},{24,8},{28,12},{1,17},{... | collective-permute-start | bytes 98312 | tf_op jit(solution)/shard_map/ppermute | solution.py:189
  14.3 10.7 %collective-permute-start = (bf16[288,128]{1,0:T(8,128)(2,1)S(1)}, bf16[288,128]{1,0:T(8,128)(2,1)S(1)}, u32[]{:S(2)}, u32[]{:S(2)}) collective-permute-start(bf16[288,128]{1,0:T(8,128)(2,1)S(1)} %get-tuple-element.30), channel_id=1, source_target_pairs={{0,4},{4,0},{8,12},{12,8},{16,20},{20,16},{24,28},{28,24},{1,5},{5... | collective-permute-start | bytes 221192 | tf_op jit(solution)/shard_map/ppermute | solution.py:189
  15.8 9.8 %collective-permute-start.1 = (bf16[288,128]{1,0:T(8,128)(2,1)S(1)}, bf16[288,128]{1,0:T(8,128)(2,1)S(1)}, u32[]{:S(2)}, u32[]{:S(2)}) collective-permute-start(bf16[288,128]{1,0:T(8,128)(2,1)S(1)} %get-tuple-element.31), channel_id=1, source_target_pairs={{0,8},{4,12},{8,0},{12,4},{16,24},{20,28},{24,16},{28,20},{1,9},{5... | collective-permute-start | bytes 221192 | tf_op jit(solution)/shard_map/ppermute | solution.py:189
  17.3 8.2 %collective-permute-start.2 = (bf16[288,128]{1,0:T(8,128)(2,1)S(1)}, bf16[288,128]{1,0:T(8,128)(2,1)S(1)}, u32[]{:S(2)}, u32[]{:S(2)}) collective-permute-start(bf16[288,128]{1,0:T(8,128)(2,1)S(1)} %get-tuple-element.32), channel_id=1, source_target_pairs={{0,12},{4,8},{8,4},{12,0},{16,28},{20,24},{24,20},{28,16},{1,13},{... | collective-permute-start | bytes 221192 | tf_op jit(solution)/shard_map/ppermute | solution.py:189
  22.1 5.3 %collective-permute-start.6 = (bf16[64,512]{1,0:T(8,128)(2,1)S(1)}, bf16[64,512]{1,0:T(8,128)(2,1)S(1)}, u32[]{:S(2)}, u32[]{:S(2)}) collective-permute-start(bf16[64,512]{1,0:T(8,128)(2,1)S(1)} %pad_maximum_fusion.refs_4_), channel_id=1, source_target_pairs={{0,12},{4,8},{8,4},{12,0},{16,28},{20,24},{24,20},{28,16},{1,13},{... | collective-permute-start | bytes 196616 | tf_op jit(solution)/shard_map/ppermute | solution.py:189
  22.9 5.1 %collective-permute-start.5 = (bf16[64,512]{1,0:T(8,128)(2,1)S(1)}, bf16[64,512]{1,0:T(8,128)(2,1)S(1)}, u32[]{:S(2)}, u32[]{:S(2)}) collective-permute-start(bf16[64,512]{1,0:T(8,128)(2,1)S(1)} %pad_maximum_fusion.refs_4_), channel_id=1, source_target_pairs={{0,8},{4,12},{8,0},{12,4},{16,24},{20,28},{24,16},{28,20},{1,9},{5... | collective-permute-start | bytes 196616 | tf_op jit(solution)/shard_map/ppermute | solution.py:189
  25.0 4.3 %collective-permute-start.4 = (bf16[64,512]{1,0:T(8,128)(2,1)S(1)}, bf16[64,512]{1,0:T(8,128)(2,1)S(1)}, u32[]{:S(2)}, u32[]{:S(2)}) collective-permute-start(bf16[64,512]{1,0:T(8,128)(2,1)S(1)} %pad_maximum_fusion.refs_4_), channel_id=1, source_target_pairs={{0,4},{4,0},{8,12},{12,8},{16,20},{20,16},{24,28},{28,24},{1,5},{5... | collective-permute-start | bytes 196616 | tf_op jit(solution)/shard_map/ppermute | solution.py:189
  29.5 7.3 %collective-permute-start.7 = (bf16[192,256]{1,0:T(8,128)(2,1)S(1)}, bf16[192,256]{1,0:T(8,128)(2,1)S(1)}, u32[]{:S(2)}, u32[]{:S(2)}) collective-permute-start(bf16[192,256]{1,0:T(8,128)(2,1)S(1)} %get-tuple-element.34), channel_id=1, source_target_pairs={{0,16},{4,20},{8,24},{12,28},{16,0},{20,4},{24,8},{28,12},{1,17},{... | collective-permute-start | bytes 294920 | tf_op jit(solution)/shard_map/ppermute | solution.py:189
  29.9 7.5 %collective-permute-start.8 = (bf16[96,256]{1,0:T(8,128)(2,1)S(1)}, bf16[96,256]{1,0:T(8,128)(2,1)S(1)}, u32[]{:S(2)}, u32[]{:S(2)}) collective-permute-start(bf16[96,256]{1,0:T(8,128)(2,1)S(1)} %get-tuple-element.38), channel_id=1, source_target_pairs={{0,16},{4,20},{8,24},{12,28},{16,0},{20,4},{24,8},{28,12},{1,17},{... | collective-permute-start | bytes 147464 | tf_op jit(solution)/shard_map/ppermute | solution.py:189
  38.4 16.4 %all-to-all-start.1 = ((bf16[32,8,640]{2,1,0:T(8,128)(2,1)}), bf16[32,8,640]{2,1,0:T(8,128)(2,1)S(1)}, u32[]{:S(2)}, u32[]{:S(2)}) async-start(bf16[32,8,640]{2,1,0:T(8,128)(2,1)} %bitcast.14), calls=%async_computation.1 | async-start | bytes 655360 | tf_op jit(solution)/shard_map/all_to_all | solution.py:246
  41.9 6.5 %collective-permute-start.9 = (bf16[288,128]{1,0:T(8,128)(2,1)S(1)}, bf16[288,128]{1,0:T(8,128)(2,1)S(1)}, u32[]{:S(2)}, u32[]{:S(2)}) collective-permute-start(bf16[288,128]{1,0:T(8,128)(2,1)S(1)} %get-tuple-element.45), channel_id=1, source_target_pairs={{0,4},{4,0},{8,12},{12,8},{16,20},{20,16},{24,28},{28,24},{1,5},{5... | collective-permute-start | bytes 221192 | tf_op jit(solution)/shard_map/ppermute | solution.py:189
  43.8 7.0 %collective-permute-start.10 = (bf16[288,128]{1,0:T(8,128)(2,1)S(1)}, bf16[288,128]{1,0:T(8,128)(2,1)S(1)}, u32[]{:S(2)}, u32[]{:S(2)}) collective-permute-start(bf16[288,128]{1,0:T(8,128)(2,1)S(1)} %get-tuple-element.46), channel_id=1, source_target_pairs={{0,8},{4,12},{8,0},{12,4},{16,24},{20,28},{24,16},{28,20},{1,9},{5... | collective-permute-start | bytes 221192 | tf_op jit(solution)/shard_map/ppermute | solution.py:189
  45.2 8.6 %collective-permute-start.11 = (bf16[288,128]{1,0:T(8,128)(2,1)S(1)}, bf16[288,128]{1,0:T(8,128)(2,1)S(1)}, u32[]{:S(2)}, u32[]{:S(2)}) collective-permute-start(bf16[288,128]{1,0:T(8,128)(2,1)S(1)} %get-tuple-element.47), channel_id=1, source_target_pairs={{0,12},{4,8},{8,4},{12,0},{16,28},{20,24},{24,20},{28,16},{1,13},{... | collective-permute-start | bytes 221192 | tf_op jit(solution)/shard_map/ppermute | solution.py:189
  54.8 0.7 %copy-start.6 = (bf16[1,128,8]{1,2,0:T(8,128)(2,1)S(1)}, bf16[1,128,8]{1,2,0:T(8,128)(2,1)}, u32[]{:S(2)}) copy-start(bf16[1,128,8]{1,2,0:T(8,128)(2,1)} %param.8) | copy-start | bytes 6148

commit v2 on v0

--- a/solution.py
+++ b/solution.py
@@ -1,10 +1,295 @@
 import jax
 import jax.numpy as jnp
 from jax import lax
+from jax.experimental import pallas as pl
+from jax.experimental.pallas import tpu as pltpu
+from jax.sharding import Mesh
 from jax.sharding import PartitionSpec as P
 
 TOPK = 8
 EXP_DEV = 4
+PARTS = 4
+CAP = 8
+LANES = 128
+F32 = jnp.float32
+BF16 = jnp.bfloat16
+
+
+def dot(left, right, ldim, rdim):
+    return lax.dot_general(
+        left, right, (((ldim,), (rdim,)), ((), ())), preferred_element_type=F32
+    )
+
+
+def call(kernel, *args, out, scratch=(), space=pltpu.VMEM, after=(), cost=None):
+    spec = pl.BlockSpec(memory_space=pltpu.VMEM)
+    return pl.pallas_call(
+        kernel,
+        out_shape=[jax.ShapeDtypeStruct(s, d) for s, d in out],
+        in_specs=[pl.BlockSpec(memory_space=space)] * len(args)
+        + [pl.BlockSpec(memory_space=pl.ANY)] * len(after),
+        out_specs=[spec] * len(out),
+        scratch_shapes=list(scratch),
+        cost_estimate=cost,
+        compiler_params=pltpu.CompilerParams(vmem_limit_bytes=32 << 20),
+    )(*args, *after)
+
+
+def in_hbm(*arrays):
+    return [pltpu.with_memory_space_constraint(a, pltpu.HBM) for a in arrays]
+
+
+def fetch(sources, targets, sems):
+    copies = [
+        pltpu.make_async_copy(source, target, sems.at[n])
+        for n, (source, target) in enumerate(zip(sources, targets))
+    ]
+    for copy in copies:
+        copy.start()
+    return copies
+
+
+def position():
+    return lax.axis_index("q"), lax.axis_index("p")
+
+
+def block(index, size):
+    return pl.ds(pl.multiple_of(index * size, size), size)
+
+
+def spread_kernel(gate_ref, up_ref, down_ref, saved_ref, both_ref, last_ref, *rest):
+    mine_ref, across_ref, saved, sems = rest
+    hidden = gate_ref.shape[1]
+    half = mine_ref.shape[1]
+    q, _ = position()
+    targets = (both_ref.at[:, :hidden], both_ref.at[:, hidden:], last_ref)
+    copies = fetch((saved_ref, gate_ref, up_ref, down_ref), (saved, *targets), sems)
+    copies[0].wait()
+    mine_ref[...] = saved[:, block(q, half)]
+    across_ref[...] = saved[:, block(1 - q, half)]
+    for copy in copies[1:]:
+        copy.wait()
+
+
+def route_kernel(ids_hbm, scales_hbm, grads_hbm, send_ref, hits_ref, ids_ref, scales_ref, *rest):
+    grads_ref, sems = rest
+    copies = fetch((ids_hbm, scales_hbm, grads_hbm), (ids_ref, scales_ref, grads_ref), sems)
+    slots, tokens = hits_ref.shape
+    owners = slots // CAP
+    half = send_ref.shape[1]
+    earlier = lax.broadcasted_iota(jnp.int32, (tokens, tokens), 0) < (
+        lax.broadcasted_iota(jnp.int32, (tokens, tokens), 1)
+    )
+    before = jnp.where(earlier, 1.0, 0.0).astype(BF16)
+    slot = lax.broadcasted_iota(jnp.int32, (CAP, tokens), 0).astype(F32)
+    copies[0].wait()
+    copies[1].wait()
+    ids = ids_ref[...]
+    weights = scales_ref[...].astype(F32)
+    hits, scales = [], []
+    for j in range(owners):
+        match = ids == j * EXP_DEV
+        hits.append(jnp.sum(jnp.where(match, 1.0, 0.0), axis=0, keepdims=True))
+        scales.append(jnp.sum(jnp.where(match, weights, 0.0), axis=0, keepdims=True))
+    pad = [jnp.zeros((1, tokens), F32)] * (-owners % 8)
+    hit = jnp.concatenate(hits + pad, axis=0)
+    place = dot(hit.astype(BF16), before, 1, 0)
+    chosen, scaled = [], []
+    for j in range(owners):
+        here = (place[j : j + 1] == slot) & (hits[j] > 0.0)
+        chosen.append(jnp.where(here, 1.0, 0.0))
+        scaled.append(jnp.where(here, scales[j], 0.0))
+    hits_ref[...] = jnp.concatenate(chosen, axis=0).astype(BF16)
+    picks = jnp.concatenate(scaled, axis=0).astype(BF16)
+    copies[2].wait()
+    rows = dot(picks, grads_ref[...], 1, 0).astype(BF16)
+    for h in range(2):
+        send_ref[h * slots : (h + 1) * slots, :] = rows[:, h * half : (h + 1) * half]
+
+
+def gate_up_kernel(mine_ref, theirs_ref, *refs):
+    weights, (pair_ref, own_ref, sent_ref) = refs[:PARTS], refs[PARTS:]
+    q, p = position()
+    slots = mine_ref.shape[0]
+    width = weights[0].shape[0]
+    pair_ref[block(q, slots), :] = mine_ref[...]
+    pair_ref[block(1 - q, slots), :] = theirs_ref[...]
+    total = None
+    for k in range(PARTS):
+        term = dot(pair_ref[:, block(p ^ k, width)], weights[k][...], 1, 0)
+        total = term if total is None else total + term
+    own_ref[...] = total
+    sent_ref[...] = total.astype(BF16)
+
+
+def down_kernel(routed_ref, *refs):
+    weights, (own_ref, sent_ref) = refs[:PARTS], refs[PARTS:]
+    _, p = position()
+    width = weights[0].shape[0]
+    total = None
+    for k in range(PARTS):
+        term = dot(routed_ref[:, block(p ^ k, width)], weights[k][...], 1, 0)
+        total = term if total is None else total + term
+    own_ref[...] = total
+    sent_ref[...] = total.astype(BF16)
+
+
+def delta_kernel(gate_up_ref, other_ref, down_ref, down_other_ref, pair_ref, routed_ref, *refs):
+    weights, back_ref, sends = refs[:PARTS], refs[PARTS], refs[PARTS + 1 :]
+    _, p = position()
+    width = weights[0].shape[0]
+    hidden_width = down_ref.shape[1]
+    half = pair_ref.shape[1]
+    both = gate_up_ref[...] + other_ref[...].astype(F32)
+    hidden_grad = down_ref[...] + down_other_ref[...].astype(F32)
+    pre_gate, pre_up = both[:, :hidden_width], both[:, hidden_width:]
+    sigmoid = jax.nn.sigmoid(pre_gate)
+    activated = pre_gate * sigmoid
+    hidden = (activated * pre_up).astype(BF16)
+    gate_delta = hidden_grad * pre_up * sigmoid * (1.0 + pre_gate * (1.0 - sigmoid))
+    gate_delta = gate_delta.astype(BF16)
+    up_delta = (hidden_grad * activated).astype(BF16)
+    route = jnp.sum(hidden.astype(F32) * hidden_grad, axis=1, keepdims=True)
+    back_ref[:, half:] = jnp.broadcast_to(route, (route.shape[0], LANES)).astype(BF16)
+    for k in range(PARTS):
+        lanes = block(p ^ k, width)
+        back_ref[:, lanes] = (
+            dot(gate_delta, weights[k][:, :hidden_width], 1, 1)
+            + dot(up_delta, weights[k][:, hidden_width : 2 * hidden_width], 1, 1)
+        ).astype(BF16)
+        sends[k][:, :hidden_width] = gate_delta
+        sends[k][:, hidden_width : 2 * hidden_width] = up_delta
+        sends[k][:, 2 * hidden_width : 3 * hidden_width] = hidden
+        sends[k][:, 3 * hidden_width : 3 * hidden_width + width] = pair_ref[:, lanes]
+        sends[k][:, 3 * hidden_width + width :] = routed_ref[:, lanes]
+
+
+def grads_step(replicas):
+    def grads_kernel(*refs):
+        parts, outs = refs[:PARTS], refs[PARTS:]
+        hidden_width = outs[0].shape[1]
+        width = outs[0].shape[0]
+        start = 3 * hidden_width
+        for i in range(3):
+            first = start if i < 2 else start + width
+            total = None
+            for part in parts:
+                term = dot(
+                    part[:, first : first + width],
+                    part[:, i * hidden_width : (i + 1) * hidden_width],
+                    0,
+                    0,
+                )
+                total = term if total is None else total + term
+            outs[i][...] = total / replicas
+
+    return grads_kernel
+
+
+def tokens_kernel(ids_ref, scales_ref, hits_ref, rows_ref, _, input_grad_ref, route_ref):
+    slots = hits_ref.shape[0]
+    half = input_grad_ref.shape[1] // 2
+    hits = hits_ref[...]
+    for h in range(2):
+        input_grad_ref[:, h * half : (h + 1) * half] = dot(
+            hits, rows_ref[h * slots : (h + 1) * slots, :half], 0, 0
+        ).astype(BF16)
+    spread = hits.astype(F32) * rows_ref[0:slots, half:].astype(F32)
+    ids = ids_ref[...]
+    out = jnp.zeros(ids.shape, F32)
+    for j in range(slots // CAP):
+        value = jnp.sum(spread[j * CAP : (j + 1) * CAP], axis=0, keepdims=True)
+        out = jnp.where(ids == j * EXP_DEV, value, out)
+    route_ref[...] = (out / scales_ref[...].astype(F32)).astype(BF16)
+
+
+def body(expert_ids, route_weights, out_grad, saved_inputs, gate_weight, up_weight, down_weight):
+    owners = lax.axis_size("exp")
+    replicas = lax.axis_size("q") * PARTS
+    tokens, features = out_grad.shape[1:]
+    slots = saved_inputs.shape[2]
+    width, hidden_width = gate_weight.shape[1:]
+    half, rows = features // 2, 2 * slots
+
+    def in_half(value, mask):
+        return lax.ppermute(value, "p", [(i, i ^ mask) for i in range(PARTS)])
+
+    def across_halves(value):
+        return lax.ppermute(value, "q", [(0, 1), (1, 0)])
+
+    def exchange(value):
+        blocks = value.reshape(2 * owners, CAP, value.shape[1])
+        return lax.all_to_all(blocks, ("q", "exp"), 0, 0, tiled=True).reshape(value.shape)
+
+    both, last, mine, across = call(
+        spread_kernel,
+        *in_hbm(gate_weight[0], up_weight[0], down_weight[0], saved_inputs[0, 0]),
+        out=[((width, 2 * hidden_width), BF16), ((width, hidden_width), BF16)]
+        + [((slots, half), BF16)] * 2,
+        scratch=[pltpu.VMEM((slots, features), BF16), pltpu.SemaphoreType.DMA((4,))],
+        space=pltpu.HBM,
+    )
+    theirs = across_halves(across)
+    both = [both] + [in_half(both, k) for k in range(1, PARTS)]
+    last = [last] + [in_half(last, k) for k in range(1, PARTS)]
+    sent, hits, ids, scales = call(
+        route_kernel,
+        *in_hbm(expert_ids[0].T, route_weights[0].T, out_grad[0]),
+        out=[
+            ((rows, half), BF16),
+            ((slots, tokens), BF16),
+            ((TOPK, tokens), jnp.int32),
+            ((TOPK, tokens), BF16),
+        ],
+        scratch=[pltpu.VMEM((tokens, features), BF16), pltpu.SemaphoreType.DMA((3,))],
+        space=pltpu.HBM,
+    )
+    routed = exchange(sent)
+    pair, gate_up, partial = call(
+        gate_up_kernel,
+        mine,
+        theirs,
+        *both,
+        out=[
+            ((rows, half), BF16),
+            ((rows, 2 * hidden_width), F32),
+            ((rows, 2 * hidden_width), BF16),
+        ],
+    )
+    other = across_halves(partial)
+    down, partial = call(
+        down_kernel,
+        routed,
+        *last,
+        out=[((rows, hidden_width), F32), ((rows, hidden_width), BF16)],
+    )
+    back, *sends = call(
+        delta_kernel,
+        gate_up,
+        other,
+        down,
+        across_halves(partial),
+        pair,
+        routed,
+        *both,
+        out=[((rows, half + LANES), BF16)]
+        + [((rows, 3 * hidden_width + 2 * width), BF16)] * PARTS,
+    )
+    returned = exchange(back)
+    sends = [sends[0]] + [in_half(sends[k], k) for k in range(1, PARTS)]
+    gate_grad, up_grad, down_grad = call(
+        grads_step(replicas), *sends, out=[((width, hidden_width), F32)] * 3
+    )
+    input_grad, route_grad = call(
+        tokens_kernel,
+        ids,
+        scales,
+        hits,
+        returned,
+        after=in_hbm(gate_grad),
+        out=[((tokens, features), BF16), ((TOPK, tokens), BF16)],
+    )
+    return (input_grad[None], route_grad.T[None], gate_grad[None], up_grad[None], down_grad[None])
 
 
 def slot_table(block_ids, slot_count, owners):
@@ -33,7 +318,7 @@
     )
 
 
-def body(expert_ids, route_weights, out_grad, saved_inputs, gate_weight, up_weight, down_weight):
+def general_body(expert_ids, route_weights, out_grad, saved_inputs, gate_weight, up_weight, down_weight):
     owners = lax.axis_size("exp")
     replicas = lax.axis_size("rep")
     tokens_here = out_grad.shape[1]
@@ -138,20 +423,26 @@
 
 
 def solution(mesh):
+    replicas, owners = mesh.shape["rep"], mesh.shape["exp"]
+    if replicas == 2 * PARTS:
+        step, rep = body, ("q", "p")
+        mesh = Mesh(mesh.devices.reshape(2, PARTS, owners), ("q", "p", "exp"))
+    else:
+        step, rep = general_body, "rep"
     in_specs = (
-        P("rep", "exp", None),
-        P("rep", "exp", None),
-        P("rep", "exp", None),
-        P("rep", "exp", None, None),
-        P("exp", "rep", None),
-        P("exp", "rep", None),
-        P("exp", "rep", None),
+        P(rep, "exp", None),
+        P(rep, "exp", None),
+        P(rep, "exp", None),
+        P(rep, "exp", None, None),
+        P("exp", rep, None),
+        P("exp", rep, None),
+        P("exp", rep, None),
     )
     out_specs = (
-        P("rep", "exp", None),
-        P("rep", "exp", None),
-        P("exp", "rep", None),
-        P("exp", "rep", None),
-        P("exp", "rep", None),
-    )
-    return jax.shard_map(body, mesh=mesh, in_specs=in_specs, out_specs=out_specs, check_vma=False)
+        P(rep, "exp", None),
+        P(rep, "exp", None),
+        P("exp", rep, None),
+        P("exp", rep, None),
+        P("exp", rep, None),
+    )
+    return jax.shard_map(step, mesh=mesh, in_specs=in_specs, out_specs=out_specs, check_vma=False)

time: 240 us -> 45.6 us (0.19)
  blocking collectives: 111 us -> 0 us
  waiting for transfers between devices: 88.7 us -> 13 us
  starting transfers between devices: 7.52 us -> 24.9 us
  between operations: 14.2 us -> 0.69 us
  other arithmetic: 8.79 us -> 0 us
  Pallas kernels: 0 us -> 6.67 us
  local copies, waits for them, and re-layouts: 5.86 us -> 0 us
  matrix products: 3.3 us -> 0 us
    all_gather x3 -> x0, blocking collectives: 97.4 us -> none  [the longest x1 33 us: body(): lax.all_gather(gate_weight[0], 'rep', axis=0, tiled=True)]
    reduce_scatter x1 -> x0, waiting for transfers between devices: 85.4 us -> none  [body(): lax.psum_scatter(jnp.concatenate([jnp.concatenate([first_contract(inputs_...]
    ppermute x0 -> x12, starting transfers between devices: none -> 18.2 us  [the longest x9 12.5 us: in_half(): return lax.ppermute(value, 'p', [(i, i ^ mask) for i in range(PARTS)])]
    all_to_all x2 -> x0, blocking collectives: 13.3 us -> none  [the longest x1 7.19 us: body(): lax.all_to_all(slot_route.reshape(owners, capacity), 'exp', split_axis=0,...]
    ppermute x0 -> x12, waiting for transfers between devices: none -> 11.6 us  [the longest x9 7.27 us: in_half(): return lax.ppermute(value, 'p', [(i, i ^ mask) for i in range(PARTS)])]
    pallas_call x0 -> x7, Pallas kernels: none -> 6.67 us  [call(): pl.pallas_call(kernel, out_shape=[jax.ShapeDtypeStruct(s, d) for s, d in...]
    unnamed x18 -> x0, local copies, waits for them, and re-layouts: 4.08 us -> none
    dot_general x8 -> x0, matrix products: 3.3 us -> none  [the longest x2 1.33 us: second_contract(): lax.dot_general(left, right, (((1,), (1,)), ((), ())), preferred_element_...]
  transfers between devices with their start and end apart: 3 -> 14, of which waited for: 2 -> 6; matrix products, arithmetic and copies ran while one was open for 2% -> 0% of each run, Pallas kernels for 0% -> 8%
where the time goes in v2:
time: 45.6 us; the launch traced here: 45.3 us
  starting transfers between devices  24.9 us (55%)
  waiting for transfers between devices  13 us (29%)
  Pallas kernels  6.67 us (15%)
  between operations  0.69 us (2%)
    ppermute x9, starting transfers between devices, in_half(): return lax.ppermute(value, 'p', [(i, i ^ mask) for i in range(PARTS)])  12.5 us
    ppermute x9, waiting for transfers between devices, in_half(): return lax.ppermute(value, 'p', [(i, i ^ mask) for i in range(PARTS)])  7.27 us
    all_to_all x2, starting transfers between devices, exchange(): lax.all_to_all(blocks, ('q', 'exp'), 0, 0, tiled=True).reshape(value.shape)  6.72 us
    pallas_call x7, Pallas kernels, call(): pl.pallas_call(kernel, out_shape=[jax.ShapeDtypeStruct(s, d) for s, d in...  6.67 us
    ppermute x3, starting transfers between devices, across_halves(): return lax.ppermute(value, 'q', [(0, 1), (1, 0)])  5.72 us
    ppermute x3, waiting for transfers between devices, across_halves(): return lax.ppermute(value, 'q', [(0, 1), (1, 0)])  4.33 us
    all_to_all x2, waiting for transfers between devices, exchange(): lax.all_to_all(blocks, ('q', 'exp'), 0, 0, tiled=True).reshape(value.shape)  1.39 us
  transfers between devices with their start and end apart: 14, of which 6 were waited for; matrix products, arithmetic and copies ran while one was open for 0% of the time, Pallas kernels for 8%

profile of v2, /device:TPU:0, one launch (start us, length us, event | category | flops | bytes accessed | tf_op | source)
XLA Modules:
  0.0 45.3 jit_solution(13733587942074437913)
XLA Ops:
  0.6 1.1 %shard_map.111 = (bf16[128,768]{1,0:T(8,128)(2,1)S(1)}, bf16[128,384]{1,0:T(8,128)(2,1)S(1)}, bf16[32,512]{1,0:T(8,128)(2,1)S(1)}, bf16[32,512]{1,0:T(8,128)(2,1)S(1)}) custom-call(bf16[128,384]{1,0:T(8,128)(2,1)} %bitcast.27, bf16[128,384]{1,0:T(8,128)(2,1)} %bitcast.28, bf16[128,384]{1,0:T(8,128)(2,1)} %bitcast.29, bf16[32,1024]{1,0:T(8,128)(2,1)} %bitcast.30), custom_call_target="tpu_custom_call" | custom-call | tf_op jit(solution)/shard_map/pallas_call | solution.py:26
  1.7 4.0 %collective-permute-start.3 = (bf16[128,768]{1,0:T(8,128)(2,1)S(1)}, bf16[128,768]{1,0:T(8,128)(2,1)S(1)}, u32[]{:S(2)}, u32[]{:S(2)}) collective-permute-start(bf16[128,768]{1,0:T(8,128)(2,1)S(1)} %get-tuple-element.33.refs_0_), channel_id=1, source_target_pairs={{0,12},{4,8},{8,4},{12,0},{1,13},{5,9},{9,5},{13,1},{2,14},{6,10},... | collective-permute-start | bytes 589832 | tf_op jit(solution)/shard_map/ppermute | solution.py:215
  5.7 0.4 collective-permute-start.2
  6.2 0.2 collective-permute-start.1
  6.4 2.9 %collective-permute-start = (bf16[32,512]{1,0:T(8,128)(2,1)S(1)}, bf16[32,512]{1,0:T(8,128)(2,1)S(1)}, u32[]{:S(2)}, u32[]{:S(2)}) collective-permute-start(bf16[32,512]{1,0:T(8,128)(2,1)S(1)} %get-tuple-element.32), channel_id=1, source_target_pairs={{0,16},{16,0},{1,17},{17,1},{2,18},{18,2},{3,19},{19,3},{4,20},{20... | collective-permute-start | bytes 98312 | tf_op jit(solution)/shard_map/ppermute | solution.py:218
  9.3 1.8 %shard_map.110 = (bf16[64,512]{1,0:T(8,128)(2,1)}, bf16[32,128]{1,0:T(8,128)(2,1)S(1)}, s32[8,128]{1,0:T(8,128)S(1)}, bf16[8,128]{1,0:T(8,128)(2,1)S(1)}) custom-call(s32[8,128]{1,0:T(8,128)} %bitcast.31, bf16[8,128]{1,0:T(8,128)(2,1)} %bitcast.32, bf16[128,1024]{1,0:T(8,128)(2,1)} %bitcast.25), custom_call_target="tpu_custom_call" | custom-call | tf_op jit(solution)/shard_map/pallas_call | solution.py:26
  11.1 3.4 %all-to-all-start = ((bf16[8,8,512]{2,1,0:T(8,128)(2,1)}), bf16[8,8,512]{2,1,0:T(8,128)(2,1)S(1)}, u32[]{:S(2)}, u32[]{:S(2)}) async-start(bf16[8,8,512]{2,1,0:T(8,128)(2,1)} %bitcast.9), calls=%async_computation | async-start | bytes 131072 | tf_op jit(solution)/shard_map/all_to_all | solution.py:222
  14.5 2.6 %collective-permute-start.7 = (bf16[128,384]{1,0:T(8,128)(2,1)S(1)}, bf16[128,384]{1,0:T(8,128)(2,1)S(1)}, u32[]{:S(2)}, u32[]{:S(2)}) collective-permute-start(bf16[128,384]{1,0:T(8,128)(2,1)S(1)} %get-tuple-element.37.refs_0_), channel_id=1, source_target_pairs={{0,12},{4,8},{8,4},{12,0},{1,13},{5,9},{9,5},{13,1},{2,14},{6,10},... | collective-permute-start | bytes 294920 | tf_op jit(solution)/shard_map/ppermute | solution.py:215
  17.1 0.0 collective-permute-done.theirs_ref
  17.1 1.3 %collective-permute-start.6 = (bf16[128,384]{1,0:T(8,128)(2,1)S(1)}, bf16[128,384]{1,0:T(8,128)(2,1)S(1)}, u32[]{:S(2)}, u32[]{:S(2)}) collective-permute-start(bf16[128,384]{1,0:T(8,128)(2,1)S(1)} %get-tuple-element.37.refs_0_), channel_id=1, source_target_pairs={{0,8},{4,12},{8,0},{12,4},{1,9},{5,13},{9,1},{13,5},{2,10},{6,14},... | collective-permute-start | bytes 294920 | tf_op jit(solution)/shard_map/ppermute | solution.py:215
  18.3 0.0 collective-permute-done.3.refs_3_
  18.3 0.5 %collective-permute-start.5 = (bf16[128,384]{1,0:T(8,128)(2,1)S(1)}, bf16[128,384]{1,0:T(8,128)(2,1)S(1)}, u32[]{:S(2)}, u32[]{:S(2)}) collective-permute-start(bf16[128,384]{1,0:T(8,128)(2,1)S(1)} %get-tuple-element.37.refs_0_), channel_id=1, source_target_pairs={{0,4},{4,0},{8,12},{12,8},{1,5},{5,1},{9,13},{13,9},{2,6},{6,2},{1... | collective-permute-start | bytes 294920 | tf_op jit(solution)/shard_map/ppermute | solution.py:215
  18.8 0.0 collective-permute-done.2.refs_2_
  18.8 0.0 collective-permute-done.1.refs_1_
  18.8 0.3 shard_map.112
  19.1 2.1 %collective-permute-start.4 = (bf16[64,768]{1,0:T(8,128)(2,1)S(1)}, bf16[64,768]{1,0:T(8,128)(2,1)S(1)}, u32[]{:S(2)}, u32[]{:S(2)}) collective-permute-start(bf16[64,768]{1,0:T(8,128)(2,1)S(1)} %get-tuple-element.35), channel_id=1, source_target_pairs={{0,16},{16,0},{1,17},{17,1},{2,18},{18,2},{3,19},{19,3},{4,20},{20... | collective-permute-start | bytes 294920 | tf_op jit(solution)/shard_map/ppermute | solution.py:218
  21.2 0.6 %collective-permute-done.7.refs_3_ = bf16[128,384]{1,0:T(8,128)(2,1)S(1)} collective-permute-done((bf16[128,384]{1,0:T(8,128)(2,1)S(1)}, bf16[128,384]{1,0:T(8,128)(2,1)S(1)}, u32[]{:S(2)}, u32[]{:S(2)}) %collective-permute-start.7) | collective-permute-done | bytes 98336 | tf_op jit(solution)/shard_map/ppermute | solution.py:215
  21.8 3.6 %collective-permute-done.6.refs_2_ = bf16[128,384]{1,0:T(8,128)(2,1)S(1)} collective-permute-done((bf16[128,384]{1,0:T(8,128)(2,1)S(1)}, bf16[128,384]{1,0:T(8,128)(2,1)S(1)}, u32[]{:S(2)}, u32[]{:S(2)}) %collective-permute-start.6) | collective-permute-done | bytes 98336 | tf_op jit(solution)/shard_map/ppermute | solution.py:215
  25.3 0.0 collective-permute-done.5.refs_1_
  25.3 0.0 all-to-all-done
  25.3 0.2 shard_map.113
  25.6 0.7 %collective-permute-start.8 = (bf16[64,384]{1,0:T(8,128)(2,1)S(1)}, bf16[64,384]{1,0:T(8,128)(2,1)S(1)}, u32[]{:S(2)}, u32[]{:S(2)}) collective-permute-start(bf16[64,384]{1,0:T(8,128)(2,1)S(1)} %get-tuple-element.39), channel_id=1, source_target_pairs={{0,16},{16,0},{1,17},{17,1},{2,18},{18,2},{3,19},{19,3},{4,20},{20... | collective-permute-start | bytes 147464 | tf_op jit(solution)/shard_map/ppermute | solution.py:218
  26.3 4.3 %collective-permute-done.8.down_other_ref = bf16[64,384]{1,0:T(8,128)(2,1)S(1)} collective-permute-done((bf16[64,384]{1,0:T(8,128)(2,1)S(1)}, bf16[64,384]{1,0:T(8,128)(2,1)S(1)}, u32[]{:S(2)}, u32[]{:S(2)}) %collective-permute-start.8) | collective-permute-done | bytes 49184 | tf_op jit(solution)/shard_map/ppermute | solution.py:218
  30.6 0.0 collective-permute-done.4.other_ref
  30.6 1.1 %shard_map.114 = (bf16[64,640]{1,0:T(8,128)(2,1)}, bf16[64,1408]{1,0:T(8,128)(2,1)S(1)}, bf16[64,1408]{1,0:T(8,128)(2,1)S(1)}, bf16[64,1408]{1,0:T(8,128)(2,1)S(1)}, bf16[64,1408]{1,0:T(8,128)(2,1)S(1)}) custom-call(f32[64,768]{1,0:T(8,128)S(1)} %get-tuple-element.34.gate_up_ref, bf16[64,768]{1,0:T(8,128)(2,1)S(1)} %collective-permute-done.4.other_ref, ...), custom_call_target="tpu_custom_call" | custom-call | tf_op jit(solution)/shard_map/pallas_call | solution.py:26
  31.7 0.1 collective-permute-start.9
  31.9 0.3 collective-permute-start.10
  32.2 3.1 %collective-permute-start.11 = (bf16[64,1408]{1,0:T(8,128)(2,1)S(1)}, bf16[64,1408]{1,0:T(8,128)(2,1)S(1)}, u32[]{:S(2)}, u32[]{:S(2)}) collective-permute-start(bf16[64,1408]{1,0:T(8,128)(2,1)S(1)} %get-tuple-element.45), channel_id=1, source_target_pairs={{0,12},{4,8},{8,4},{12,0},{1,13},{5,9},{9,5},{13,1},{2,14},{6,10},... | collective-permute-start | bytes 540680 | tf_op jit(solution)/shard_map/ppermute | solution.py:215
  35.2 3.4 %all-to-all-start.1 = ((bf16[8,8,640]{2,1,0:T(8,128)(2,1)}), bf16[8,8,640]{2,1,0:T(8,128)(2,1)S(1)}, u32[]{:S(2)}, u32[]{:S(2)}) async-start(bf16[8,8,640]{2,1,0:T(8,128)(2,1)} %bitcast.11), calls=%async_computation.1 | async-start | bytes 163840 | tf_op jit(solution)/shard_map/all_to_all | solution.py:222
  38.6 0.6 %collective-permute-done.9.refs_1_ = bf16[64,1408]{1,0:T(8,128)(2,1)S(1)} collective-permute-done((bf16[64,1408]{1,0:T(8,128)(2,1)S(1)}, bf16[64,1408]{1,0:T(8,128)(2,1)S(1)}, u32[]{:S(2)}, u32[]{:S(2)}) %collective-permute-start.9) | collective-permute-done | bytes 180256 | tf_op jit(solution)/shard_map/ppermute | solution.py:215
  39.2 0.0 collective-permute-done.10.refs_2_
  39.2 2.5 %collective-permute-done.11.refs_3_ = bf16[64,1408]{1,0:T(8,128)(2,1)S(1)} collective-permute-done((bf16[64,1408]{1,0:T(8,128)(2,1)S(1)}, bf16[64,1408]{1,0:T(8,128)(2,1)S(1)}, u32[]{:S(2)}, u32[]{:S(2)}) %collective-permute-start.11) | collective-permute-done | bytes 180256 | tf_op jit(solution)/shard_map/ppermute | solution.py:215
  41.7 1.2 %shard_map.115 = (f32[128,384]{1,0:T(8,128)}, f32[128,384]{1,0:T(8,128)}, f32[128,384]{1,0:T(8,128)}) custom-call(bf16[64,1408]{1,0:T(8,128)(2,1)S(1)} %get-tuple-element.42.refs_0_, bf16[64,1408]{1,0:T(8,128)(2,1)S(1)} %collective-permute-done.9.refs_1_, bf16[64,1408]{1,0:T(8,128)(2,1)S(1)} %collective-permute-done.10.refs_2_, ...), custom_call_target="tpu_custom_call" | custom-call | tf_op jit(solution)/shard_map/pallas_call | solution.py:26
  42.9 1.4 %all-to-all-done.1 = bf16[8,8,640]{2,1,0:T(8,128)(2,1)S(1)} async-done(((bf16[8,8,640]{2,1,0:T(8,128)(2,1)}), bf16[8,8,640]{2,1,0:T(8,128)(2,1)S(1)}, u32[]{:S(2)}, u32[]{:S(2)}) %all-to-all-start.1) | async-done | bytes 81952 | tf_op jit(solution)/shard_map/all_to_all | solution.py:222
  44.3 1.0 %shard_map.116 = (bf16[128,1024]{1,0:T(8,128)(2,1)}, bf16[8,128]{1,0:T(8,128)(2,1)}) custom-call(s32[8,128]{1,0:T(8,128)S(1)} %get-tuple-element.28.ids_ref, bf16[8,128]{1,0:T(8,128)(2,1)S(1)} %get-tuple-element.29.scales_ref, bf16[32,128]{1,0:T(8,128)(2,1)S(1)} %get-tuple-element.30.hits_ref, bf16[64,640]{1,0:T(8,128)(2,1)S(1)} %bitcast.24, ...), custom_call_target="tpu_custom_call" | custom-call | tf_op jit(solution)/shard_map/pallas_call | solution.py:26
Async XLA Ops:
  1.7 16.6 %collective-permute-start.3 = (bf16[128,768]{1,0:T(8,128)(2,1)S(1)}, bf16[128,768]{1,0:T(8,128)(2,1)S(1)}, u32[]{:S(2)}, u32[]{:S(2)}) collective-permute-start(bf16[128,768]{1,0:T(8,128)(2,1)S(1)} %get-tuple-element.33.refs_0_), channel_id=1, source_target_pairs={{0,12},{4,8},{8,4},{12,0},{1,13},{5,9},{9,5},{13,1},{2,14},{6,10},... | collective-permute-start | bytes 589832 | tf_op jit(solution)/shard_map/ppermute | solution.py:215
  5.7 13.1 %collective-permute-start.2 = (bf16[128,768]{1,0:T(8,128)(2,1)S(1)}, bf16[128,768]{1,0:T(8,128)(2,1)S(1)}, u32[]{:S(2)}, u32[]{:S(2)}) collective-permute-start(bf16[128,768]{1,0:T(8,128)(2,1)S(1)} %get-tuple-element.33.refs_0_), channel_id=1, source_target_pairs={{0,8},{4,12},{8,0},{12,4},{1,9},{5,13},{9,1},{13,5},{2,10},{6,14},... | collective-permute-start | bytes 589832 | tf_op jit(solution)/shard_map/ppermute | solution.py:215
  6.2 12.7 %collective-permute-start.1 = (bf16[128,768]{1,0:T(8,128)(2,1)S(1)}, bf16[128,768]{1,0:T(8,128)(2,1)S(1)}, u32[]{:S(2)}, u32[]{:S(2)}) collective-permute-start(bf16[128,768]{1,0:T(8,128)(2,1)S(1)} %get-tuple-element.33.refs_0_), channel_id=1, source_target_pairs={{0,4},{4,0},{8,12},{12,8},{1,5},{5,1},{9,13},{13,9},{2,6},{6,2},{1... | collective-permute-start | bytes 589832 | tf_op jit(solution)/shard_map/ppermute | solution.py:215
  6.4 10.7 %collective-permute-start = (bf16[32,512]{1,0:T(8,128)(2,1)S(1)}, bf16[32,512]{1,0:T(8,128)(2,1)S(1)}, u32[]{:S(2)}, u32[]{:S(2)}) collective-permute-start(bf16[32,512]{1,0:T(8,128)(2,1)S(1)} %get-tuple-element.32), channel_id=1, source_target_pairs={{0,16},{16,0},{1,17},{17,1},{2,18},{18,2},{3,19},{19,3},{4,20},{20... | collective-permute-start | bytes 98312 | tf_op jit(solution)/shard_map/ppermute | solution.py:218
  11.1 14.2 %all-to-all-start = ((bf16[8,8,512]{2,1,0:T(8,128)(2,1)}), bf16[8,8,512]{2,1,0:T(8,128)(2,1)S(1)}, u32[]{:S(2)}, u32[]{:S(2)}) async-start(bf16[8,8,512]{2,1,0:T(8,128)(2,1)} %bitcast.9), calls=%async_computation | async-start | bytes 131072 | tf_op jit(solution)/shard_map/all_to_all | solution.py:222
  14.5 7.3 %collective-permute-start.7 = (bf16[128,384]{1,0:T(8,128)(2,1)S(1)}, bf16[128,384]{1,0:T(8,128)(2,1)S(1)}, u32[]{:S(2)}, u32[]{:S(2)}) collective-permute-start(bf16[128,384]{1,0:T(8,128)(2,1)S(1)} %get-tuple-element.37.refs_0_), channel_id=1, source_target_pairs={{0,12},{4,8},{8,4},{12,0},{1,13},{5,9},{9,5},{13,1},{2,14},{6,10},... | collective-permute-start | bytes 294920 | tf_op jit(solution)/shard_map/ppermute | solution.py:215
  17.1 8.3 %collective-permute-start.6 = (bf16[128,384]{1,0:T(8,128)(2,1)S(1)}, bf16[128,384]{1,0:T(8,128)(2,1)S(1)}, u32[]{:S(2)}, u32[]{:S(2)}) collective-permute-start(bf16[128,384]{1,0:T(8,128)(2,1)S(1)} %get-tuple-element.37.refs_0_), channel_id=1, source_target_pairs={{0,8},{4,12},{8,0},{12,4},{1,9},{5,13},{9,1},{13,5},{2,10},{6,14},... | collective-permute-start | bytes 294920 | tf_op jit(solution)/shard_map/ppermute | solution.py:215
  18.3 7.0 %collective-permute-start.5 = (bf16[128,384]{1,0:T(8,128)(2,1)S(1)}, bf16[128,384]{1,0:T(8,128)(2,1)S(1)}, u32[]{:S(2)}, u32[]{:S(2)}) collective-permute-start(bf16[128,384]{1,0:T(8,128)(2,1)S(1)} %get-tuple-element.37.refs_0_), channel_id=1, source_target_pairs={{0,4},{4,0},{8,12},{12,8},{1,5},{5,1},{9,13},{13,9},{2,6},{6,2},{1... | collective-permute-start | bytes 294920 | tf_op jit(solution)/shard_map/ppermute | solution.py:215
  19.1 11.5 %collective-permute-start.4 = (bf16[64,768]{1,0:T(8,128)(2,1)S(1)}, bf16[64,768]{1,0:T(8,128)(2,1)S(1)}, u32[]{:S(2)}, u32[]{:S(2)}) collective-permute-start(bf16[64,768]{1,0:T(8,128)(2,1)S(1)} %get-tuple-element.35), channel_id=1, source_target_pairs={{0,16},{16,0},{1,17},{17,1},{2,18},{18,2},{3,19},{19,3},{4,20},{20... | collective-permute-start | bytes 294920 | tf_op jit(solution)/shard_map/ppermute | solution.py:218
  25.6 5.1 %collective-permute-start.8 = (bf16[64,384]{1,0:T(8,128)(2,1)S(1)}, bf16[64,384]{1,0:T(8,128)(2,1)S(1)}, u32[]{:S(2)}, u32[]{:S(2)}) collective-permute-start(bf16[64,384]{1,0:T(8,128)(2,1)S(1)} %get-tuple-element.39), channel_id=1, source_target_pairs={{0,16},{16,0},{1,17},{17,1},{2,18},{18,2},{3,19},{19,3},{4,20},{20... | collective-permute-start | bytes 147464 | tf_op jit(solution)/shard_map/ppermute | solution.py:218
  31.7 7.4 %collective-permute-start.9 = (bf16[64,1408]{1,0:T(8,128)(2,1)S(1)}, bf16[64,1408]{1,0:T(8,128)(2,1)S(1)}, u32[]{:S(2)}, u32[]{:S(2)}) collective-permute-start(bf16[64,1408]{1,0:T(8,128)(2,1)S(1)} %get-tuple-element.43), channel_id=1, source_target_pairs={{0,4},{4,0},{8,12},{12,8},{1,5},{5,1},{9,13},{13,9},{2,6},{6,2},{1... | collective-permute-start | bytes 540680 | tf_op jit(solution)/shard_map/ppermute | solution.py:215
  31.9 7.3 %collective-permute-start.10 = (bf16[64,1408]{1,0:T(8,128)(2,1)S(1)}, bf16[64,1408]{1,0:T(8,128)(2,1)S(1)}, u32[]{:S(2)}, u32[]{:S(2)}) collective-permute-start(bf16[64,1408]{1,0:T(8,128)(2,1)S(1)} %get-tuple-element.44), channel_id=1, source_target_pairs={{0,8},{4,12},{8,0},{12,4},{1,9},{5,13},{9,1},{13,5},{2,10},{6,14},... | collective-permute-start | bytes 540680 | tf_op jit(solution)/shard_map/ppermute | solution.py:215
  32.2 9.5 %collective-permute-start.11 = (bf16[64,1408]{1,0:T(8,128)(2,1)S(1)}, bf16[64,1408]{1,0:T(8,128)(2,1)S(1)}, u32[]{:S(2)}, u32[]{:S(2)}) collective-permute-start(bf16[64,1408]{1,0:T(8,128)(2,1)S(1)} %get-tuple-element.45), channel_id=1, source_target_pairs={{0,12},{4,8},{8,4},{12,0},{1,13},{5,9},{9,5},{13,1},{2,14},{6,10},... | collective-permute-start | bytes 540680 | tf_op jit(solution)/shard_map/ppermute | solution.py:215
  35.2 9.1 %all-to-all-start.1 = ((bf16[8,8,640]{2,1,0:T(8,128)(2,1)}), bf16[8,8,640]{2,1,0:T(8,128)(2,1)S(1)}, u32[]{:S(2)}, u32[]{:S(2)}) async-start(bf16[8,8,640]{2,1,0:T(8,128)(2,1)} %bitcast.11), calls=%async_computation.1 | async-start | bytes 163840 | tf_op jit(solution)/shard_map/all_to_all | solution.py:222

commit v3 on v2

--- a/solution.py
+++ b/solution.py
@@ -12,6 +12,7 @@
 CAP = 8
 LANES = 128
 F32 = jnp.float32
+RETURN_COST = pl.CostEstimate(flops=3 * 10**9, transcendentals=0, bytes_accessed=9 * 10**6)
 BF16 = jnp.bfloat16
 
 
@@ -21,18 +22,17 @@
     )
 
 
-def call(kernel, *args, out, scratch=(), space=pltpu.VMEM, after=(), cost=None):
+def call(kernel, *args, out, scratch=(), space=pltpu.VMEM, cost=None):
     spec = pl.BlockSpec(memory_space=pltpu.VMEM)
     return pl.pallas_call(
         kernel,
         out_shape=[jax.ShapeDtypeStruct(s, d) for s, d in out],
-        in_specs=[pl.BlockSpec(memory_space=space)] * len(args)
-        + [pl.BlockSpec(memory_space=pl.ANY)] * len(after),
+        in_specs=[pl.BlockSpec(memory_space=space)] * len(args),
         out_specs=[spec] * len(out),
         scratch_shapes=list(scratch),
         cost_estimate=cost,
         compiler_params=pltpu.CompilerParams(vmem_limit_bytes=32 << 20),
-    )(*args, *after)
+    )(*args)
 
 
 def in_hbm(*arrays):
@@ -57,13 +57,15 @@
     return pl.ds(pl.multiple_of(index * size, size), size)
 
 
-def spread_kernel(gate_ref, up_ref, down_ref, saved_ref, both_ref, last_ref, *rest):
+def spread_kernel(gate_ref, up_ref, down_ref, saved_ref, whole_ref, both_ref, last_ref, *rest):
     mine_ref, across_ref, saved, sems = rest
     hidden = gate_ref.shape[1]
     half = mine_ref.shape[1]
     q, _ = position()
     targets = (both_ref.at[:, :hidden], both_ref.at[:, hidden:], last_ref)
-    copies = fetch((saved_ref, gate_ref, up_ref, down_ref), (saved, *targets), sems)
+    sources = (gate_ref, up_ref, down_ref)
+    again = [whole_ref.at[:, i * hidden : (i + 1) * hidden] for i in range(3)]
+    copies = fetch((saved_ref, *sources, *sources), (saved, *targets, *again), sems)
     copies[0].wait()
     mine_ref[...] = saved[:, block(q, half)]
     across_ref[...] = saved[:, block(1 - q, half)]
@@ -99,7 +101,7 @@
         here = (place[j : j + 1] == slot) & (hits[j] > 0.0)
         chosen.append(jnp.where(here, 1.0, 0.0))
         scaled.append(jnp.where(here, scales[j], 0.0))
-    hits_ref[...] = jnp.concatenate(chosen, axis=0).astype(BF16)
+    hits_ref[...] = jnp.concatenate(chosen, axis=0)
     picks = jnp.concatenate(scaled, axis=0).astype(BF16)
     copies[2].wait()
     rows = dot(picks, grads_ref[...], 1, 0).astype(BF16)
@@ -116,7 +118,8 @@
     pair_ref[block(1 - q, slots), :] = theirs_ref[...]
     total = None
     for k in range(PARTS):
-        term = dot(pair_ref[:, block(p ^ k, width)], weights[k][...], 1, 0)
+        columns = weights[k][:, : own_ref.shape[1]]
+        term = dot(pair_ref[:, block(p ^ k, width)], columns, 1, 0)
         total = term if total is None else total + term
     own_ref[...] = total
     sent_ref[...] = total.astype(BF16)
@@ -128,15 +131,17 @@
     width = weights[0].shape[0]
     total = None
     for k in range(PARTS):
-        term = dot(routed_ref[:, block(p ^ k, width)], weights[k][...], 1, 0)
+        columns = weights[k][:, weights[k].shape[1] - own_ref.shape[1] :]
+        term = dot(routed_ref[:, block(p ^ k, width)], columns, 1, 0)
         total = term if total is None else total + term
     own_ref[...] = total
     sent_ref[...] = total.astype(BF16)
 
 
 def delta_kernel(gate_up_ref, other_ref, down_ref, down_other_ref, pair_ref, routed_ref, *refs):
-    weights, back_ref, sends = refs[:PARTS], refs[PARTS], refs[PARTS + 1 :]
-    _, p = position()
+    weights, kept_ref, swap_ref, sends = refs[:PARTS], refs[PARTS], refs[PARTS + 1], refs[PARTS + 2 : -1]
+    back_ref = refs[-1]
+    q, p = position()
     width = weights[0].shape[0]
     hidden_width = down_ref.shape[1]
     half = pair_ref.shape[1]
@@ -162,6 +167,20 @@
         sends[k][:, 2 * hidden_width : 3 * hidden_width] = hidden
         sends[k][:, 3 * hidden_width : 3 * hidden_width + width] = pair_ref[:, lanes]
         sends[k][:, 3 * hidden_width + width :] = routed_ref[:, lanes]
+    slots = kept_ref.shape[0]
+    kept_ref[...] = back_ref[block(q, slots), :]
+    swap_ref[...] = back_ref[block(1 - q, slots), :]
+
+
+def return_kernel(kept_ref, swap_ref, *refs):
+    outs, rows_ref = refs[:-1], refs[-1]
+    q, _ = position()
+    half = kept_ref.shape[1] - LANES
+    rows_ref[:, block(q, half)] = kept_ref[:, :half].astype(F32)
+    rows_ref[:, block(1 - q, half)] = swap_ref[:, :half].astype(F32)
+    rows_ref[:, 2 * half :] = kept_ref[:, half:].astype(F32)
+    for m, out in enumerate(outs):
+        out[...] = rows_ref[block(lax.axis_index("exp") ^ m, CAP), :].astype(BF16)
 
 
 def grads_step(replicas):
@@ -186,21 +205,21 @@
     return grads_kernel
 
 
-def tokens_kernel(ids_ref, scales_ref, hits_ref, rows_ref, _, input_grad_ref, route_ref):
-    slots = hits_ref.shape[0]
-    half = input_grad_ref.shape[1] // 2
-    hits = hits_ref[...]
-    for h in range(2):
-        input_grad_ref[:, h * half : (h + 1) * half] = dot(
-            hits, rows_ref[h * slots : (h + 1) * slots, :half], 0, 0
-        ).astype(BF16)
-    spread = hits.astype(F32) * rows_ref[0:slots, half:].astype(F32)
+def tokens_kernel(ids_ref, scales_ref, hits_ref, *refs):
+    pieces, (input_grad_ref, route_ref) = refs[:-2], refs[-2:]
+    features = input_grad_ref.shape[1]
     ids = ids_ref[...]
     out = jnp.zeros(ids.shape, F32)
-    for j in range(slots // CAP):
-        value = jnp.sum(spread[j * CAP : (j + 1) * CAP], axis=0, keepdims=True)
-        out = jnp.where(ids == j * EXP_DEV, value, out)
+    hits = []
+    for m, piece in enumerate(pieces):
+        expert = lax.axis_index("exp") ^ m
+        hits.append(hits_ref[block(expert, CAP), :])
+        value = jnp.sum(hits[m] * piece[:, features:].astype(F32), axis=0, keepdims=True)
+        out = jnp.where(ids == expert * EXP_DEV, value, out)
     route_ref[...] = (out / scales_ref[...].astype(F32)).astype(BF16)
+    rows = jnp.concatenate([piece[:, :features].astype(F32) for piece in pieces], axis=0)
+    hits = jnp.concatenate(hits, axis=0)
+    input_grad_ref[...] = dot(hits.astype(BF16), rows.astype(BF16), 0, 0).astype(BF16)
 
 
 def body(expert_ids, route_weights, out_grad, saved_inputs, gate_weight, up_weight, down_weight):
@@ -221,23 +240,24 @@
         blocks = value.reshape(2 * owners, CAP, value.shape[1])
         return lax.all_to_all(blocks, ("q", "exp"), 0, 0, tiled=True).reshape(value.shape)
 
-    both, last, mine, across = call(
+    whole, both, last, mine, across = call(
         spread_kernel,
         *in_hbm(gate_weight[0], up_weight[0], down_weight[0], saved_inputs[0, 0]),
-        out=[((width, 2 * hidden_width), BF16), ((width, hidden_width), BF16)]
+        out=[((width, n * hidden_width), BF16) for n in (3, 2, 1)]
         + [((slots, half), BF16)] * 2,
-        scratch=[pltpu.VMEM((slots, features), BF16), pltpu.SemaphoreType.DMA((4,))],
+        scratch=[pltpu.VMEM((slots, features), BF16), pltpu.SemaphoreType.DMA((7,))],
         space=pltpu.HBM,
     )
     theirs = across_halves(across)
-    both = [both] + [in_half(both, k) for k in range(1, PARTS)]
-    last = [last] + [in_half(last, k) for k in range(1, PARTS)]
+    whole = in_half(whole, PARTS - 1)
+    both = [both] + [in_half(both, k) for k in range(1, PARTS - 1)] + [whole]
+    last = [last] + [in_half(last, k) for k in range(1, PARTS - 1)] + [whole]
     sent, hits, ids, scales = call(
         route_kernel,
         *in_hbm(expert_ids[0].T, route_weights[0].T, out_grad[0]),
         out=[
             ((rows, half), BF16),
-            ((slots, tokens), BF16),
+            ((slots, tokens), F32),
             ((TOPK, tokens), jnp.int32),
             ((TOPK, tokens), BF16),
         ],
@@ -263,7 +283,7 @@
         *last,
         out=[((rows, hidden_width), F32), ((rows, hidden_width), BF16)],
     )
-    back, *sends = call(
+    kept, swapped, *sends = call(
         delta_kernel,
         gate_up,
         other,
@@ -272,10 +292,22 @@
         pair,
         routed,
         *both,
-        out=[((rows, half + LANES), BF16)]
+        out=[((slots, half + LANES), BF16)] * 2
         + [((rows, 3 * hidden_width + 2 * width), BF16)] * PARTS,
-    )
-    returned = exchange(back)
+        scratch=[pltpu.VMEM((rows, half + LANES), BF16)],
+    )
+    pieces = call(
+        return_kernel,
+        kept,
+        across_halves(swapped),
+        cost=RETURN_COST,
+        out=[((CAP, features + LANES), BF16)] * owners,
+        scratch=[pltpu.VMEM((slots, features + LANES), F32)],
+    )
+    pieces = [pieces[0]] + [
+        lax.ppermute(pieces[m], "exp", [(i, i ^ m) for i in range(owners)])
+        for m in range(1, owners)
+    ]
     sends = [sends[0]] + [in_half(sends[k], k) for k in range(1, PARTS)]
     gate_grad, up_grad, down_grad = call(
         grads_step(replicas), *sends, out=[((width, hidden_width), F32)] * 3
@@ -285,8 +317,7 @@
         ids,
         scales,
         hits,
-        returned,
-        after=in_hbm(gate_grad),
+        *pieces,
         out=[((tokens, features), BF16), ((TOPK, tokens), BF16)],
     )
     return (input_grad[None], route_grad.T[None], gate_grad[None], up_grad[None], down_grad[None])

time: 45.6 us -> 43 us (0.943)
  waiting for transfers between devices: 13 us -> 7.65 us
  starting transfers between devices: 24.9 us -> 28.2 us
    ppermute x3 -> x4, starting transfers between devices: 5.72 us -> 12.6 us  [across_halves(): return lax.ppermute(value, 'q', [(0, 1), (1, 0)])]
    ppermute x9 -> x8, waiting for transfers between devices: 7.27 us -> 1.45 us  [in_half(): return lax.ppermute(value, 'p', [(i, i ^ mask) for i in range(PARTS)])]
    all_to_all x2 -> x1, starting transfers between devices: 6.72 us -> 3.36 us  [exchange(): lax.all_to_all(blocks, ('q', 'exp'), 0, 0, tiled=True).reshape(value.shape)]
    ppermute x9 -> x8, starting transfers between devices: 12.5 us -> 9.79 us  [in_half(): return lax.ppermute(value, 'p', [(i, i ^ mask) for i in range(PARTS)])]
    ppermute x0 -> x3, starting transfers between devices: none -> 2.38 us  [body(): lax.ppermute(pieces[m], 'exp', [(i, i ^ m) for i in range(owners)])]
    ppermute x0 -> x3, waiting for transfers between devices: none -> 2.31 us  [body(): lax.ppermute(pieces[m], 'exp', [(i, i ^ m) for i in range(owners)])]
    all_to_all x2 -> x1, waiting for transfers between devices: 1.39 us -> 0.01 us  [exchange(): lax.all_to_all(blocks, ('q', 'exp'), 0, 0, tiled=True).reshape(value.shape)]
    ppermute x3 -> x4, waiting for transfers between devices: 4.33 us -> 3.88 us  [across_halves(): return lax.ppermute(value, 'q', [(0, 1), (1, 0)])]
  transfers between devices with their start and end apart: 14 -> 16, of which waited for: 6 -> 7; matrix products, arithmetic and copies ran while one was open for 0% -> 0% of each run, Pallas kernels for 8% -> 8%
where the time goes in v3:
time: 43 us; the launch traced here: 42.7 us
  starting transfers between devices  28.2 us (66%)
  waiting for transfers between devices  7.65 us (18%)
  Pallas kernels  6.23 us (14%)
  between operations  0.71 us (2%)
    ppermute x4, starting transfers between devices, across_halves(): return lax.ppermute(value, 'q', [(0, 1), (1, 0)])  12.6 us
    ppermute x8, starting transfers between devices, in_half(): return lax.ppermute(value, 'p', [(i, i ^ mask) for i in range(PARTS)])  9.79 us
    pallas_call x8, Pallas kernels, call(): pl.pallas_call(kernel, out_shape=[jax.ShapeDtypeStruct(s, d) for s, d in...  6.23 us
    ppermute x4, waiting for transfers between devices, across_halves(): return lax.ppermute(value, 'q', [(0, 1), (1, 0)])  3.88 us
    all_to_all x1, starting transfers between devices, exchange(): lax.all_to_all(blocks, ('q', 'exp'), 0, 0, tiled=True).reshape(value.shape)  3.36 us
    ppermute x3, starting transfers between devices, body(): lax.ppermute(pieces[m], 'exp', [(i, i ^ m) for i in range(owners)])  2.38 us
    ppermute x3, waiting for transfers between devices, body(): lax.ppermute(pieces[m], 'exp', [(i, i ^ m) for i in range(owners)])  2.31 us
    ppermute x8, waiting for transfers between devices, in_half(): return lax.ppermute(value, 'p', [(i, i ^ mask) for i in range(PARTS)])  1.45 us
  transfers between devices with their start and end apart: 16, of which 7 were waited for; matrix products, arithmetic and copies ran while one was open for 0% of the time, Pallas kernels for 8%

profile of v3, /device:TPU:0, one launch (start us, length us, event | category | flops | bytes accessed | tf_op | source)
XLA Modules:
  0.0 42.7 jit_solution(12021633001064970636)
XLA Ops:
  0.6 1.2 %shard_map.111 = (bf16[128,1152]{1,0:T(8,128)(2,1)S(1)}, bf16[128,768]{1,0:T(8,128)(2,1)S(1)}, bf16[128,384]{1,0:T(8,128)(2,1)S(1)}, bf16[32,512]{1,0:T(8,128)(2,1)S(1)}, bf16[32,512]{1,0:T(8,128)(2,1)S(1)}) custom-call(bf16[128,384]{1,0:T(8,128)(2,1)} %bitcast.23, bf16[128,384]{1,0:T(8,128)(2,1)} %bitcast.24, bf16[128,384]{1,0:T(8,128)(2,1)} %bitcast.25, ...), custom_call_target="tpu_custom_call" | custom-call | tf_op jit(solution)/shard_map/pallas_call | solution.py:27
  1.9 4.0 %collective-permute-start.3 = (bf16[128,1152]{1,0:T(8,128)(2,1)S(1)}, bf16[128,1152]{1,0:T(8,128)(2,1)S(1)}, u32[]{:S(2)}, u32[]{:S(2)}) collective-permute-start(bf16[128,1152]{1,0:T(8,128)(2,1)S(1)} %get-tuple-element.40), channel_id=1, source_target_pairs={{0,12},{4,8},{8,4},{12,0},{1,13},{5,9},{9,5},{13,1},{2,14},{6,10},... | collective-permute-start | bytes 884744 | tf_op jit(solution)/shard_map/ppermute | solution.py:234
  5.9 0.4 %collective-permute-start.2 = (bf16[128,768]{1,0:T(8,128)(2,1)S(1)}, bf16[128,768]{1,0:T(8,128)(2,1)S(1)}, u32[]{:S(2)}, u32[]{:S(2)}) collective-permute-start(bf16[128,768]{1,0:T(8,128)(2,1)S(1)} %get-tuple-element.39.refs_0_), channel_id=1, source_target_pairs={{0,8},{4,12},{8,0},{12,4},{1,9},{5,13},{9,1},{13,5},{2,10},{6,14},... | collective-permute-start | bytes 589832 | tf_op jit(solution)/shard_map/ppermute | solution.py:234
  6.3 0.2 collective-permute-start.1
  6.5 2.9 %collective-permute-start = (bf16[32,512]{1,0:T(8,128)(2,1)S(1)}, bf16[32,512]{1,0:T(8,128)(2,1)S(1)}, u32[]{:S(2)}, u32[]{:S(2)}) collective-permute-start(bf16[32,512]{1,0:T(8,128)(2,1)S(1)} %get-tuple-element.38), channel_id=1, source_target_pairs={{0,16},{16,0},{1,17},{17,1},{2,18},{18,2},{3,19},{19,3},{4,20},{20... | collective-permute-start | bytes 98312 | tf_op jit(solution)/shard_map/ppermute | solution.py:237
  9.5 1.8 %shard_map.110 = (bf16[64,512]{1,0:T(8,128)(2,1)}, f32[32,128]{1,0:T(8,128)S(1)}, s32[8,128]{1,0:T(8,128)S(1)}, bf16[8,128]{1,0:T(8,128)(2,1)S(1)}) custom-call(s32[8,128]{1,0:T(8,128)} %bitcast.27, bf16[8,128]{1,0:T(8,128)(2,1)} %bitcast.28, bf16[128,1024]{1,0:T(8,128)(2,1)} %bitcast.22), custom_call_target="tpu_custom_call" | custom-call | tf_op jit(solution)/shard_map/pallas_call | solution.py:27
  11.3 3.4 %all-to-all-start = ((bf16[8,8,512]{2,1,0:T(8,128)(2,1)}), bf16[8,8,512]{2,1,0:T(8,128)(2,1)S(1)}, u32[]{:S(2)}, u32[]{:S(2)}) async-start(bf16[8,8,512]{2,1,0:T(8,128)(2,1)} %bitcast.9), calls=%async_computation | async-start | bytes 131072 | tf_op jit(solution)/shard_map/all_to_all | solution.py:241
  14.7 1.6 %collective-permute-start.6 = (bf16[128,384]{1,0:T(8,128)(2,1)S(1)}, bf16[128,384]{1,0:T(8,128)(2,1)S(1)}, u32[]{:S(2)}, u32[]{:S(2)}) collective-permute-start(bf16[128,384]{1,0:T(8,128)(2,1)S(1)} %get-tuple-element.44.refs_0_), channel_id=1, source_target_pairs={{0,8},{4,12},{8,0},{12,4},{1,9},{5,13},{9,1},{13,5},{2,10},{6,14},... | collective-permute-start | bytes 294920 | tf_op jit(solution)/shard_map/ppermute | solution.py:234
  16.3 1.8 %collective-permute-done.theirs_ref = bf16[32,512]{1,0:T(8,128)(2,1)S(1)} collective-permute-done((bf16[32,512]{1,0:T(8,128)(2,1)S(1)}, bf16[32,512]{1,0:T(8,128)(2,1)S(1)}, u32[]{:S(2)}, u32[]{:S(2)}) %collective-permute-start) | collective-permute-done | bytes 32800 | tf_op jit(solution)/shard_map/ppermute | solution.py:237
  18.1 0.0 collective-permute-start.5
  18.1 0.2 collective-permute-done.2.refs_2_
  18.3 0.0 collective-permute-done.1.refs_1_
  18.3 0.0 collective-permute-done.3.refs_3_
  18.3 0.3 shard_map.112
  18.6 3.3 %collective-permute-start.4 = (bf16[64,768]{1,0:T(8,128)(2,1)S(1)}, bf16[64,768]{1,0:T(8,128)(2,1)S(1)}, u32[]{:S(2)}, u32[]{:S(2)}) collective-permute-start(bf16[64,768]{1,0:T(8,128)(2,1)S(1)} %get-tuple-element.42), channel_id=1, source_target_pairs={{0,16},{16,0},{1,17},{17,1},{2,18},{18,2},{3,19},{19,3},{4,20},{20... | collective-permute-start | bytes 294920 | tf_op jit(solution)/shard_map/ppermute | solution.py:237
  21.8 0.0 collective-permute-done.6.refs_2_
  21.8 0.9 %collective-permute-done.5.refs_1_ = bf16[128,384]{1,0:T(8,128)(2,1)S(1)} collective-permute-done((bf16[128,384]{1,0:T(8,128)(2,1)S(1)}, bf16[128,384]{1,0:T(8,128)(2,1)S(1)}, u32[]{:S(2)}, u32[]{:S(2)}) %collective-permute-start.5) | collective-permute-done | bytes 98336 | tf_op jit(solution)/shard_map/ppermute | solution.py:234
  22.7 0.0 all-to-all-done
  22.7 0.2 shard_map.113
  22.9 3.4 %collective-permute-start.7 = (bf16[64,384]{1,0:T(8,128)(2,1)S(1)}, bf16[64,384]{1,0:T(8,128)(2,1)S(1)}, u32[]{:S(2)}, u32[]{:S(2)}) collective-permute-start(bf16[64,384]{1,0:T(8,128)(2,1)S(1)} %get-tuple-element.46), channel_id=1, source_target_pairs={{0,16},{16,0},{1,17},{17,1},{2,18},{18,2},{3,19},{19,3},{4,20},{20... | collective-permute-start | bytes 147464 | tf_op jit(solution)/shard_map/ppermute | solution.py:237
  26.4 2.1 %collective-permute-done.7.down_other_ref = bf16[64,384]{1,0:T(8,128)(2,1)S(1)} collective-permute-done((bf16[64,384]{1,0:T(8,128)(2,1)S(1)}, bf16[64,384]{1,0:T(8,128)(2,1)S(1)}, u32[]{:S(2)}, u32[]{:S(2)}) %collective-permute-start.7) | collective-permute-done | bytes 49184 | tf_op jit(solution)/shard_map/ppermute | solution.py:237
  28.5 0.0 collective-permute-done.4.other_ref
  28.5 0.5 %shard_map.114 = (bf16[32,640]{1,0:T(8,128)(2,1)S(1)}, bf16[32,640]{1,0:T(8,128)(2,1)S(1)}, bf16[64,1408]{1,0:T(8,128)(2,1)S(1)}, bf16[64,1408]{1,0:T(8,128)(2,1...) custom-call(f32[64,768]{1,0:T(8,128)S(1)} %get-tuple-element.41.gate_up_ref, ...), custom_call_target="tpu_custom_call" | custom-call | tf_op jit(solution)/shard_map/pallas_call | solution.py:27
  29.0 3.0 %collective-permute-start.8 = (bf16[32,640]{1,0:T(8,128)(2,1)S(1)}, bf16[32,640]{1,0:T(8,128)(2,1)S(1)}, u32[]{:S(2)}, u32[]{:S(2)}) collective-permute-start(bf16[32,640]{1,0:T(8,128)(2,1)S(1)} %get-tuple-element.49), channel_id=1, source_target_pairs={{0,16},{16,0},{1,17},{17,1},{2,18},{18,2},{3,19},{19,3},{4,20},{20... | collective-permute-start | bytes 122888 | tf_op jit(solution)/shard_map/ppermute | solution.py:237
  31.9 0.1 collective-permute-start.12
  32.0 1.5 %collective-permute-start.13 = (bf16[64,1408]{1,0:T(8,128)(2,1)S(1)}, bf16[64,1408]{1,0:T(8,128)(2,1)S(1)}, u32[]{:S(2)}, u32[]{:S(2)}) collective-permute-start(bf16[64,1408]{1,0:T(8,128)(2,1)S(1)} %get-tuple-element.58), channel_id=1, source_target_pairs={{0,8},{4,12},{8,0},{12,4},{1,9},{5,13},{9,1},{13,5},{2,10},{6,14},... | collective-permute-start | bytes 540680 | tf_op jit(solution)/shard_map/ppermute | solution.py:234
  33.5 1.9 %collective-permute-start.14 = (bf16[64,1408]{1,0:T(8,128)(2,1)S(1)}, bf16[64,1408]{1,0:T(8,128)(2,1)S(1)}, u32[]{:S(2)}, u32[]{:S(2)}) collective-permute-start(bf16[64,1408]{1,0:T(8,128)(2,1)S(1)} %get-tuple-element.59), channel_id=1, source_target_pairs={{0,12},{4,8},{8,4},{12,0},{1,13},{5,9},{9,5},{13,1},{2,14},{6,10},... | collective-permute-start | bytes 540680 | tf_op jit(solution)/shard_map/ppermute | solution.py:234
  35.4 0.0 collective-permute-done.8.swap_ref
  35.5 0.1 collective-permute-start.9
  35.5 1.4 %collective-permute-start.10 = (bf16[8,1152]{1,0:T(8,128)(2,1)S(1)}, bf16[8,1152]{1,0:T(8,128)(2,1)S(1)}, u32[]{:S(2)}, u32[]{:S(2)}) collective-permute-start(bf16[8,1152]{1,0:T(8,128)(2,1)S(1)} %get-tuple-element.52), channel_id=1, source_target_pairs={{0,2},{1,3},{2,0},{3,1},{4,6},{5,7},{6,4},{7,5},{8,10},{9,11},{10,... | collective-permute-start | bytes 55304 | tf_op jit(solution)/shard_map/ppermute | solution.py:308
  37.0 0.0 collective-permute-done.9.refs_1_
  37.0 0.9 %collective-permute-start.11 = (bf16[8,1152]{1,0:T(8,128)(2,1)S(1)}, bf16[8,1152]{1,0:T(8,128)(2,1)S(1)}, u32[]{:S(2)}, u32[]{:S(2)}) collective-permute-start(bf16[8,1152]{1,0:T(8,128)(2,1)S(1)} %get-tuple-element.53), channel_id=1, source_target_pairs={{0,3},{1,2},{2,1},{3,0},{4,7},{5,6},{6,5},{7,4},{8,11},{9,10},{10,... | collective-permute-start | bytes 55304 | tf_op jit(solution)/shard_map/ppermute | solution.py:308
  37.9 1.5 %collective-permute-done.10.refs_2_ = bf16[8,1152]{1,0:T(8,128)(2,1)S(1)} collective-permute-done((bf16[8,1152]{1,0:T(8,128)(2,1)S(1)}, bf16[8,1152]{1,0:T(8,128)(2,1)S(1)}, u32[]{:S(2)}, u32[]{:S(2)}) %collective-permute-start.10) | collective-permute-done | bytes 18464 | tf_op jit(solution)/shard_map/ppermute | solution.py:308
  39.4 0.8 %collective-permute-done.11.refs_3_ = bf16[8,1152]{1,0:T(8,128)(2,1)S(1)} collective-permute-done((bf16[8,1152]{1,0:T(8,128)(2,1)S(1)}, bf16[8,1152]{1,0:T(8,128)(2,1)S(1)}, u32[]{:S(2)}, u32[]{:S(2)}) %collective-permute-start.11) | collective-permute-done | bytes 18464 | tf_op jit(solution)/shard_map/ppermute | solution.py:308
  40.2 1.0 %shard_map.116 = (bf16[128,1024]{1,0:T(8,128)(2,1)}, bf16[8,128]{1,0:T(8,128)(2,1)}) custom-call(s32[8,128]{1,0:T(8,128)S(1)} %get-tuple-element.34.ids_ref, bf16[8,128]{1,0:T(8,128)(2,1)S(1)} %get-tuple-element.35.scales_ref, f32[32,128]{1,0:T(8,128)S(1)} %get-tuple-element.36.hits_ref, bf16[8,1152]{1,0:T(8,128)(2,1)S(1)} %get-tuple-element.50.refs_0_, ...), custom_call_target="tpu_custom_call" | custom-call | tf_op jit(solution)/shard_map/pallas_call | solution.py:27
  41.1 0.0 collective-permute-done.12.refs_1_
  41.1 0.0 collective-permute-done.13.refs_2_
  41.1 0.4 collective-permute-done.14.refs_3_
  41.5 1.2 %shard_map.117 = (f32[128,384]{1,0:T(8,128)}, f32[128,384]{1,0:T(8,128)}, f32[128,384]{1,0:T(8,128)}) custom-call(bf16[64,1408]{1,0:T(8,128)(2,1)S(1)} %get-tuple-element.56.refs_0_, bf16[64,1408]{1,0:T(8,128)(2,1)S(1)} %collective-permute-done.12.refs_1_, bf16[64,1408]{1,0:T(8,128)(2,1)S(1)} %collective-permute-done.13.refs_2_, ...), custom_call_target="tpu_custom_call" | custom-call | tf_op jit(solution)/shard_map/pallas_call | solution.py:27
  (1 shorter events, 0.0 us)
Async XLA Ops:
  1.9 16.4 %collective-permute-start.3 = (bf16[128,1152]{1,0:T(8,128)(2,1)S(1)}, bf16[128,1152]{1,0:T(8,128)(2,1)S(1)}, u32[]{:S(2)}, u32[]{:S(2)}) collective-permute-start(bf16[128,1152]{1,0:T(8,128)(2,1)S(1)} %get-tuple-element.40), channel_id=1, source_target_pairs={{0,12},{4,8},{8,4},{12,0},{1,13},{5,9},{9,5},{13,1},{2,14},{6,10},... | collective-permute-start | bytes 884744 | tf_op jit(solution)/shard_map/ppermute | solution.py:234
  5.9 12.4 %collective-permute-start.2 = (bf16[128,768]{1,0:T(8,128)(2,1)S(1)}, bf16[128,768]{1,0:T(8,128)(2,1)S(1)}, u32[]{:S(2)}, u32[]{:S(2)}) collective-permute-start(bf16[128,768]{1,0:T(8,128)(2,1)S(1)} %get-tuple-element.39.refs_0_), channel_id=1, source_target_pairs={{0,8},{4,12},{8,0},{12,4},{1,9},{5,13},{9,1},{13,5},{2,10},{6,14},... | collective-permute-start | bytes 589832 | tf_op jit(solution)/shard_map/ppermute | solution.py:234
  6.3 12.0 %collective-permute-start.1 = (bf16[128,768]{1,0:T(8,128)(2,1)S(1)}, bf16[128,768]{1,0:T(8,128)(2,1)S(1)}, u32[]{:S(2)}, u32[]{:S(2)}) collective-permute-start(bf16[128,768]{1,0:T(8,128)(2,1)S(1)} %get-tuple-element.39.refs_0_), channel_id=1, source_target_pairs={{0,4},{4,0},{8,12},{12,8},{1,5},{5,1},{9,13},{13,9},{2,6},{6,2},{1... | collective-permute-start | bytes 589832 | tf_op jit(solution)/shard_map/ppermute | solution.py:234
  6.5 11.6 %collective-permute-start = (bf16[32,512]{1,0:T(8,128)(2,1)S(1)}, bf16[32,512]{1,0:T(8,128)(2,1)S(1)}, u32[]{:S(2)}, u32[]{:S(2)}) collective-permute-start(bf16[32,512]{1,0:T(8,128)(2,1)S(1)} %get-tuple-element.38), channel_id=1, source_target_pairs={{0,16},{16,0},{1,17},{17,1},{2,18},{18,2},{3,19},{19,3},{4,20},{20... | collective-permute-start | bytes 98312 | tf_op jit(solution)/shard_map/ppermute | solution.py:237
  11.3 11.4 %all-to-all-start = ((bf16[8,8,512]{2,1,0:T(8,128)(2,1)}), bf16[8,8,512]{2,1,0:T(8,128)(2,1)S(1)}, u32[]{:S(2)}, u32[]{:S(2)}) async-start(bf16[8,8,512]{2,1,0:T(8,128)(2,1)} %bitcast.9), calls=%async_computation | async-start | bytes 131072 | tf_op jit(solution)/shard_map/all_to_all | solution.py:241
  14.7 7.2 %collective-permute-start.6 = (bf16[128,384]{1,0:T(8,128)(2,1)S(1)}, bf16[128,384]{1,0:T(8,128)(2,1)S(1)}, u32[]{:S(2)}, u32[]{:S(2)}) collective-permute-start(bf16[128,384]{1,0:T(8,128)(2,1)S(1)} %get-tuple-element.44.refs_0_), channel_id=1, source_target_pairs={{0,8},{4,12},{8,0},{12,4},{1,9},{5,13},{9,1},{13,5},{2,10},{6,14},... | collective-permute-start | bytes 294920 | tf_op jit(solution)/shard_map/ppermute | solution.py:234
  18.1 4.6 %collective-permute-start.5 = (bf16[128,384]{1,0:T(8,128)(2,1)S(1)}, bf16[128,384]{1,0:T(8,128)(2,1)S(1)}, u32[]{:S(2)}, u32[]{:S(2)}) collective-permute-start(bf16[128,384]{1,0:T(8,128)(2,1)S(1)} %get-tuple-element.44.refs_0_), channel_id=1, source_target_pairs={{0,4},{4,0},{8,12},{12,8},{1,5},{5,1},{9,13},{13,9},{2,6},{6,2},{1... | collective-permute-start | bytes 294920 | tf_op jit(solution)/shard_map/ppermute | solution.py:234
  18.6 9.9 %collective-permute-start.4 = (bf16[64,768]{1,0:T(8,128)(2,1)S(1)}, bf16[64,768]{1,0:T(8,128)(2,1)S(1)}, u32[]{:S(2)}, u32[]{:S(2)}) collective-permute-start(bf16[64,768]{1,0:T(8,128)(2,1)S(1)} %get-tuple-element.42), channel_id=1, source_target_pairs={{0,16},{16,0},{1,17},{17,1},{2,18},{18,2},{3,19},{19,3},{4,20},{20... | collective-permute-start | bytes 294920 | tf_op jit(solution)/shard_map/ppermute | solution.py:237
  22.9 5.5 %collective-permute-start.7 = (bf16[64,384]{1,0:T(8,128)(2,1)S(1)}, bf16[64,384]{1,0:T(8,128)(2,1)S(1)}, u32[]{:S(2)}, u32[]{:S(2)}) collective-permute-start(bf16[64,384]{1,0:T(8,128)(2,1)S(1)} %get-tuple-element.46), channel_id=1, source_target_pairs={{0,16},{16,0},{1,17},{17,1},{2,18},{18,2},{3,19},{19,3},{4,20},{20... | collective-permute-start | bytes 147464 | tf_op jit(solution)/shard_map/ppermute | solution.py:237
  29.0 6.5 %collective-permute-start.8 = (bf16[32,640]{1,0:T(8,128)(2,1)S(1)}, bf16[32,640]{1,0:T(8,128)(2,1)S(1)}, u32[]{:S(2)}, u32[]{:S(2)}) collective-permute-start(bf16[32,640]{1,0:T(8,128)(2,1)S(1)} %get-tuple-element.49), channel_id=1, source_target_pairs={{0,16},{16,0},{1,17},{17,1},{2,18},{18,2},{3,19},{19,3},{4,20},{20... | collective-permute-start | bytes 122888 | tf_op jit(solution)/shard_map/ppermute | solution.py:237
  31.9 9.2 %collective-permute-start.12 = (bf16[64,1408]{1,0:T(8,128)(2,1)S(1)}, bf16[64,1408]{1,0:T(8,128)(2,1)S(1)}, u32[]{:S(2)}, u32[]{:S(2)}) collective-permute-start(bf16[64,1408]{1,0:T(8,128)(2,1)S(1)} %get-tuple-element.57), channel_id=1, source_target_pairs={{0,4},{4,0},{8,12},{12,8},{1,5},{5,1},{9,13},{13,9},{2,6},{6,2},{1... | collective-permute-start | bytes 540680 | tf_op jit(solution)/shard_map/ppermute | solution.py:234
  32.0 9.1 %collective-permute-start.13 = (bf16[64,1408]{1,0:T(8,128)(2,1)S(1)}, bf16[64,1408]{1,0:T(8,128)(2,1)S(1)}, u32[]{:S(2)}, u32[]{:S(2)}) collective-permute-start(bf16[64,1408]{1,0:T(8,128)(2,1)S(1)} %get-tuple-element.58), channel_id=1, source_target_pairs={{0,8},{4,12},{8,0},{12,4},{1,9},{5,13},{9,1},{13,5},{2,10},{6,14},... | collective-permute-start | bytes 540680 | tf_op jit(solution)/shard_map/ppermute | solution.py:234
  33.5 8.0 %collective-permute-start.14 = (bf16[64,1408]{1,0:T(8,128)(2,1)S(1)}, bf16[64,1408]{1,0:T(8,128)(2,1)S(1)}, u32[]{:S(2)}, u32[]{:S(2)}) collective-permute-start(bf16[64,1408]{1,0:T(8,128)(2,1)S(1)} %get-tuple-element.59), channel_id=1, source_target_pairs={{0,12},{4,8},{8,4},{12,0},{1,13},{5,9},{9,5},{13,1},{2,14},{6,10},... | collective-permute-start | bytes 540680 | tf_op jit(solution)/shard_map/ppermute | solution.py:234
  35.5 1.5 %collective-permute-start.9 = (bf16[8,1152]{1,0:T(8,128)(2,1)S(1)}, bf16[8,1152]{1,0:T(8,128)(2,1)S(1)}, u32[]{:S(2)}, u32[]{:S(2)}) collective-permute-start(bf16[8,1152]{1,0:T(8,128)(2,1)S(1)} %get-tuple-element.51), channel_id=1, source_target_pairs={{0,1},{1,0},{2,3},{3,2},{4,5},{5,4},{6,7},{7,6},{8,9},{9,8},{10,11... | collective-permute-start | bytes 55304 | tf_op jit(solution)/shard_map/ppermute | solution.py:308
  35.5 3.8 %collective-permute-start.10 = (bf16[8,1152]{1,0:T(8,128)(2,1)S(1)}, bf16[8,1152]{1,0:T(8,128)(2,1)S(1)}, u32[]{:S(2)}, u32[]{:S(2)}) collective-permute-start(bf16[8,1152]{1,0:T(8,128)(2,1)S(1)} %get-tuple-element.52), channel_id=1, source_target_pairs={{0,2},{1,3},{2,0},{3,1},{4,6},{5,7},{6,4},{7,5},{8,10},{9,11},{10,... | collective-permute-start | bytes 55304 | tf_op jit(solution)/shard_map/ppermute | solution.py:308
  37.0 3.2 %collective-permute-start.11 = (bf16[8,1152]{1,0:T(8,128)(2,1)S(1)}, bf16[8,1152]{1,0:T(8,128)(2,1)S(1)}, u32[]{:S(2)}, u32[]{:S(2)}) collective-permute-start(bf16[8,1152]{1,0:T(8,128)(2,1)S(1)} %get-tuple-element.53), channel_id=1, source_target_pairs={{0,3},{1,2},{2,1},{3,0},{4,7},{5,6},{6,5},{7,4},{8,11},{9,10},{10,... | collective-permute-start | bytes 55304 | tf_op jit(solution)/shard_map/ppermute | solution.py:308

commit v4 on v3

--- a/solution.py
+++ b/solution.py
@@ -9,10 +9,10 @@
 TOPK = 8
 EXP_DEV = 4
 PARTS = 4
+CUT = 3
 CAP = 8
 LANES = 128
 F32 = jnp.float32
-RETURN_COST = pl.CostEstimate(flops=3 * 10**9, transcendentals=0, bytes_accessed=9 * 10**6)
 BF16 = jnp.bfloat16
 
 
@@ -22,7 +22,7 @@
     )
 
 
-def call(kernel, *args, out, scratch=(), space=pltpu.VMEM, cost=None):
+def call(kernel, *args, out, scratch=(), space=pltpu.VMEM, busy_us=None):
     spec = pl.BlockSpec(memory_space=pltpu.VMEM)
     return pl.pallas_call(
         kernel,
@@ -30,7 +30,9 @@
         in_specs=[pl.BlockSpec(memory_space=space)] * len(args),
         out_specs=[spec] * len(out),
         scratch_shapes=list(scratch),
-        cost_estimate=cost,
+        cost_estimate=busy_us and pl.CostEstimate(
+            flops=busy_us * 10**9, transcendentals=0, bytes_accessed=busy_us * 3 * 10**6
+        ),
         compiler_params=pltpu.CompilerParams(vmem_limit_bytes=32 << 20),
     )(*args)
 
@@ -57,15 +59,20 @@
     return pl.ds(pl.multiple_of(index * size, size), size)
 
 
-def spread_kernel(gate_ref, up_ref, down_ref, saved_ref, whole_ref, both_ref, last_ref, *rest):
-    mine_ref, across_ref, saved, sems = rest
+def spread_kernel(*refs):
+    (gate_ref, up_ref, down_ref, saved_ref, ids_ref, scales_ref, grads_ref), refs = refs[:7], refs[7:]
+    whole_ref, both_ref, last_ref, mine_ref, across_ref, *kept, saved, sems = refs
     hidden = gate_ref.shape[1]
     half = mine_ref.shape[1]
     q, _ = position()
+    sources = (gate_ref, up_ref, down_ref)
     targets = (both_ref.at[:, :hidden], both_ref.at[:, hidden:], last_ref)
-    sources = (gate_ref, up_ref, down_ref)
     again = [whole_ref.at[:, i * hidden : (i + 1) * hidden] for i in range(3)]
-    copies = fetch((saved_ref, *sources, *sources), (saved, *targets, *again), sems)
+    copies = fetch(
+        (saved_ref, *sources, *sources, ids_ref, scales_ref, grads_ref),
+        (saved, *targets, *again, *kept),
+        sems,
+    )
     copies[0].wait()
     mine_ref[...] = saved[:, block(q, half)]
     across_ref[...] = saved[:, block(1 - q, half)]
@@ -73,9 +80,7 @@
         copy.wait()
 
 
-def route_kernel(ids_hbm, scales_hbm, grads_hbm, send_ref, hits_ref, ids_ref, scales_ref, *rest):
-    grads_ref, sems = rest
-    copies = fetch((ids_hbm, scales_hbm, grads_hbm), (ids_ref, scales_ref, grads_ref), sems)
+def route_kernel(ids_ref, scales_ref, grads_ref, send_ref, hits_ref):
     slots, tokens = hits_ref.shape
     owners = slots // CAP
     half = send_ref.shape[1]
@@ -84,8 +89,6 @@
     )
     before = jnp.where(earlier, 1.0, 0.0).astype(BF16)
     slot = lax.broadcasted_iota(jnp.int32, (CAP, tokens), 0).astype(F32)
-    copies[0].wait()
-    copies[1].wait()
     ids = ids_ref[...]
     weights = scales_ref[...].astype(F32)
     hits, scales = [], []
@@ -103,7 +106,6 @@
         scaled.append(jnp.where(here, scales[j], 0.0))
     hits_ref[...] = jnp.concatenate(chosen, axis=0)
     picks = jnp.concatenate(scaled, axis=0).astype(BF16)
-    copies[2].wait()
     rows = dot(picks, grads_ref[...], 1, 0).astype(BF16)
     for h in range(2):
         send_ref[h * slots : (h + 1) * slots, :] = rows[:, h * half : (h + 1) * half]
@@ -185,22 +187,17 @@
 
 def grads_step(replicas):
     def grads_kernel(*refs):
-        parts, outs = refs[:PARTS], refs[PARTS:]
-        hidden_width = outs[0].shape[1]
-        width = outs[0].shape[0]
-        start = 3 * hidden_width
-        for i in range(3):
-            first = start if i < 2 else start + width
-            total = None
-            for part in parts:
-                term = dot(
-                    part[:, first : first + width],
-                    part[:, i * hidden_width : (i + 1) * hidden_width],
-                    0,
-                    0,
-                )
-                total = term if total is None else total + term
-            outs[i][...] = total / replicas
+        parts, (gate_ref, up_ref, down_ref) = refs[:PARTS], refs[PARTS:]
+        width, hidden = gate_ref.shape
+
+        def column(start, size):
+            return jnp.concatenate([part[:, start : start + size] for part in parts], axis=0)
+
+        both = dot(column(3 * hidden, width), column(0, 2 * hidden), 0, 0) / replicas
+        gate_ref[...] = both[:, :hidden]
+        up_ref[...] = both[:, hidden:]
+        down = dot(column(3 * hidden + width, width), column(2 * hidden, hidden), 0, 0)
+        down_ref[...] = down / replicas
 
     return grads_kernel
 
@@ -240,29 +237,26 @@
         blocks = value.reshape(2 * owners, CAP, value.shape[1])
         return lax.all_to_all(blocks, ("q", "exp"), 0, 0, tiled=True).reshape(value.shape)
 
-    whole, both, last, mine, across = call(
+    whole, both, last, mine, across, ids, scales, grads = call(
         spread_kernel,
         *in_hbm(gate_weight[0], up_weight[0], down_weight[0], saved_inputs[0, 0]),
+        *in_hbm(expert_ids[0].T, route_weights[0].T, out_grad[0]),
         out=[((width, n * hidden_width), BF16) for n in (3, 2, 1)]
-        + [((slots, half), BF16)] * 2,
-        scratch=[pltpu.VMEM((slots, features), BF16), pltpu.SemaphoreType.DMA((7,))],
+        + [((slots, half), BF16)] * 2
+        + [((TOPK, tokens), jnp.int32), ((TOPK, tokens), BF16), ((tokens, features), BF16)],
+        scratch=[pltpu.VMEM((slots, features), BF16), pltpu.SemaphoreType.DMA((10,))],
         space=pltpu.HBM,
     )
     theirs = across_halves(across)
-    whole = in_half(whole, PARTS - 1)
-    both = [both] + [in_half(both, k) for k in range(1, PARTS - 1)] + [whole]
-    last = [last] + [in_half(last, k) for k in range(1, PARTS - 1)] + [whole]
-    sent, hits, ids, scales = call(
+    wholes = {k: in_half(whole, k) for k in range(1, PARTS) if k != CUT}
+    both = [both] + [wholes[k] if k in wholes else in_half(both, k) for k in range(1, PARTS)]
+    last = [last] + [wholes[k] if k in wholes else in_half(last, k) for k in range(1, PARTS)]
+    sent, hits = call(
         route_kernel,
-        *in_hbm(expert_ids[0].T, route_weights[0].T, out_grad[0]),
-        out=[
-            ((rows, half), BF16),
-            ((slots, tokens), F32),
-            ((TOPK, tokens), jnp.int32),
-            ((TOPK, tokens), BF16),
-        ],
-        scratch=[pltpu.VMEM((tokens, features), BF16), pltpu.SemaphoreType.DMA((3,))],
-        space=pltpu.HBM,
+        ids,
+        scales,
+        grads,
+        out=[((rows, half), BF16), ((slots, tokens), F32)],
     )
     routed = exchange(sent)
     pair, gate_up, partial = call(
@@ -270,6 +264,7 @@
         mine,
         theirs,
         *both,
+        busy_us=5,
         out=[
             ((rows, half), BF16),
             ((rows, 2 * hidden_width), F32),
@@ -300,7 +295,7 @@
         return_kernel,
         kept,
         across_halves(swapped),
-        cost=RETURN_COST,
+        busy_us=3,
         out=[((CAP, features + LANES), BF16)] * owners,
         scratch=[pltpu.VMEM((slots, features + LANES), F32)],
     )

time: 43 us -> 41.9 us (0.974)
  starting transfers between devices: 28.2 us -> 26.5 us
  waiting for transfers between devices: 7.65 us -> 9.26 us
  Pallas kernels: 6.23 us -> 5.25 us
    ppermute x4, starting transfers between devices: 12.6 us -> 9.56 us  [across_halves(): return lax.ppermute(value, 'q', [(0, 1), (1, 0)])]
    ppermute x8 -> x7, waiting for transfers between devices: 1.45 us -> 3.37 us  [in_half(): return lax.ppermute(value, 'p', [(i, i ^ mask) for i in range(PARTS)])]
    ppermute x8 -> x7, starting transfers between devices: 9.79 us -> 11 us  [in_half(): return lax.ppermute(value, 'p', [(i, i ^ mask) for i in range(PARTS)])]
    pallas_call x8, Pallas kernels: 6.23 us -> 5.25 us  [call(): pl.pallas_call(kernel, out_shape=[jax.ShapeDtypeStruct(s, d) for s, d in...]
  transfers between devices with their start and end apart: 16 -> 15, of which waited for: 7 -> 7; matrix products, arithmetic and copies ran while one was open for 0% -> 0% of each run, Pallas kernels for 8% -> 6%
where the time goes in v4:
time: 41.9 us; the launch traced here: 41.7 us
  starting transfers between devices  26.5 us (63%)
  waiting for transfers between devices  9.26 us (22%)
  Pallas kernels  5.25 us (13%)
  between operations  0.7 us (2%)
    ppermute x7, starting transfers between devices, in_half(): return lax.ppermute(value, 'p', [(i, i ^ mask) for i in range(PARTS)])  11 us
    ppermute x4, starting transfers between devices, across_halves(): return lax.ppermute(value, 'q', [(0, 1), (1, 0)])  9.56 us
    pallas_call x8, Pallas kernels, call(): pl.pallas_call(kernel, out_shape=[jax.ShapeDtypeStruct(s, d) for s, d in...  5.25 us
    ppermute x4, waiting for transfers between devices, across_halves(): return lax.ppermute(value, 'q', [(0, 1), (1, 0)])  3.58 us
    ppermute x7, waiting for transfers between devices, in_half(): return lax.ppermute(value, 'p', [(i, i ^ mask) for i in range(PARTS)])  3.37 us
    all_to_all x1, starting transfers between devices, exchange(): lax.all_to_all(blocks, ('q', 'exp'), 0, 0, tiled=True).reshape(value.shape)  3.35 us
    ppermute x3, starting transfers between devices, body(): lax.ppermute(pieces[m], 'exp', [(i, i ^ m) for i in range(owners)])  2.52 us
    ppermute x3, waiting for transfers between devices, body(): lax.ppermute(pieces[m], 'exp', [(i, i ^ m) for i in range(owners)])  2.31 us
  transfers between devices with their start and end apart: 15, of which 7 were waited for; matrix products, arithmetic and copies ran while one was open for 0% of the time, Pallas kernels for 6%

profile of v4, /device:TPU:0, one launch (start us, length us, event | category | flops | bytes accessed | tf_op | source)
XLA Modules:
  0.0 41.7 jit_solution(9155304050074763432)
XLA Ops:
  0.6 1.4 %shard_map.110 = (bf16[128,1152]{1,0:T(8,128)(2,1)S(1)}, bf16[128,768]{1,0:T(8,128)(2,1)S(1)}, bf16[128,384]{1,0:T(8,128)(2,1)S(1)}, bf16[32,512]{1,0:T(8,128)(2...) custom-call(bf16[128,384]{1,0:T(8,128)(2,1)} %bitcast.23, ...), custom_call_target="tpu_custom_call" | custom-call | tf_op jit(solution)/shard_map/pallas_call | solution.py:27
  2.0 3.1 %collective-permute-start.2 = (bf16[128,1152]{1,0:T(8,128)(2,1)S(1)}, bf16[128,1152]{1,0:T(8,128)(2,1)S(1)}, u32[]{:S(2)}, u32[]{:S(2)}) collective-permute-start(bf16[128,1152]{1,0:T(8,128)(2,1)S(1)} %get-tuple-element.42), channel_id=1, source_target_pairs={{0,8},{4,12},{8,0},{12,4},{1,9},{5,13},{9,1},{13,5},{2,10},{6,14},... | collective-permute-start | bytes 884744 | tf_op jit(solution)/shard_map/ppermute | solution.py:231
  5.1 1.5 %collective-permute-start.1 = (bf16[128,1152]{1,0:T(8,128)(2,1)S(1)}, bf16[128,1152]{1,0:T(8,128)(2,1)S(1)}, u32[]{:S(2)}, u32[]{:S(2)}) collective-permute-start(bf16[128,1152]{1,0:T(8,128)(2,1)S(1)} %get-tuple-element.42), channel_id=1, source_target_pairs={{0,4},{4,0},{8,12},{12,8},{1,5},{5,1},{9,13},{13,9},{2,6},{6,2},{1... | collective-permute-start | bytes 884744 | tf_op jit(solution)/shard_map/ppermute | solution.py:231
  6.6 0.0 collective-permute-start.3
  6.6 3.0 %collective-permute-start = (bf16[32,512]{1,0:T(8,128)(2,1)S(1)}, bf16[32,512]{1,0:T(8,128)(2,1)S(1)}, u32[]{:S(2)}, u32[]{:S(2)}) collective-permute-start(bf16[32,512]{1,0:T(8,128)(2,1)S(1)} %get-tuple-element.40), channel_id=1, source_target_pairs={{0,16},{16,0},{1,17},{17,1},{2,18},{18,2},{3,19},{19,3},{4,20},{20... | collective-permute-start | bytes 98312 | tf_op jit(solution)/shard_map/ppermute | solution.py:234
  9.6 0.9 %shard_map.111 = (bf16[64,512]{1,0:T(8,128)(2,1)}, f32[32,128]{1,0:T(8,128)S(1)}) custom-call(s32[8,128]{1,0:T(8,128)S(1)} %get-tuple-element.35.ids_ref, bf16[8,128]{1,0:T(8,128)(2,1)S(1)} %get-tuple-element.36.scales_ref, bf16[128,1024]{1,0:T(8,128)(2,1)S(1)} %get-tuple-element.37.grads_ref), custom_call_target="tpu_custom_call" | custom-call | tf_op jit(solution)/shard_map/pallas_call | solution.py:27
  10.5 3.4 %all-to-all-start = ((bf16[8,8,512]{2,1,0:T(8,128)(2,1)}), bf16[8,8,512]{2,1,0:T(8,128)(2,1)S(1)}, u32[]{:S(2)}, u32[]{:S(2)}) async-start(bf16[8,8,512]{2,1,0:T(8,128)(2,1)} %bitcast.9), calls=%async_computation | async-start | bytes 131072 | tf_op jit(solution)/shard_map/all_to_all | solution.py:238
  13.9 2.6 %collective-permute-start.5 = (bf16[128,384]{1,0:T(8,128)(2,1)S(1)}, bf16[128,384]{1,0:T(8,128)(2,1)S(1)}, u32[]{:S(2)}, u32[]{:S(2)}) collective-permute-start(bf16[128,384]{1,0:T(8,128)(2,1)S(1)} %get-tuple-element.46.refs_0_), channel_id=1, source_target_pairs={{0,12},{4,8},{8,4},{12,0},{1,13},{5,9},{9,5},{13,1},{2,14},{6,10},... | collective-permute-start | bytes 294920 | tf_op jit(solution)/shard_map/ppermute | solution.py:231
  16.5 0.2 collective-permute-done.theirs_ref
  16.7 1.7 %collective-permute-done.3.refs_3_ = bf16[128,768]{1,0:T(8,128)(2,1)S(1)} collective-permute-done((bf16[128,768]{1,0:T(8,128)(2,1)S(1)}, bf16[128,768]{1,0:T(8,128)(2,1)S(1)}, u32[]{:S(2)}, u32[]{:S(2)}) %collective-permute-start.3) | collective-permute-done | bytes 196640 | tf_op jit(solution)/shard_map/ppermute | solution.py:231
  18.4 0.0 collective-permute-done.2.refs_2_
  18.4 0.0 collective-permute-done.1.refs_1_
  18.4 0.3 shard_map.112
  18.6 2.1 %collective-permute-start.4 = (bf16[64,768]{1,0:T(8,128)(2,1)S(1)}, bf16[64,768]{1,0:T(8,128)(2,1)S(1)}, u32[]{:S(2)}, u32[]{:S(2)}) collective-permute-start(bf16[64,768]{1,0:T(8,128)(2,1)S(1)} %get-tuple-element.44), channel_id=1, source_target_pairs={{0,16},{16,0},{1,17},{17,1},{2,18},{18,2},{3,19},{19,3},{4,20},{20... | collective-permute-start | bytes 294920 | tf_op jit(solution)/shard_map/ppermute | solution.py:234
  20.7 0.2 collective-permute-done.5.refs_3_
  20.9 0.0 all-to-all-done
  20.9 0.2 shard_map.113
  21.1 2.7 %collective-permute-start.6 = (bf16[64,384]{1,0:T(8,128)(2,1)S(1)}, bf16[64,384]{1,0:T(8,128)(2,1)S(1)}, u32[]{:S(2)}, u32[]{:S(2)}) collective-permute-start(bf16[64,384]{1,0:T(8,128)(2,1)S(1)} %get-tuple-element.48), channel_id=1, source_target_pairs={{0,16},{16,0},{1,17},{17,1},{2,18},{18,2},{3,19},{19,3},{4,20},{20... | collective-permute-start | bytes 147464 | tf_op jit(solution)/shard_map/ppermute | solution.py:234
  23.8 3.4 %collective-permute-done.6.down_other_ref = bf16[64,384]{1,0:T(8,128)(2,1)S(1)} collective-permute-done((bf16[64,384]{1,0:T(8,128)(2,1)S(1)}, bf16[64,384]{1,0:T(8,128)(2,1)S(1)}, u32[]{:S(2)}, u32[]{:S(2)}) %collective-permute-start.6) | collective-permute-done | bytes 49184 | tf_op jit(solution)/shard_map/ppermute | solution.py:234
  27.2 0.0 collective-permute-done.4.other_ref
  27.2 0.5 %shard_map.114 = (bf16[32,640]{1,0:T(8,128)(2,1)S(1)}, bf16[32,640]{1,0:T(8,128)(2,1)S(1)}, bf16[64,1408]{1,0:T(8,128)(2,1)S(1)}, bf16[64,1408]{1,0:T(8,128)(2,1...) custom-call(f32[64,768]{1,0:T(8,128)S(1)} %get-tuple-element.43.gate_up_ref, ...), custom_call_target="tpu_custom_call" | custom-call | tf_op jit(solution)/shard_map/pallas_call | solution.py:27
  27.7 1.8 %collective-permute-start.7 = (bf16[32,640]{1,0:T(8,128)(2,1)S(1)}, bf16[32,640]{1,0:T(8,128)(2,1)S(1)}, u32[]{:S(2)}, u32[]{:S(2)}) collective-permute-start(bf16[32,640]{1,0:T(8,128)(2,1)S(1)} %get-tuple-element.51), channel_id=1, source_target_pairs={{0,16},{16,0},{1,17},{17,1},{2,18},{18,2},{3,19},{19,3},{4,20},{20... | collective-permute-start | bytes 122888 | tf_op jit(solution)/shard_map/ppermute | solution.py:234
  29.5 0.4 %collective-permute-start.11 = (bf16[64,1408]{1,0:T(8,128)(2,1)S(1)}, bf16[64,1408]{1,0:T(8,128)(2,1)S(1)}, u32[]{:S(2)}, u32[]{:S(2)}) collective-permute-start(bf16[64,1408]{1,0:T(8,128)(2,1)S(1)} %get-tuple-element.59), channel_id=1, source_target_pairs={{0,4},{4,0},{8,12},{12,8},{1,5},{5,1},{9,13},{13,9},{2,6},{6,2},{1... | collective-permute-start | bytes 540680 | tf_op jit(solution)/shard_map/ppermute | solution.py:231
  29.9 3.2 %collective-permute-start.12 = (bf16[64,1408]{1,0:T(8,128)(2,1)S(1)}, bf16[64,1408]{1,0:T(8,128)(2,1)S(1)}, u32[]{:S(2)}, u32[]{:S(2)}) collective-permute-start(bf16[64,1408]{1,0:T(8,128)(2,1)S(1)} %get-tuple-element.60), channel_id=1, source_target_pairs={{0,8},{4,12},{8,0},{12,4},{1,9},{5,13},{9,1},{13,5},{2,10},{6,14},... | collective-permute-start | bytes 540680 | tf_op jit(solution)/shard_map/ppermute | solution.py:231
  33.1 0.2 collective-permute-start.13
  33.3 0.0 collective-permute-done.7.swap_ref
  33.4 0.1 collective-permute-start.8
  33.4 1.6 %collective-permute-start.9 = (bf16[8,1152]{1,0:T(8,128)(2,1)S(1)}, bf16[8,1152]{1,0:T(8,128)(2,1)S(1)}, u32[]{:S(2)}, u32[]{:S(2)}) collective-permute-start(bf16[8,1152]{1,0:T(8,128)(2,1)S(1)} %get-tuple-element.54), channel_id=1, source_target_pairs={{0,2},{1,3},{2,0},{3,1},{4,6},{5,7},{6,4},{7,5},{8,10},{9,11},{10,... | collective-permute-start | bytes 55304 | tf_op jit(solution)/shard_map/ppermute | solution.py:303
  35.0 0.0 collective-permute-done.8.refs_1_
  35.0 0.9 %collective-permute-start.10 = (bf16[8,1152]{1,0:T(8,128)(2,1)S(1)}, bf16[8,1152]{1,0:T(8,128)(2,1)S(1)}, u32[]{:S(2)}, u32[]{:S(2)}) collective-permute-start(bf16[8,1152]{1,0:T(8,128)(2,1)S(1)} %get-tuple-element.55), channel_id=1, source_target_pairs={{0,3},{1,2},{2,1},{3,0},{4,7},{5,6},{6,5},{7,4},{8,11},{9,10},{10,... | collective-permute-start | bytes 55304 | tf_op jit(solution)/shard_map/ppermute | solution.py:303
  35.9 1.4 %collective-permute-done.9.refs_2_ = bf16[8,1152]{1,0:T(8,128)(2,1)S(1)} collective-permute-done((bf16[8,1152]{1,0:T(8,128)(2,1)S(1)}, bf16[8,1152]{1,0:T(8,128)(2,1)S(1)}, u32[]{:S(2)}, u32[]{:S(2)}) %collective-permute-start.9) | collective-permute-done | bytes 18464 | tf_op jit(solution)/shard_map/ppermute | solution.py:303
  37.3 0.9 %collective-permute-done.10.refs_3_ = bf16[8,1152]{1,0:T(8,128)(2,1)S(1)} collective-permute-done((bf16[8,1152]{1,0:T(8,128)(2,1)S(1)}, bf16[8,1152]{1,0:T(8,128)(2,1)S(1)}, u32[]{:S(2)}, u32[]{:S(2)}) %collective-permute-start.10) | collective-permute-done | bytes 18464 | tf_op jit(solution)/shard_map/ppermute | solution.py:303
  38.2 1.0 %shard_map.116 = (bf16[128,1024]{1,0:T(8,128)(2,1)}, bf16[8,128]{1,0:T(8,128)(2,1)}) custom-call(s32[8,128]{1,0:T(8,128)S(1)} %get-tuple-element.35.ids_ref, bf16[8,128]{1,0:T(8,128)(2,1)S(1)} %get-tuple-element.36.scales_ref, f32[32,128]{1,0:T(8,128)S(1)} %get-tuple-element.38.hits_ref, bf16[8,1152]{1,0:T(8,128)(2,1)S(1)} %get-tuple-element.52.refs_0_, ...), custom_call_target="tpu_custom_call" | custom-call | tf_op jit(solution)/shard_map/pallas_call | solution.py:27
  39.2 0.0 collective-permute-done.11.refs_1_
  39.2 0.0 collective-permute-done.12.refs_2_
  39.2 1.5 %collective-permute-done.13.refs_3_ = bf16[64,1408]{1,0:T(8,128)(2,1)S(1)} collective-permute-done((bf16[64,1408]{1,0:T(8,128)(2,1)S(1)}, bf16[64,1408]{1,0:T(8,128)(2,1)S(1)}, u32[]{:S(2)}, u32[]{:S(2)}) %collective-permute-start.13) | collective-permute-done | bytes 180256 | tf_op jit(solution)/shard_map/ppermute | solution.py:231
  40.7 1.0 %shard_map.117 = (f32[128,384]{1,0:T(8,128)}, f32[128,384]{1,0:T(8,128)}, f32[128,384]{1,0:T(8,128)}) custom-call(bf16[64,1408]{1,0:T(8,128)(2,1)S(1)} %get-tuple-element.58.refs_0_, bf16[64,1408]{1,0:T(8,128)(2,1)S(1)} %collective-permute-done.11.refs_1_, bf16[64,1408]{1,0:T(8,128)(2,1)S(1)} %collective-permute-done.12.refs_2_, ...), custom_call_target="tpu_custom_call" | custom-call | tf_op jit(solution)/shard_map/pallas_call | solution.py:27
  (1 shorter events, 0.0 us)
Async XLA Ops:
  2.0 16.4 %collective-permute-start.2 = (bf16[128,1152]{1,0:T(8,128)(2,1)S(1)}, bf16[128,1152]{1,0:T(8,128)(2,1)S(1)}, u32[]{:S(2)}, u32[]{:S(2)}) collective-permute-start(bf16[128,1152]{1,0:T(8,128)(2,1)S(1)} %get-tuple-element.42), channel_id=1, source_target_pairs={{0,8},{4,12},{8,0},{12,4},{1,9},{5,13},{9,1},{13,5},{2,10},{6,14},... | collective-permute-start | bytes 884744 | tf_op jit(solution)/shard_map/ppermute | solution.py:231
  5.1 13.3 %collective-permute-start.1 = (bf16[128,1152]{1,0:T(8,128)(2,1)S(1)}, bf16[128,1152]{1,0:T(8,128)(2,1)S(1)}, u32[]{:S(2)}, u32[]{:S(2)}) collective-permute-start(bf16[128,1152]{1,0:T(8,128)(2,1)S(1)} %get-tuple-element.42), channel_id=1, source_target_pairs={{0,4},{4,0},{8,12},{12,8},{1,5},{5,1},{9,13},{13,9},{2,6},{6,2},{1... | collective-permute-start | bytes 884744 | tf_op jit(solution)/shard_map/ppermute | solution.py:231
  6.6 11.8 %collective-permute-start.3 = (bf16[128,768]{1,0:T(8,128)(2,1)S(1)}, bf16[128,768]{1,0:T(8,128)(2,1)S(1)}, u32[]{:S(2)}, u32[]{:S(2)}) collective-permute-start(bf16[128,768]{1,0:T(8,128)(2,1)S(1)} %get-tuple-element.41.refs_0_), channel_id=1, source_target_pairs={{0,12},{4,8},{8,4},{12,0},{1,13},{5,9},{9,5},{13,1},{2,14},{6,10},... | collective-permute-start | bytes 589832 | tf_op jit(solution)/shard_map/ppermute | solution.py:231
  6.6 10.0 %collective-permute-start = (bf16[32,512]{1,0:T(8,128)(2,1)S(1)}, bf16[32,512]{1,0:T(8,128)(2,1)S(1)}, u32[]{:S(2)}, u32[]{:S(2)}) collective-permute-start(bf16[32,512]{1,0:T(8,128)(2,1)S(1)} %get-tuple-element.40), channel_id=1, source_target_pairs={{0,16},{16,0},{1,17},{17,1},{2,18},{18,2},{3,19},{19,3},{4,20},{20... | collective-permute-start | bytes 98312 | tf_op jit(solution)/shard_map/ppermute | solution.py:234
  10.5 10.4 %all-to-all-start = ((bf16[8,8,512]{2,1,0:T(8,128)(2,1)}), bf16[8,8,512]{2,1,0:T(8,128)(2,1)S(1)}, u32[]{:S(2)}, u32[]{:S(2)}) async-start(bf16[8,8,512]{2,1,0:T(8,128)(2,1)} %bitcast.9), calls=%async_computation | async-start | bytes 131072 | tf_op jit(solution)/shard_map/all_to_all | solution.py:238
  13.9 7.0 %collective-permute-start.5 = (bf16[128,384]{1,0:T(8,128)(2,1)S(1)}, bf16[128,384]{1,0:T(8,128)(2,1)S(1)}, u32[]{:S(2)}, u32[]{:S(2)}) collective-permute-start(bf16[128,384]{1,0:T(8,128)(2,1)S(1)} %get-tuple-element.46.refs_0_), channel_id=1, source_target_pairs={{0,12},{4,8},{8,4},{12,0},{1,13},{5,9},{9,5},{13,1},{2,14},{6,10},... | collective-permute-start | bytes 294920 | tf_op jit(solution)/shard_map/ppermute | solution.py:231
  18.6 8.6 %collective-permute-start.4 = (bf16[64,768]{1,0:T(8,128)(2,1)S(1)}, bf16[64,768]{1,0:T(8,128)(2,1)S(1)}, u32[]{:S(2)}, u32[]{:S(2)}) collective-permute-start(bf16[64,768]{1,0:T(8,128)(2,1)S(1)} %get-tuple-element.44), channel_id=1, source_target_pairs={{0,16},{16,0},{1,17},{17,1},{2,18},{18,2},{3,19},{19,3},{4,20},{20... | collective-permute-start | bytes 294920 | tf_op jit(solution)/shard_map/ppermute | solution.py:234
  21.1 6.1 %collective-permute-start.6 = (bf16[64,384]{1,0:T(8,128)(2,1)S(1)}, bf16[64,384]{1,0:T(8,128)(2,1)S(1)}, u32[]{:S(2)}, u32[]{:S(2)}) collective-permute-start(bf16[64,384]{1,0:T(8,128)(2,1)S(1)} %get-tuple-element.48), channel_id=1, source_target_pairs={{0,16},{16,0},{1,17},{17,1},{2,18},{18,2},{3,19},{19,3},{4,20},{20... | collective-permute-start | bytes 147464 | tf_op jit(solution)/shard_map/ppermute | solution.py:234
  27.7 5.6 %collective-permute-start.7 = (bf16[32,640]{1,0:T(8,128)(2,1)S(1)}, bf16[32,640]{1,0:T(8,128)(2,1)S(1)}, u32[]{:S(2)}, u32[]{:S(2)}) collective-permute-start(bf16[32,640]{1,0:T(8,128)(2,1)S(1)} %get-tuple-element.51), channel_id=1, source_target_pairs={{0,16},{16,0},{1,17},{17,1},{2,18},{18,2},{3,19},{19,3},{4,20},{20... | collective-permute-start | bytes 122888 | tf_op jit(solution)/shard_map/ppermute | solution.py:234
  29.5 9.7 %collective-permute-start.11 = (bf16[64,1408]{1,0:T(8,128)(2,1)S(1)}, bf16[64,1408]{1,0:T(8,128)(2,1)S(1)}, u32[]{:S(2)}, u32[]{:S(2)}) collective-permute-start(bf16[64,1408]{1,0:T(8,128)(2,1)S(1)} %get-tuple-element.59), channel_id=1, source_target_pairs={{0,4},{4,0},{8,12},{12,8},{1,5},{5,1},{9,13},{13,9},{2,6},{6,2},{1... | collective-permute-start | bytes 540680 | tf_op jit(solution)/shard_map/ppermute | solution.py:231
  29.9 9.3 %collective-permute-start.12 = (bf16[64,1408]{1,0:T(8,128)(2,1)S(1)}, bf16[64,1408]{1,0:T(8,128)(2,1)S(1)}, u32[]{:S(2)}, u32[]{:S(2)}) collective-permute-start(bf16[64,1408]{1,0:T(8,128)(2,1)S(1)} %get-tuple-element.60), channel_id=1, source_target_pairs={{0,8},{4,12},{8,0},{12,4},{1,9},{5,13},{9,1},{13,5},{2,10},{6,14},... | collective-permute-start | bytes 540680 | tf_op jit(solution)/shard_map/ppermute | solution.py:231
  33.1 7.6 %collective-permute-start.13 = (bf16[64,1408]{1,0:T(8,128)(2,1)S(1)}, bf16[64,1408]{1,0:T(8,128)(2,1)S(1)}, u32[]{:S(2)}, u32[]{:S(2)}) collective-permute-start(bf16[64,1408]{1,0:T(8,128)(2,1)S(1)} %get-tuple-element.61), channel_id=1, source_target_pairs={{0,12},{4,8},{8,4},{12,0},{1,13},{5,9},{9,5},{13,1},{2,14},{6,10},... | collective-permute-start | bytes 540680 | tf_op jit(solution)/shard_map/ppermute | solution.py:231
  33.4 1.7 %collective-permute-start.8 = (bf16[8,1152]{1,0:T(8,128)(2,1)S(1)}, bf16[8,1152]{1,0:T(8,128)(2,1)S(1)}, u32[]{:S(2)}, u32[]{:S(2)}) collective-permute-start(bf16[8,1152]{1,0:T(8,128)(2,1)S(1)} %get-tuple-element.53), channel_id=1, source_target_pairs={{0,1},{1,0},{2,3},{3,2},{4,5},{5,4},{6,7},{7,6},{8,9},{9,8},{10,11... | collective-permute-start | bytes 55304 | tf_op jit(solution)/shard_map/ppermute | solution.py:303
  33.4 3.8 %collective-permute-start.9 = (bf16[8,1152]{1,0:T(8,128)(2,1)S(1)}, bf16[8,1152]{1,0:T(8,128)(2,1)S(1)}, u32[]{:S(2)}, u32[]{:S(2)}) collective-permute-start(bf16[8,1152]{1,0:T(8,128)(2,1)S(1)} %get-tuple-element.54), channel_id=1, source_target_pairs={{0,2},{1,3},{2,0},{3,1},{4,6},{5,7},{6,4},{7,5},{8,10},{9,11},{10,... | collective-permute-start | bytes 55304 | tf_op jit(solution)/shard_map/ppermute | solution.py:303
  35.0 3.2 %collective-permute-start.10 = (bf16[8,1152]{1,0:T(8,128)(2,1)S(1)}, bf16[8,1152]{1,0:T(8,128)(2,1)S(1)}, u32[]{:S(2)}, u32[]{:S(2)}) collective-permute-start(bf16[8,1152]{1,0:T(8,128)(2,1)S(1)} %get-tuple-element.55), channel_id=1, source_target_pairs={{0,3},{1,2},{2,1},{3,0},{4,7},{5,6},{6,5},{7,4},{8,11},{9,10},{10,... | collective-permute-start | bytes 55304 | tf_op jit(solution)/shard_map/ppermute | solution.py:303

commit v5 on v4

--- a/solution.py
+++ b/solution.py
@@ -303,7 +303,7 @@
         lax.ppermute(pieces[m], "exp", [(i, i ^ m) for i in range(owners)])
         for m in range(1, owners)
     ]
-    sends = [sends[0]] + [in_half(sends[k], k) for k in range(1, PARTS)]
+    sends = [sends[0]] + [in_half(sends[k], k) for k in (3, 1, 2)]
     gate_grad, up_grad, down_grad = call(
         grads_step(replicas), *sends, out=[((width, hidden_width), F32)] * 3
     )

time: 41.9 us -> 41.6 us (level)
  no operation moved by 1% of the time
where the time goes in v5:
time: 41.6 us; the launch traced here: 41.4 us
  starting transfers between devices  26.5 us (64%)
  waiting for transfers between devices  9 us (22%)
  Pallas kernels  5.25 us (13%)
  between operations  0.7 us (2%)
    ppermute x7, starting transfers between devices, in_half(): return lax.ppermute(value, 'p', [(i, i ^ mask) for i in range(PARTS)])  11 us
    ppermute x4, starting transfers between devices, across_halves(): return lax.ppermute(value, 'q', [(0, 1), (1, 0)])  9.56 us
    pallas_call x8, Pallas kernels, call(): pl.pallas_call(kernel, out_shape=[jax.ShapeDtypeStruct(s, d) for s, d in...  5.25 us
    ppermute x4, waiting for transfers between devices, across_halves(): return lax.ppermute(value, 'q', [(0, 1), (1, 0)])  3.58 us
    all_to_all x1, starting transfers between devices, exchange(): lax.all_to_all(blocks, ('q', 'exp'), 0, 0, tiled=True).reshape(value.shape)  3.35 us
    ppermute x7, waiting for transfers between devices, in_half(): return lax.ppermute(value, 'p', [(i, i ^ mask) for i in range(PARTS)])  3.11 us
    ppermute x3, starting transfers between devices, body(): lax.ppermute(pieces[m], 'exp', [(i, i ^ m) for i in range(owners)])  2.52 us
    ppermute x3, waiting for transfers between devices, body(): lax.ppermute(pieces[m], 'exp', [(i, i ^ m) for i in range(owners)])  2.31 us
  transfers between devices with their start and end apart: 15, of which 7 were waited for; matrix products, arithmetic and copies ran while one was open for 0% of the time, Pallas kernels for 6%

profile of v5, /device:TPU:0, one launch (start us, length us, event | category | flops | bytes accessed | tf_op | source)
XLA Modules:
  0.0 41.4 jit_solution(9083431901946920563)
XLA Ops:
  0.6 1.4 %shard_map.110 = (bf16[128,1152]{1,0:T(8,128)(2,1)S(1)}, bf16[128,768]{1,0:T(8,128)(2,1)S(1)}, bf16[128,384]{1,0:T(8,128)(2,1)S(1)}, bf16[32,512]{1,0:T(8,128)(2...) custom-call(bf16[128,384]{1,0:T(8,128)(2,1)} %bitcast.23, ...), custom_call_target="tpu_custom_call" | custom-call | tf_op jit(solution)/shard_map/pallas_call | solution.py:27
  2.0 3.1 %collective-permute-start.2 = (bf16[128,1152]{1,0:T(8,128)(2,1)S(1)}, bf16[128,1152]{1,0:T(8,128)(2,1)S(1)}, u32[]{:S(2)}, u32[]{:S(2)}) collective-permute-start(bf16[128,1152]{1,0:T(8,128)(2,1)S(1)} %get-tuple-element.42), channel_id=1, source_target_pairs={{0,8},{4,12},{8,0},{12,4},{1,9},{5,13},{9,1},{13,5},{2,10},{6,14},... | collective-permute-start | bytes 884744 | tf_op jit(solution)/shard_map/ppermute | solution.py:231
  5.1 1.5 %collective-permute-start.1 = (bf16[128,1152]{1,0:T(8,128)(2,1)S(1)}, bf16[128,1152]{1,0:T(8,128)(2,1)S(1)}, u32[]{:S(2)}, u32[]{:S(2)}) collective-permute-start(bf16[128,1152]{1,0:T(8,128)(2,1)S(1)} %get-tuple-element.42), channel_id=1, source_target_pairs={{0,4},{4,0},{8,12},{12,8},{1,5},{5,1},{9,13},{13,9},{2,6},{6,2},{1... | collective-permute-start | bytes 884744 | tf_op jit(solution)/shard_map/ppermute | solution.py:231
  6.6 0.0 collective-permute-start.3
  6.6 3.0 %collective-permute-start = (bf16[32,512]{1,0:T(8,128)(2,1)S(1)}, bf16[32,512]{1,0:T(8,128)(2,1)S(1)}, u32[]{:S(2)}, u32[]{:S(2)}) collective-permute-start(bf16[32,512]{1,0:T(8,128)(2,1)S(1)} %get-tuple-element.40), channel_id=1, source_target_pairs={{0,16},{16,0},{1,17},{17,1},{2,18},{18,2},{3,19},{19,3},{4,20},{20... | collective-permute-start | bytes 98312 | tf_op jit(solution)/shard_map/ppermute | solution.py:234
  9.6 0.9 %shard_map.111 = (bf16[64,512]{1,0:T(8,128)(2,1)}, f32[32,128]{1,0:T(8,128)S(1)}) custom-call(s32[8,128]{1,0:T(8,128)S(1)} %get-tuple-element.35.ids_ref, bf16[8,128]{1,0:T(8,128)(2,1)S(1)} %get-tuple-element.36.scales_ref, bf16[128,1024]{1,0:T(8,128)(2,1)S(1)} %get-tuple-element.37.grads_ref), custom_call_target="tpu_custom_call" | custom-call | tf_op jit(solution)/shard_map/pallas_call | solution.py:27
  10.5 3.4 %all-to-all-start = ((bf16[8,8,512]{2,1,0:T(8,128)(2,1)}), bf16[8,8,512]{2,1,0:T(8,128)(2,1)S(1)}, u32[]{:S(2)}, u32[]{:S(2)}) async-start(bf16[8,8,512]{2,1,0:T(8,128)(2,1)} %bitcast.9), calls=%async_computation | async-start | bytes 131072 | tf_op jit(solution)/shard_map/all_to_all | solution.py:238
  13.9 2.6 %collective-permute-start.5 = (bf16[128,384]{1,0:T(8,128)(2,1)S(1)}, bf16[128,384]{1,0:T(8,128)(2,1)S(1)}, u32[]{:S(2)}, u32[]{:S(2)}) collective-permute-start(bf16[128,384]{1,0:T(8,128)(2,1)S(1)} %get-tuple-element.46.refs_0_), channel_id=1, source_target_pairs={{0,12},{4,8},{8,4},{12,0},{1,13},{5,9},{9,5},{13,1},{2,14},{6,10},... | collective-permute-start | bytes 294920 | tf_op jit(solution)/shard_map/ppermute | solution.py:231
  16.5 0.2 collective-permute-done.theirs_ref
  16.7 1.7 %collective-permute-done.3.refs_3_ = bf16[128,768]{1,0:T(8,128)(2,1)S(1)} collective-permute-done((bf16[128,768]{1,0:T(8,128)(2,1)S(1)}, bf16[128,768]{1,0:T(8,128)(2,1)S(1)}, u32[]{:S(2)}, u32[]{:S(2)}) %collective-permute-start.3) | collective-permute-done | bytes 196640 | tf_op jit(solution)/shard_map/ppermute | solution.py:231
  18.4 0.0 collective-permute-done.2.refs_2_
  18.4 0.0 collective-permute-done.1.refs_1_
  18.4 0.3 shard_map.112
  18.6 2.1 %collective-permute-start.4 = (bf16[64,768]{1,0:T(8,128)(2,1)S(1)}, bf16[64,768]{1,0:T(8,128)(2,1)S(1)}, u32[]{:S(2)}, u32[]{:S(2)}) collective-permute-start(bf16[64,768]{1,0:T(8,128)(2,1)S(1)} %get-tuple-element.44), channel_id=1, source_target_pairs={{0,16},{16,0},{1,17},{17,1},{2,18},{18,2},{3,19},{19,3},{4,20},{20... | collective-permute-start | bytes 294920 | tf_op jit(solution)/shard_map/ppermute | solution.py:234
  20.7 0.2 collective-permute-done.5.refs_3_
  20.9 0.0 all-to-all-done
  20.9 0.2 shard_map.113
  21.1 2.7 %collective-permute-start.6 = (bf16[64,384]{1,0:T(8,128)(2,1)S(1)}, bf16[64,384]{1,0:T(8,128)(2,1)S(1)}, u32[]{:S(2)}, u32[]{:S(2)}) collective-permute-start(bf16[64,384]{1,0:T(8,128)(2,1)S(1)} %get-tuple-element.48), channel_id=1, source_target_pairs={{0,16},{16,0},{1,17},{17,1},{2,18},{18,2},{3,19},{19,3},{4,20},{20... | collective-permute-start | bytes 147464 | tf_op jit(solution)/shard_map/ppermute | solution.py:234
  23.8 3.4 %collective-permute-done.6.down_other_ref = bf16[64,384]{1,0:T(8,128)(2,1)S(1)} collective-permute-done((bf16[64,384]{1,0:T(8,128)(2,1)S(1)}, bf16[64,384]{1,0:T(8,128)(2,1)S(1)}, u32[]{:S(2)}, u32[]{:S(2)}) %collective-permute-start.6) | collective-permute-done | bytes 49184 | tf_op jit(solution)/shard_map/ppermute | solution.py:234
  27.2 0.0 collective-permute-done.4.other_ref
  27.2 0.5 %shard_map.114 = (bf16[32,640]{1,0:T(8,128)(2,1)S(1)}, bf16[32,640]{1,0:T(8,128)(2,1)S(1)}, bf16[64,1408]{1,0:T(8,128)(2,1)S(1)}, bf16[64,1408]{1,0:T(8,128)(2,1...) custom-call(f32[64,768]{1,0:T(8,128)S(1)} %get-tuple-element.43.gate_up_ref, ...), custom_call_target="tpu_custom_call" | custom-call | tf_op jit(solution)/shard_map/pallas_call | solution.py:27
  27.7 1.8 %collective-permute-start.7 = (bf16[32,640]{1,0:T(8,128)(2,1)S(1)}, bf16[32,640]{1,0:T(8,128)(2,1)S(1)}, u32[]{:S(2)}, u32[]{:S(2)}) collective-permute-start(bf16[32,640]{1,0:T(8,128)(2,1)S(1)} %get-tuple-element.51), channel_id=1, source_target_pairs={{0,16},{16,0},{1,17},{17,1},{2,18},{18,2},{3,19},{19,3},{4,20},{20... | collective-permute-start | bytes 122888 | tf_op jit(solution)/shard_map/ppermute | solution.py:234
  29.5 3.0 %collective-permute-start.11 = (bf16[64,1408]{1,0:T(8,128)(2,1)S(1)}, bf16[64,1408]{1,0:T(8,128)(2,1)S(1)}, u32[]{:S(2)}, u32[]{:S(2)}) collective-permute-start(bf16[64,1408]{1,0:T(8,128)(2,1)S(1)} %get-tuple-element.59), channel_id=1, source_target_pairs={{0,12},{4,8},{8,4},{12,0},{1,13},{5,9},{9,5},{13,1},{2,14},{6,10},... | collective-permute-start | bytes 540680 | tf_op jit(solution)/shard_map/ppermute | solution.py:231
  32.5 0.8 %collective-permute-start.12 = (bf16[64,1408]{1,0:T(8,128)(2,1)S(1)}, bf16[64,1408]{1,0:T(8,128)(2,1)S(1)}, u32[]{:S(2)}, u32[]{:S(2)}) collective-permute-start(bf16[64,1408]{1,0:T(8,128)(2,1)S(1)} %get-tuple-element.60), channel_id=1, source_target_pairs={{0,4},{4,0},{8,12},{12,8},{1,5},{5,1},{9,13},{13,9},{2,6},{6,2},{1... | collective-permute-start | bytes 540680 | tf_op jit(solution)/shard_map/ppermute | solution.py:231
  33.3 0.0 collective-permute-start.13
  33.3 0.0 collective-permute-done.7.swap_ref
  33.4 0.1 collective-permute-start.8
  33.4 1.6 %collective-permute-start.9 = (bf16[8,1152]{1,0:T(8,128)(2,1)S(1)}, bf16[8,1152]{1,0:T(8,128)(2,1)S(1)}, u32[]{:S(2)}, u32[]{:S(2)}) collective-permute-start(bf16[8,1152]{1,0:T(8,128)(2,1)S(1)} %get-tuple-element.54), channel_id=1, source_target_pairs={{0,2},{1,3},{2,0},{3,1},{4,6},{5,7},{6,4},{7,5},{8,10},{9,11},{10,... | collective-permute-start | bytes 55304 | tf_op jit(solution)/shard_map/ppermute | solution.py:303
  35.0 0.0 collective-permute-done.8.refs_1_
  35.0 0.9 %collective-permute-start.10 = (bf16[8,1152]{1,0:T(8,128)(2,1)S(1)}, bf16[8,1152]{1,0:T(8,128)(2,1)S(1)}, u32[]{:S(2)}, u32[]{:S(2)}) collective-permute-start(bf16[8,1152]{1,0:T(8,128)(2,1)S(1)} %get-tuple-element.55), channel_id=1, source_target_pairs={{0,3},{1,2},{2,1},{3,0},{4,7},{5,6},{6,5},{7,4},{8,11},{9,10},{10,... | collective-permute-start | bytes 55304 | tf_op jit(solution)/shard_map/ppermute | solution.py:303
  35.9 1.4 %collective-permute-done.9.refs_2_ = bf16[8,1152]{1,0:T(8,128)(2,1)S(1)} collective-permute-done((bf16[8,1152]{1,0:T(8,128)(2,1)S(1)}, bf16[8,1152]{1,0:T(8,128)(2,1)S(1)}, u32[]{:S(2)}, u32[]{:S(2)}) %collective-permute-start.9) | collective-permute-done | bytes 18464 | tf_op jit(solution)/shard_map/ppermute | solution.py:303
  37.3 0.9 %collective-permute-done.10.refs_3_ = bf16[8,1152]{1,0:T(8,128)(2,1)S(1)} collective-permute-done((bf16[8,1152]{1,0:T(8,128)(2,1)S(1)}, bf16[8,1152]{1,0:T(8,128)(2,1)S(1)}, u32[]{:S(2)}, u32[]{:S(2)}) %collective-permute-start.10) | collective-permute-done | bytes 18464 | tf_op jit(solution)/shard_map/ppermute | solution.py:303
  38.2 1.0 %shard_map.116 = (bf16[128,1024]{1,0:T(8,128)(2,1)}, bf16[8,128]{1,0:T(8,128)(2,1)}) custom-call(s32[8,128]{1,0:T(8,128)S(1)} %get-tuple-element.35.ids_ref, bf16[8,128]{1,0:T(8,128)(2,1)S(1)} %get-tuple-element.36.scales_ref, f32[32,128]{1,0:T(8,128)S(1)} %get-tuple-element.38.hits_ref, bf16[8,1152]{1,0:T(8,128)(2,1)S(1)} %get-tuple-element.52.refs_0_, ...), custom_call_target="tpu_custom_call" | custom-call | tf_op jit(solution)/shard_map/pallas_call | solution.py:27
  39.2 0.0 collective-permute-done.11.refs_1_
  39.2 1.2 %collective-permute-done.12.refs_2_ = bf16[64,1408]{1,0:T(8,128)(2,1)S(1)} collective-permute-done((bf16[64,1408]{1,0:T(8,128)(2,1)S(1)}, bf16[64,1408]{1,0:T(8,128)(2,1)S(1)}, u32[]{:S(2)}, u32[]{:S(2)}) %collective-permute-start.12) | collective-permute-done | bytes 180256 | tf_op jit(solution)/shard_map/ppermute | solution.py:231
  40.4 0.0 collective-permute-done.13.refs_3_
  40.4 1.0 %shard_map.117 = (f32[128,384]{1,0:T(8,128)}, f32[128,384]{1,0:T(8,128)}, f32[128,384]{1,0:T(8,128)}) custom-call(bf16[64,1408]{1,0:T(8,128)(2,1)S(1)} %get-tuple-element.58.refs_0_, bf16[64,1408]{1,0:T(8,128)(2,1)S(1)} %collective-permute-done.11.refs_1_, bf16[64,1408]{1,0:T(8,128)(2,1)S(1)} %collective-permute-done.12.refs_2_, ...), custom_call_target="tpu_custom_call" | custom-call | tf_op jit(solution)/shard_map/pallas_call | solution.py:27
  (1 shorter events, 0.0 us)
Async XLA Ops:
  2.0 16.4 %collective-permute-start.2 = (bf16[128,1152]{1,0:T(8,128)(2,1)S(1)}, bf16[128,1152]{1,0:T(8,128)(2,1)S(1)}, u32[]{:S(2)}, u32[]{:S(2)}) collective-permute-start(bf16[128,1152]{1,0:T(8,128)(2,1)S(1)} %get-tuple-element.42), channel_id=1, source_target_pairs={{0,8},{4,12},{8,0},{12,4},{1,9},{5,13},{9,1},{13,5},{2,10},{6,14},... | collective-permute-start | bytes 884744 | tf_op jit(solution)/shard_map/ppermute | solution.py:231
  5.1 13.3 %collective-permute-start.1 = (bf16[128,1152]{1,0:T(8,128)(2,1)S(1)}, bf16[128,1152]{1,0:T(8,128)(2,1)S(1)}, u32[]{:S(2)}, u32[]{:S(2)}) collective-permute-start(bf16[128,1152]{1,0:T(8,128)(2,1)S(1)} %get-tuple-element.42), channel_id=1, source_target_pairs={{0,4},{4,0},{8,12},{12,8},{1,5},{5,1},{9,13},{13,9},{2,6},{6,2},{1... | collective-permute-start | bytes 884744 | tf_op jit(solution)/shard_map/ppermute | solution.py:231
  6.6 11.8 %collective-permute-start.3 = (bf16[128,768]{1,0:T(8,128)(2,1)S(1)}, bf16[128,768]{1,0:T(8,128)(2,1)S(1)}, u32[]{:S(2)}, u32[]{:S(2)}) collective-permute-start(bf16[128,768]{1,0:T(8,128)(2,1)S(1)} %get-tuple-element.41.refs_0_), channel_id=1, source_target_pairs={{0,12},{4,8},{8,4},{12,0},{1,13},{5,9},{9,5},{13,1},{2,14},{6,10},... | collective-permute-start | bytes 589832 | tf_op jit(solution)/shard_map/ppermute | solution.py:231
  6.6 10.0 %collective-permute-start = (bf16[32,512]{1,0:T(8,128)(2,1)S(1)}, bf16[32,512]{1,0:T(8,128)(2,1)S(1)}, u32[]{:S(2)}, u32[]{:S(2)}) collective-permute-start(bf16[32,512]{1,0:T(8,128)(2,1)S(1)} %get-tuple-element.40), channel_id=1, source_target_pairs={{0,16},{16,0},{1,17},{17,1},{2,18},{18,2},{3,19},{19,3},{4,20},{20... | collective-permute-start | bytes 98312 | tf_op jit(solution)/shard_map/ppermute | solution.py:234
  10.5 10.4 %all-to-all-start = ((bf16[8,8,512]{2,1,0:T(8,128)(2,1)}), bf16[8,8,512]{2,1,0:T(8,128)(2,1)S(1)}, u32[]{:S(2)}, u32[]{:S(2)}) async-start(bf16[8,8,512]{2,1,0:T(8,128)(2,1)} %bitcast.9), calls=%async_computation | async-start | bytes 131072 | tf_op jit(solution)/shard_map/all_to_all | solution.py:238
  13.9 7.0 %collective-permute-start.5 = (bf16[128,384]{1,0:T(8,128)(2,1)S(1)}, bf16[128,384]{1,0:T(8,128)(2,1)S(1)}, u32[]{:S(2)}, u32[]{:S(2)}) collective-permute-start(bf16[128,384]{1,0:T(8,128)(2,1)S(1)} %get-tuple-element.46.refs_0_), channel_id=1, source_target_pairs={{0,12},{4,8},{8,4},{12,0},{1,13},{5,9},{9,5},{13,1},{2,14},{6,10},... | collective-permute-start | bytes 294920 | tf_op jit(solution)/shard_map/ppermute | solution.py:231
  18.6 8.6 %collective-permute-start.4 = (bf16[64,768]{1,0:T(8,128)(2,1)S(1)}, bf16[64,768]{1,0:T(8,128)(2,1)S(1)}, u32[]{:S(2)}, u32[]{:S(2)}) collective-permute-start(bf16[64,768]{1,0:T(8,128)(2,1)S(1)} %get-tuple-element.44), channel_id=1, source_target_pairs={{0,16},{16,0},{1,17},{17,1},{2,18},{18,2},{3,19},{19,3},{4,20},{20... | collective-permute-start | bytes 294920 | tf_op jit(solution)/shard_map/ppermute | solution.py:234
  21.1 6.1 %collective-permute-start.6 = (bf16[64,384]{1,0:T(8,128)(2,1)S(1)}, bf16[64,384]{1,0:T(8,128)(2,1)S(1)}, u32[]{:S(2)}, u32[]{:S(2)}) collective-permute-start(bf16[64,384]{1,0:T(8,128)(2,1)S(1)} %get-tuple-element.48), channel_id=1, source_target_pairs={{0,16},{16,0},{1,17},{17,1},{2,18},{18,2},{3,19},{19,3},{4,20},{20... | collective-permute-start | bytes 147464 | tf_op jit(solution)/shard_map/ppermute | solution.py:234
  27.7 5.6 %collective-permute-start.7 = (bf16[32,640]{1,0:T(8,128)(2,1)S(1)}, bf16[32,640]{1,0:T(8,128)(2,1)S(1)}, u32[]{:S(2)}, u32[]{:S(2)}) collective-permute-start(bf16[32,640]{1,0:T(8,128)(2,1)S(1)} %get-tuple-element.51), channel_id=1, source_target_pairs={{0,16},{16,0},{1,17},{17,1},{2,18},{18,2},{3,19},{19,3},{4,20},{20... | collective-permute-start | bytes 122888 | tf_op jit(solution)/shard_map/ppermute | solution.py:234
  29.5 9.7 %collective-permute-start.11 = (bf16[64,1408]{1,0:T(8,128)(2,1)S(1)}, bf16[64,1408]{1,0:T(8,128)(2,1)S(1)}, u32[]{:S(2)}, u32[]{:S(2)}) collective-permute-start(bf16[64,1408]{1,0:T(8,128)(2,1)S(1)} %get-tuple-element.59), channel_id=1, source_target_pairs={{0,12},{4,8},{8,4},{12,0},{1,13},{5,9},{9,5},{13,1},{2,14},{6,10},... | collective-permute-start | bytes 540680 | tf_op jit(solution)/shard_map/ppermute | solution.py:231
  32.5 7.9 %collective-permute-start.12 = (bf16[64,1408]{1,0:T(8,128)(2,1)S(1)}, bf16[64,1408]{1,0:T(8,128)(2,1)S(1)}, u32[]{:S(2)}, u32[]{:S(2)}) collective-permute-start(bf16[64,1408]{1,0:T(8,128)(2,1)S(1)} %get-tuple-element.60), channel_id=1, source_target_pairs={{0,4},{4,0},{8,12},{12,8},{1,5},{5,1},{9,13},{13,9},{2,6},{6,2},{1... | collective-permute-start | bytes 540680 | tf_op jit(solution)/shard_map/ppermute | solution.py:231
  33.3 7.1 %collective-permute-start.13 = (bf16[64,1408]{1,0:T(8,128)(2,1)S(1)}, bf16[64,1408]{1,0:T(8,128)(2,1)S(1)}, u32[]{:S(2)}, u32[]{:S(2)}) collective-permute-start(bf16[64,1408]{1,0:T(8,128)(2,1)S(1)} %get-tuple-element.61), channel_id=1, source_target_pairs={{0,8},{4,12},{8,0},{12,4},{1,9},{5,13},{9,1},{13,5},{2,10},{6,14},... | collective-permute-start | bytes 540680 | tf_op jit(solution)/shard_map/ppermute | solution.py:231
  33.4 1.7 %collective-permute-start.8 = (bf16[8,1152]{1,0:T(8,128)(2,1)S(1)}, bf16[8,1152]{1,0:T(8,128)(2,1)S(1)}, u32[]{:S(2)}, u32[]{:S(2)}) collective-permute-start(bf16[8,1152]{1,0:T(8,128)(2,1)S(1)} %get-tuple-element.53), channel_id=1, source_target_pairs={{0,1},{1,0},{2,3},{3,2},{4,5},{5,4},{6,7},{7,6},{8,9},{9,8},{10,11... | collective-permute-start | bytes 55304 | tf_op jit(solution)/shard_map/ppermute | solution.py:303
  33.4 3.8 %collective-permute-start.9 = (bf16[8,1152]{1,0:T(8,128)(2,1)S(1)}, bf16[8,1152]{1,0:T(8,128)(2,1)S(1)}, u32[]{:S(2)}, u32[]{:S(2)}) collective-permute-start(bf16[8,1152]{1,0:T(8,128)(2,1)S(1)} %get-tuple-element.54), channel_id=1, source_target_pairs={{0,2},{1,3},{2,0},{3,1},{4,6},{5,7},{6,4},{7,5},{8,10},{9,11},{10,... | collective-permute-start | bytes 55304 | tf_op jit(solution)/shard_map/ppermute | solution.py:303
  35.0 3.2 %collective-permute-start.10 = (bf16[8,1152]{1,0:T(8,128)(2,1)S(1)}, bf16[8,1152]{1,0:T(8,128)(2,1)S(1)}, u32[]{:S(2)}, u32[]{:S(2)}) collective-permute-start(bf16[8,1152]{1,0:T(8,128)(2,1)S(1)} %get-tuple-element.55), channel_id=1, source_target_pairs={{0,3},{1,2},{2,1},{3,0},{4,7},{5,6},{6,5},{7,4},{8,11},{9,10},{10,... | collective-permute-start | bytes 55304 | tf_op jit(solution)/shard_map/ppermute | solution.py:303

commit v6 on v5

--- a/solution.py
+++ b/solution.py
@@ -193,11 +193,11 @@
         def column(start, size):
             return jnp.concatenate([part[:, start : start + size] for part in parts], axis=0)
 
-        both = dot(column(3 * hidden, width), column(0, 2 * hidden), 0, 0) / replicas
+        both = dot(column(3 * hidden, width), column(0, 2 * hidden), 0, 0) * (1.0 / replicas)
         gate_ref[...] = both[:, :hidden]
         up_ref[...] = both[:, hidden:]
         down = dot(column(3 * hidden + width, width), column(2 * hidden, hidden), 0, 0)
-        down_ref[...] = down / replicas
+        down_ref[...] = down * (1.0 / replicas)
 
     return grads_kernel
 

time: 41.6 us -> 41.6 us (level)
  no operation moved by 1% of the time
where the time goes in v6:
time: 41.6 us; the launch traced here: 41.4 us
  starting transfers between devices  26.5 us (64%)
  waiting for transfers between devices  9 us (22%)
  Pallas kernels  5.25 us (13%)
  between operations  0.7 us (2%)
    ppermute x7, starting transfers between devices, in_half(): return lax.ppermute(value, 'p', [(i, i ^ mask) for i in range(PARTS)])  11 us
    ppermute x4, starting transfers between devices, across_halves(): return lax.ppermute(value, 'q', [(0, 1), (1, 0)])  9.56 us
    pallas_call x8, Pallas kernels, call(): pl.pallas_call(kernel, out_shape=[jax.ShapeDtypeStruct(s, d) for s, d in...  5.25 us
    ppermute x4, waiting for transfers between devices, across_halves(): return lax.ppermute(value, 'q', [(0, 1), (1, 0)])  3.58 us
    all_to_all x1, starting transfers between devices, exchange(): lax.all_to_all(blocks, ('q', 'exp'), 0, 0, tiled=True).reshape(value.shape)  3.35 us
    ppermute x7, waiting for transfers between devices, in_half(): return lax.ppermute(value, 'p', [(i, i ^ mask) for i in range(PARTS)])  3.11 us
    ppermute x3, starting transfers between devices, body(): lax.ppermute(pieces[m], 'exp', [(i, i ^ m) for i in range(owners)])  2.52 us
    ppermute x3, waiting for transfers between devices, body(): lax.ppermute(pieces[m], 'exp', [(i, i ^ m) for i in range(owners)])  2.31 us
  transfers between devices with their start and end apart: 15, of which 7 were waited for; matrix products, arithmetic and copies ran while one was open for 0% of the time, Pallas kernels for 6%

profile of v6, /device:TPU:0, one launch (start us, length us, event | category | flops | bytes accessed | tf_op | source)
XLA Modules:
  0.0 41.4 jit_solution(9083431901946920563)
XLA Ops:
  0.6 1.4 %shard_map.110 = (bf16[128,1152]{1,0:T(8,128)(2,1)S(1)}, bf16[128,768]{1,0:T(8,128)(2,1)S(1)}, bf16[128,384]{1,0:T(8,128)(2,1)S(1)}, bf16[32,512]{1,0:T(8,128)(2...) custom-call(bf16[128,384]{1,0:T(8,128)(2,1)} %bitcast.23, ...), custom_call_target="tpu_custom_call" | custom-call | tf_op jit(solution)/shard_map/pallas_call | solution.py:27
  2.0 3.1 %collective-permute-start.2 = (bf16[128,1152]{1,0:T(8,128)(2,1)S(1)}, bf16[128,1152]{1,0:T(8,128)(2,1)S(1)}, u32[]{:S(2)}, u32[]{:S(2)}) collective-permute-start(bf16[128,1152]{1,0:T(8,128)(2,1)S(1)} %get-tuple-element.42), channel_id=1, source_target_pairs={{0,8},{4,12},{8,0},{12,4},{1,9},{5,13},{9,1},{13,5},{2,10},{6,14},... | collective-permute-start | bytes 884744 | tf_op jit(solution)/shard_map/ppermute | solution.py:231
  5.1 1.5 %collective-permute-start.1 = (bf16[128,1152]{1,0:T(8,128)(2,1)S(1)}, bf16[128,1152]{1,0:T(8,128)(2,1)S(1)}, u32[]{:S(2)}, u32[]{:S(2)}) collective-permute-start(bf16[128,1152]{1,0:T(8,128)(2,1)S(1)} %get-tuple-element.42), channel_id=1, source_target_pairs={{0,4},{4,0},{8,12},{12,8},{1,5},{5,1},{9,13},{13,9},{2,6},{6,2},{1... | collective-permute-start | bytes 884744 | tf_op jit(solution)/shard_map/ppermute | solution.py:231
  6.6 0.0 collective-permute-start.3
  6.6 3.0 %collective-permute-start = (bf16[32,512]{1,0:T(8,128)(2,1)S(1)}, bf16[32,512]{1,0:T(8,128)(2,1)S(1)}, u32[]{:S(2)}, u32[]{:S(2)}) collective-permute-start(bf16[32,512]{1,0:T(8,128)(2,1)S(1)} %get-tuple-element.40), channel_id=1, source_target_pairs={{0,16},{16,0},{1,17},{17,1},{2,18},{18,2},{3,19},{19,3},{4,20},{20... | collective-permute-start | bytes 98312 | tf_op jit(solution)/shard_map/ppermute | solution.py:234
  9.6 0.9 %shard_map.111 = (bf16[64,512]{1,0:T(8,128)(2,1)}, f32[32,128]{1,0:T(8,128)S(1)}) custom-call(s32[8,128]{1,0:T(8,128)S(1)} %get-tuple-element.35.ids_ref, bf16[8,128]{1,0:T(8,128)(2,1)S(1)} %get-tuple-element.36.scales_ref, bf16[128,1024]{1,0:T(8,128)(2,1)S(1)} %get-tuple-element.37.grads_ref), custom_call_target="tpu_custom_call" | custom-call | tf_op jit(solution)/shard_map/pallas_call | solution.py:27
  10.5 3.4 %all-to-all-start = ((bf16[8,8,512]{2,1,0:T(8,128)(2,1)}), bf16[8,8,512]{2,1,0:T(8,128)(2,1)S(1)}, u32[]{:S(2)}, u32[]{:S(2)}) async-start(bf16[8,8,512]{2,1,0:T(8,128)(2,1)} %bitcast.9), calls=%async_computation | async-start | bytes 131072 | tf_op jit(solution)/shard_map/all_to_all | solution.py:238
  13.9 2.6 %collective-permute-start.5 = (bf16[128,384]{1,0:T(8,128)(2,1)S(1)}, bf16[128,384]{1,0:T(8,128)(2,1)S(1)}, u32[]{:S(2)}, u32[]{:S(2)}) collective-permute-start(bf16[128,384]{1,0:T(8,128)(2,1)S(1)} %get-tuple-element.46.refs_0_), channel_id=1, source_target_pairs={{0,12},{4,8},{8,4},{12,0},{1,13},{5,9},{9,5},{13,1},{2,14},{6,10},... | collective-permute-start | bytes 294920 | tf_op jit(solution)/shard_map/ppermute | solution.py:231
  16.5 0.2 collective-permute-done.theirs_ref
  16.7 1.7 %collective-permute-done.3.refs_3_ = bf16[128,768]{1,0:T(8,128)(2,1)S(1)} collective-permute-done((bf16[128,768]{1,0:T(8,128)(2,1)S(1)}, bf16[128,768]{1,0:T(8,128)(2,1)S(1)}, u32[]{:S(2)}, u32[]{:S(2)}) %collective-permute-start.3) | collective-permute-done | bytes 196640 | tf_op jit(solution)/shard_map/ppermute | solution.py:231
  18.4 0.0 collective-permute-done.2.refs_2_
  18.4 0.0 collective-permute-done.1.refs_1_
  18.4 0.3 shard_map.112
  18.6 2.1 %collective-permute-start.4 = (bf16[64,768]{1,0:T(8,128)(2,1)S(1)}, bf16[64,768]{1,0:T(8,128)(2,1)S(1)}, u32[]{:S(2)}, u32[]{:S(2)}) collective-permute-start(bf16[64,768]{1,0:T(8,128)(2,1)S(1)} %get-tuple-element.44), channel_id=1, source_target_pairs={{0,16},{16,0},{1,17},{17,1},{2,18},{18,2},{3,19},{19,3},{4,20},{20... | collective-permute-start | bytes 294920 | tf_op jit(solution)/shard_map/ppermute | solution.py:234
  20.7 0.2 collective-permute-done.5.refs_3_
  20.9 0.0 all-to-all-done
  20.9 0.2 shard_map.113
  21.1 2.7 %collective-permute-start.6 = (bf16[64,384]{1,0:T(8,128)(2,1)S(1)}, bf16[64,384]{1,0:T(8,128)(2,1)S(1)}, u32[]{:S(2)}, u32[]{:S(2)}) collective-permute-start(bf16[64,384]{1,0:T(8,128)(2,1)S(1)} %get-tuple-element.48), channel_id=1, source_target_pairs={{0,16},{16,0},{1,17},{17,1},{2,18},{18,2},{3,19},{19,3},{4,20},{20... | collective-permute-start | bytes 147464 | tf_op jit(solution)/shard_map/ppermute | solution.py:234
  23.8 3.4 %collective-permute-done.6.down_other_ref = bf16[64,384]{1,0:T(8,128)(2,1)S(1)} collective-permute-done((bf16[64,384]{1,0:T(8,128)(2,1)S(1)}, bf16[64,384]{1,0:T(8,128)(2,1)S(1)}, u32[]{:S(2)}, u32[]{:S(2)}) %collective-permute-start.6) | collective-permute-done | bytes 49184 | tf_op jit(solution)/shard_map/ppermute | solution.py:234
  27.2 0.0 collective-permute-done.4.other_ref
  27.2 0.5 %shard_map.114 = (bf16[32,640]{1,0:T(8,128)(2,1)S(1)}, bf16[32,640]{1,0:T(8,128)(2,1)S(1)}, bf16[64,1408]{1,0:T(8,128)(2,1)S(1)}, bf16[64,1408]{1,0:T(8,128)(2,1...) custom-call(f32[64,768]{1,0:T(8,128)S(1)} %get-tuple-element.43.gate_up_ref, ...), custom_call_target="tpu_custom_call" | custom-call | tf_op jit(solution)/shard_map/pallas_call | solution.py:27
  27.7 1.8 %collective-permute-start.7 = (bf16[32,640]{1,0:T(8,128)(2,1)S(1)}, bf16[32,640]{1,0:T(8,128)(2,1)S(1)}, u32[]{:S(2)}, u32[]{:S(2)}) collective-permute-start(bf16[32,640]{1,0:T(8,128)(2,1)S(1)} %get-tuple-element.51), channel_id=1, source_target_pairs={{0,16},{16,0},{1,17},{17,1},{2,18},{18,2},{3,19},{19,3},{4,20},{20... | collective-permute-start | bytes 122888 | tf_op jit(solution)/shard_map/ppermute | solution.py:234
  29.5 3.0 %collective-permute-start.11 = (bf16[64,1408]{1,0:T(8,128)(2,1)S(1)}, bf16[64,1408]{1,0:T(8,128)(2,1)S(1)}, u32[]{:S(2)}, u32[]{:S(2)}) collective-permute-start(bf16[64,1408]{1,0:T(8,128)(2,1)S(1)} %get-tuple-element.59), channel_id=1, source_target_pairs={{0,12},{4,8},{8,4},{12,0},{1,13},{5,9},{9,5},{13,1},{2,14},{6,10},... | collective-permute-start | bytes 540680 | tf_op jit(solution)/shard_map/ppermute | solution.py:231
  32.5 0.8 %collective-permute-start.12 = (bf16[64,1408]{1,0:T(8,128)(2,1)S(1)}, bf16[64,1408]{1,0:T(8,128)(2,1)S(1)}, u32[]{:S(2)}, u32[]{:S(2)}) collective-permute-start(bf16[64,1408]{1,0:T(8,128)(2,1)S(1)} %get-tuple-element.60), channel_id=1, source_target_pairs={{0,4},{4,0},{8,12},{12,8},{1,5},{5,1},{9,13},{13,9},{2,6},{6,2},{1... | collective-permute-start | bytes 540680 | tf_op jit(solution)/shard_map/ppermute | solution.py:231
  33.3 0.0 collective-permute-start.13
  33.3 0.0 collective-permute-done.7.swap_ref
  33.4 0.1 collective-permute-start.8
  33.4 1.6 %collective-permute-start.9 = (bf16[8,1152]{1,0:T(8,128)(2,1)S(1)}, bf16[8,1152]{1,0:T(8,128)(2,1)S(1)}, u32[]{:S(2)}, u32[]{:S(2)}) collective-permute-start(bf16[8,1152]{1,0:T(8,128)(2,1)S(1)} %get-tuple-element.54), channel_id=1, source_target_pairs={{0,2},{1,3},{2,0},{3,1},{4,6},{5,7},{6,4},{7,5},{8,10},{9,11},{10,... | collective-permute-start | bytes 55304 | tf_op jit(solution)/shard_map/ppermute | solution.py:303
  35.0 0.0 collective-permute-done.8.refs_1_
  35.0 0.9 %collective-permute-start.10 = (bf16[8,1152]{1,0:T(8,128)(2,1)S(1)}, bf16[8,1152]{1,0:T(8,128)(2,1)S(1)}, u32[]{:S(2)}, u32[]{:S(2)}) collective-permute-start(bf16[8,1152]{1,0:T(8,128)(2,1)S(1)} %get-tuple-element.55), channel_id=1, source_target_pairs={{0,3},{1,2},{2,1},{3,0},{4,7},{5,6},{6,5},{7,4},{8,11},{9,10},{10,... | collective-permute-start | bytes 55304 | tf_op jit(solution)/shard_map/ppermute | solution.py:303
  35.9 1.4 %collective-permute-done.9.refs_2_ = bf16[8,1152]{1,0:T(8,128)(2,1)S(1)} collective-permute-done((bf16[8,1152]{1,0:T(8,128)(2,1)S(1)}, bf16[8,1152]{1,0:T(8,128)(2,1)S(1)}, u32[]{:S(2)}, u32[]{:S(2)}) %collective-permute-start.9) | collective-permute-done | bytes 18464 | tf_op jit(solution)/shard_map/ppermute | solution.py:303
  37.3 0.9 %collective-permute-done.10.refs_3_ = bf16[8,1152]{1,0:T(8,128)(2,1)S(1)} collective-permute-done((bf16[8,1152]{1,0:T(8,128)(2,1)S(1)}, bf16[8,1152]{1,0:T(8,128)(2,1)S(1)}, u32[]{:S(2)}, u32[]{:S(2)}) %collective-permute-start.10) | collective-permute-done | bytes 18464 | tf_op jit(solution)/shard_map/ppermute | solution.py:303
  38.2 1.0 %shard_map.116 = (bf16[128,1024]{1,0:T(8,128)(2,1)}, bf16[8,128]{1,0:T(8,128)(2,1)}) custom-call(s32[8,128]{1,0:T(8,128)S(1)} %get-tuple-element.35.ids_ref, bf16[8,128]{1,0:T(8,128)(2,1)S(1)} %get-tuple-element.36.scales_ref, f32[32,128]{1,0:T(8,128)S(1)} %get-tuple-element.38.hits_ref, bf16[8,1152]{1,0:T(8,128)(2,1)S(1)} %get-tuple-element.52.refs_0_, ...), custom_call_target="tpu_custom_call" | custom-call | tf_op jit(solution)/shard_map/pallas_call | solution.py:27
  39.2 0.0 collective-permute-done.11.refs_1_
  39.2 1.2 %collective-permute-done.12.refs_2_ = bf16[64,1408]{1,0:T(8,128)(2,1)S(1)} collective-permute-done((bf16[64,1408]{1,0:T(8,128)(2,1)S(1)}, bf16[64,1408]{1,0:T(8,128)(2,1)S(1)}, u32[]{:S(2)}, u32[]{:S(2)}) %collective-permute-start.12) | collective-permute-done | bytes 180256 | tf_op jit(solution)/shard_map/ppermute | solution.py:231
  40.4 0.0 collective-permute-done.13.refs_3_
  40.4 1.0 %shard_map.117 = (f32[128,384]{1,0:T(8,128)}, f32[128,384]{1,0:T(8,128)}, f32[128,384]{1,0:T(8,128)}) custom-call(bf16[64,1408]{1,0:T(8,128)(2,1)S(1)} %get-tuple-element.58.refs_0_, bf16[64,1408]{1,0:T(8,128)(2,1)S(1)} %collective-permute-done.11.refs_1_, bf16[64,1408]{1,0:T(8,128)(2,1)S(1)} %collective-permute-done.12.refs_2_, ...), custom_call_target="tpu_custom_call" | custom-call | tf_op jit(solution)/shard_map/pallas_call | solution.py:27
  (1 shorter events, 0.0 us)
Async XLA Ops:
  2.0 16.4 %collective-permute-start.2 = (bf16[128,1152]{1,0:T(8,128)(2,1)S(1)}, bf16[128,1152]{1,0:T(8,128)(2,1)S(1)}, u32[]{:S(2)}, u32[]{:S(2)}) collective-permute-start(bf16[128,1152]{1,0:T(8,128)(2,1)S(1)} %get-tuple-element.42), channel_id=1, source_target_pairs={{0,8},{4,12},{8,0},{12,4},{1,9},{5,13},{9,1},{13,5},{2,10},{6,14},... | collective-permute-start | bytes 884744 | tf_op jit(solution)/shard_map/ppermute | solution.py:231
  5.1 13.3 %collective-permute-start.1 = (bf16[128,1152]{1,0:T(8,128)(2,1)S(1)}, bf16[128,1152]{1,0:T(8,128)(2,1)S(1)}, u32[]{:S(2)}, u32[]{:S(2)}) collective-permute-start(bf16[128,1152]{1,0:T(8,128)(2,1)S(1)} %get-tuple-element.42), channel_id=1, source_target_pairs={{0,4},{4,0},{8,12},{12,8},{1,5},{5,1},{9,13},{13,9},{2,6},{6,2},{1... | collective-permute-start | bytes 884744 | tf_op jit(solution)/shard_map/ppermute | solution.py:231
  6.6 11.8 %collective-permute-start.3 = (bf16[128,768]{1,0:T(8,128)(2,1)S(1)}, bf16[128,768]{1,0:T(8,128)(2,1)S(1)}, u32[]{:S(2)}, u32[]{:S(2)}) collective-permute-start(bf16[128,768]{1,0:T(8,128)(2,1)S(1)} %get-tuple-element.41.refs_0_), channel_id=1, source_target_pairs={{0,12},{4,8},{8,4},{12,0},{1,13},{5,9},{9,5},{13,1},{2,14},{6,10},... | collective-permute-start | bytes 589832 | tf_op jit(solution)/shard_map/ppermute | solution.py:231
  6.6 10.0 %collective-permute-start = (bf16[32,512]{1,0:T(8,128)(2,1)S(1)}, bf16[32,512]{1,0:T(8,128)(2,1)S(1)}, u32[]{:S(2)}, u32[]{:S(2)}) collective-permute-start(bf16[32,512]{1,0:T(8,128)(2,1)S(1)} %get-tuple-element.40), channel_id=1, source_target_pairs={{0,16},{16,0},{1,17},{17,1},{2,18},{18,2},{3,19},{19,3},{4,20},{20... | collective-permute-start | bytes 98312 | tf_op jit(solution)/shard_map/ppermute | solution.py:234
  10.5 10.4 %all-to-all-start = ((bf16[8,8,512]{2,1,0:T(8,128)(2,1)}), bf16[8,8,512]{2,1,0:T(8,128)(2,1)S(1)}, u32[]{:S(2)}, u32[]{:S(2)}) async-start(bf16[8,8,512]{2,1,0:T(8,128)(2,1)} %bitcast.9), calls=%async_computation | async-start | bytes 131072 | tf_op jit(solution)/shard_map/all_to_all | solution.py:238
  13.9 7.0 %collective-permute-start.5 = (bf16[128,384]{1,0:T(8,128)(2,1)S(1)}, bf16[128,384]{1,0:T(8,128)(2,1)S(1)}, u32[]{:S(2)}, u32[]{:S(2)}) collective-permute-start(bf16[128,384]{1,0:T(8,128)(2,1)S(1)} %get-tuple-element.46.refs_0_), channel_id=1, source_target_pairs={{0,12},{4,8},{8,4},{12,0},{1,13},{5,9},{9,5},{13,1},{2,14},{6,10},... | collective-permute-start | bytes 294920 | tf_op jit(solution)/shard_map/ppermute | solution.py:231
  18.6 8.6 %collective-permute-start.4 = (bf16[64,768]{1,0:T(8,128)(2,1)S(1)}, bf16[64,768]{1,0:T(8,128)(2,1)S(1)}, u32[]{:S(2)}, u32[]{:S(2)}) collective-permute-start(bf16[64,768]{1,0:T(8,128)(2,1)S(1)} %get-tuple-element.44), channel_id=1, source_target_pairs={{0,16},{16,0},{1,17},{17,1},{2,18},{18,2},{3,19},{19,3},{4,20},{20... | collective-permute-start | bytes 294920 | tf_op jit(solution)/shard_map/ppermute | solution.py:234
  21.1 6.1 %collective-permute-start.6 = (bf16[64,384]{1,0:T(8,128)(2,1)S(1)}, bf16[64,384]{1,0:T(8,128)(2,1)S(1)}, u32[]{:S(2)}, u32[]{:S(2)}) collective-permute-start(bf16[64,384]{1,0:T(8,128)(2,1)S(1)} %get-tuple-element.48), channel_id=1, source_target_pairs={{0,16},{16,0},{1,17},{17,1},{2,18},{18,2},{3,19},{19,3},{4,20},{20... | collective-permute-start | bytes 147464 | tf_op jit(solution)/shard_map/ppermute | solution.py:234
  27.7 5.6 %collective-permute-start.7 = (bf16[32,640]{1,0:T(8,128)(2,1)S(1)}, bf16[32,640]{1,0:T(8,128)(2,1)S(1)}, u32[]{:S(2)}, u32[]{:S(2)}) collective-permute-start(bf16[32,640]{1,0:T(8,128)(2,1)S(1)} %get-tuple-element.51), channel_id=1, source_target_pairs={{0,16},{16,0},{1,17},{17,1},{2,18},{18,2},{3,19},{19,3},{4,20},{20... | collective-permute-start | bytes 122888 | tf_op jit(solution)/shard_map/ppermute | solution.py:234
  29.5 9.7 %collective-permute-start.11 = (bf16[64,1408]{1,0:T(8,128)(2,1)S(1)}, bf16[64,1408]{1,0:T(8,128)(2,1)S(1)}, u32[]{:S(2)}, u32[]{:S(2)}) collective-permute-start(bf16[64,1408]{1,0:T(8,128)(2,1)S(1)} %get-tuple-element.59), channel_id=1, source_target_pairs={{0,12},{4,8},{8,4},{12,0},{1,13},{5,9},{9,5},{13,1},{2,14},{6,10},... | collective-permute-start | bytes 540680 | tf_op jit(solution)/shard_map/ppermute | solution.py:231
  32.5 7.9 %collective-permute-start.12 = (bf16[64,1408]{1,0:T(8,128)(2,1)S(1)}, bf16[64,1408]{1,0:T(8,128)(2,1)S(1)}, u32[]{:S(2)}, u32[]{:S(2)}) collective-permute-start(bf16[64,1408]{1,0:T(8,128)(2,1)S(1)} %get-tuple-element.60), channel_id=1, source_target_pairs={{0,4},{4,0},{8,12},{12,8},{1,5},{5,1},{9,13},{13,9},{2,6},{6,2},{1... | collective-permute-start | bytes 540680 | tf_op jit(solution)/shard_map/ppermute | solution.py:231
  33.3 7.1 %collective-permute-start.13 = (bf16[64,1408]{1,0:T(8,128)(2,1)S(1)}, bf16[64,1408]{1,0:T(8,128)(2,1)S(1)}, u32[]{:S(2)}, u32[]{:S(2)}) collective-permute-start(bf16[64,1408]{1,0:T(8,128)(2,1)S(1)} %get-tuple-element.61), channel_id=1, source_target_pairs={{0,8},{4,12},{8,0},{12,4},{1,9},{5,13},{9,1},{13,5},{2,10},{6,14},... | collective-permute-start | bytes 540680 | tf_op jit(solution)/shard_map/ppermute | solution.py:231
  33.4 1.7 %collective-permute-start.8 = (bf16[8,1152]{1,0:T(8,128)(2,1)S(1)}, bf16[8,1152]{1,0:T(8,128)(2,1)S(1)}, u32[]{:S(2)}, u32[]{:S(2)}) collective-permute-start(bf16[8,1152]{1,0:T(8,128)(2,1)S(1)} %get-tuple-element.53), channel_id=1, source_target_pairs={{0,1},{1,0},{2,3},{3,2},{4,5},{5,4},{6,7},{7,6},{8,9},{9,8},{10,11... | collective-permute-start | bytes 55304 | tf_op jit(solution)/shard_map/ppermute | solution.py:303
  33.4 3.8 %collective-permute-start.9 = (bf16[8,1152]{1,0:T(8,128)(2,1)S(1)}, bf16[8,1152]{1,0:T(8,128)(2,1)S(1)}, u32[]{:S(2)}, u32[]{:S(2)}) collective-permute-start(bf16[8,1152]{1,0:T(8,128)(2,1)S(1)} %get-tuple-element.54), channel_id=1, source_target_pairs={{0,2},{1,3},{2,0},{3,1},{4,6},{5,7},{6,4},{7,5},{8,10},{9,11},{10,... | collective-permute-start | bytes 55304 | tf_op jit(solution)/shard_map/ppermute | solution.py:303
  35.0 3.2 %collective-permute-start.10 = (bf16[8,1152]{1,0:T(8,128)(2,1)S(1)}, bf16[8,1152]{1,0:T(8,128)(2,1)S(1)}, u32[]{:S(2)}, u32[]{:S(2)}) collective-permute-start(bf16[8,1152]{1,0:T(8,128)(2,1)S(1)} %get-tuple-element.55), channel_id=1, source_target_pairs={{0,3},{1,2},{2,1},{3,0},{4,7},{5,6},{6,5},{7,4},{8,11},{9,10},{10,... | collective-permute-start | bytes 55304 | tf_op jit(solution)/shard_map/ppermute | solution.py:303

commit v7 on v5

--- a/solution.py
+++ b/solution.py
@@ -303,7 +303,7 @@
         lax.ppermute(pieces[m], "exp", [(i, i ^ m) for i in range(owners)])
         for m in range(1, owners)
     ]
-    sends = [sends[0]] + [in_half(sends[k], k) for k in (3, 1, 2)]
+    sends = [sends[0]] + [in_half(sends[k], k) for k in (3, 2, 1)]
     gate_grad, up_grad, down_grad = call(
         grads_step(replicas), *sends, out=[((width, hidden_width), F32)] * 3
     )

time: 41.6 us -> 41.6 us (level)
  transfers between devices with their start and end apart: 15 -> 15, of which waited for: 7 -> 8; matrix products, arithmetic and copies ran while one was open for 0% -> 0% of each run, Pallas kernels for 6% -> 6%
where the time goes in v7:
time: 41.6 us; the launch traced here: 41.4 us
  starting transfers between devices  26.5 us (64%)
  waiting for transfers between devices  9 us (22%)
  Pallas kernels  5.25 us (13%)
  between operations  0.7 us (2%)
    ppermute x7, starting transfers between devices, in_half(): return lax.ppermute(value, 'p', [(i, i ^ mask) for i in range(PARTS)])  11 us
    ppermute x4, starting transfers between devices, across_halves(): return lax.ppermute(value, 'q', [(0, 1), (1, 0)])  9.56 us
    pallas_call x8, Pallas kernels, call(): pl.pallas_call(kernel, out_shape=[jax.ShapeDtypeStruct(s, d) for s, d in...  5.25 us
    ppermute x4, waiting for transfers between devices, across_halves(): return lax.ppermute(value, 'q', [(0, 1), (1, 0)])  3.58 us
    all_to_all x1, starting transfers between devices, exchange(): lax.all_to_all(blocks, ('q', 'exp'), 0, 0, tiled=True).reshape(value.shape)  3.35 us
    ppermute x7, waiting for transfers between devices, in_half(): return lax.ppermute(value, 'p', [(i, i ^ mask) for i in range(PARTS)])  3.1 us
    ppermute x3, starting transfers between devices, body(): lax.ppermute(pieces[m], 'exp', [(i, i ^ m) for i in range(owners)])  2.52 us
    ppermute x3, waiting for transfers between devices, body(): lax.ppermute(pieces[m], 'exp', [(i, i ^ m) for i in range(owners)])  2.31 us
  transfers between devices with their start and end apart: 15, of which 8 were waited for; matrix products, arithmetic and copies ran while one was open for 0% of the time, Pallas kernels for 6%

profile of v7, /device:TPU:0, one launch (start us, length us, event | category | flops | bytes accessed | tf_op | source)
XLA Modules:
  0.0 41.4 jit_solution(11225091648402008161)
XLA Ops:
  0.6 1.4 %shard_map.110 = (bf16[128,1152]{1,0:T(8,128)(2,1)S(1)}, bf16[128,768]{1,0:T(8,128)(2,1)S(1)}, bf16[128,384]{1,0:T(8,128)(2,1)S(1)}, bf16[32,512]{1,0:T(8,128)(2...) custom-call(bf16[128,384]{1,0:T(8,128)(2,1)} %bitcast.23, ...), custom_call_target="tpu_custom_call" | custom-call | tf_op jit(solution)/shard_map/pallas_call | solution.py:27
  2.0 3.1 %collective-permute-start.2 = (bf16[128,1152]{1,0:T(8,128)(2,1)S(1)}, bf16[128,1152]{1,0:T(8,128)(2,1)S(1)}, u32[]{:S(2)}, u32[]{:S(2)}) collective-permute-start(bf16[128,1152]{1,0:T(8,128)(2,1)S(1)} %get-tuple-element.42), channel_id=1, source_target_pairs={{0,8},{4,12},{8,0},{12,4},{1,9},{5,13},{9,1},{13,5},{2,10},{6,14},... | collective-permute-start | bytes 884744 | tf_op jit(solution)/shard_map/ppermute | solution.py:231
  5.1 1.5 %collective-permute-start.1 = (bf16[128,1152]{1,0:T(8,128)(2,1)S(1)}, bf16[128,1152]{1,0:T(8,128)(2,1)S(1)}, u32[]{:S(2)}, u32[]{:S(2)}) collective-permute-start(bf16[128,1152]{1,0:T(8,128)(2,1)S(1)} %get-tuple-element.42), channel_id=1, source_target_pairs={{0,4},{4,0},{8,12},{12,8},{1,5},{5,1},{9,13},{13,9},{2,6},{6,2},{1... | collective-permute-start | bytes 884744 | tf_op jit(solution)/shard_map/ppermute | solution.py:231
  6.6 0.0 collective-permute-start.3
  6.6 3.0 %collective-permute-start = (bf16[32,512]{1,0:T(8,128)(2,1)S(1)}, bf16[32,512]{1,0:T(8,128)(2,1)S(1)}, u32[]{:S(2)}, u32[]{:S(2)}) collective-permute-start(bf16[32,512]{1,0:T(8,128)(2,1)S(1)} %get-tuple-element.40), channel_id=1, source_target_pairs={{0,16},{16,0},{1,17},{17,1},{2,18},{18,2},{3,19},{19,3},{4,20},{20... | collective-permute-start | bytes 98312 | tf_op jit(solution)/shard_map/ppermute | solution.py:234
  9.6 0.9 %shard_map.111 = (bf16[64,512]{1,0:T(8,128)(2,1)}, f32[32,128]{1,0:T(8,128)S(1)}) custom-call(s32[8,128]{1,0:T(8,128)S(1)} %get-tuple-element.35.ids_ref, bf16[8,128]{1,0:T(8,128)(2,1)S(1)} %get-tuple-element.36.scales_ref, bf16[128,1024]{1,0:T(8,128)(2,1)S(1)} %get-tuple-element.37.grads_ref), custom_call_target="tpu_custom_call" | custom-call | tf_op jit(solution)/shard_map/pallas_call | solution.py:27
  10.5 3.4 %all-to-all-start = ((bf16[8,8,512]{2,1,0:T(8,128)(2,1)}), bf16[8,8,512]{2,1,0:T(8,128)(2,1)S(1)}, u32[]{:S(2)}, u32[]{:S(2)}) async-start(bf16[8,8,512]{2,1,0:T(8,128)(2,1)} %bitcast.9), calls=%async_computation | async-start | bytes 131072 | tf_op jit(solution)/shard_map/all_to_all | solution.py:238
  13.9 2.6 %collective-permute-start.5 = (bf16[128,384]{1,0:T(8,128)(2,1)S(1)}, bf16[128,384]{1,0:T(8,128)(2,1)S(1)}, u32[]{:S(2)}, u32[]{:S(2)}) collective-permute-start(bf16[128,384]{1,0:T(8,128)(2,1)S(1)} %get-tuple-element.46.refs_0_), channel_id=1, source_target_pairs={{0,12},{4,8},{8,4},{12,0},{1,13},{5,9},{9,5},{13,1},{2,14},{6,10},... | collective-permute-start | bytes 294920 | tf_op jit(solution)/shard_map/ppermute | solution.py:231
  16.5 0.2 collective-permute-done.theirs_ref
  16.7 1.7 %collective-permute-done.3.refs_3_ = bf16[128,768]{1,0:T(8,128)(2,1)S(1)} collective-permute-done((bf16[128,768]{1,0:T(8,128)(2,1)S(1)}, bf16[128,768]{1,0:T(8,128)(2,1)S(1)}, u32[]{:S(2)}, u32[]{:S(2)}) %collective-permute-start.3) | collective-permute-done | bytes 196640 | tf_op jit(solution)/shard_map/ppermute | solution.py:231
  18.4 0.0 collective-permute-done.2.refs_2_
  18.4 0.0 collective-permute-done.1.refs_1_
  18.4 0.3 shard_map.112
  18.6 2.1 %collective-permute-start.4 = (bf16[64,768]{1,0:T(8,128)(2,1)S(1)}, bf16[64,768]{1,0:T(8,128)(2,1)S(1)}, u32[]{:S(2)}, u32[]{:S(2)}) collective-permute-start(bf16[64,768]{1,0:T(8,128)(2,1)S(1)} %get-tuple-element.44), channel_id=1, source_target_pairs={{0,16},{16,0},{1,17},{17,1},{2,18},{18,2},{3,19},{19,3},{4,20},{20... | collective-permute-start | bytes 294920 | tf_op jit(solution)/shard_map/ppermute | solution.py:234
  20.7 0.2 collective-permute-done.5.refs_3_
  20.9 0.0 all-to-all-done
  20.9 0.2 shard_map.113
  21.1 2.7 %collective-permute-start.6 = (bf16[64,384]{1,0:T(8,128)(2,1)S(1)}, bf16[64,384]{1,0:T(8,128)(2,1)S(1)}, u32[]{:S(2)}, u32[]{:S(2)}) collective-permute-start(bf16[64,384]{1,0:T(8,128)(2,1)S(1)} %get-tuple-element.48), channel_id=1, source_target_pairs={{0,16},{16,0},{1,17},{17,1},{2,18},{18,2},{3,19},{19,3},{4,20},{20... | collective-permute-start | bytes 147464 | tf_op jit(solution)/shard_map/ppermute | solution.py:234
  23.8 3.4 %collective-permute-done.6.down_other_ref = bf16[64,384]{1,0:T(8,128)(2,1)S(1)} collective-permute-done((bf16[64,384]{1,0:T(8,128)(2,1)S(1)}, bf16[64,384]{1,0:T(8,128)(2,1)S(1)}, u32[]{:S(2)}, u32[]{:S(2)}) %collective-permute-start.6) | collective-permute-done | bytes 49184 | tf_op jit(solution)/shard_map/ppermute | solution.py:234
  27.2 0.0 collective-permute-done.4.other_ref
  27.2 0.5 %shard_map.114 = (bf16[32,640]{1,0:T(8,128)(2,1)S(1)}, bf16[32,640]{1,0:T(8,128)(2,1)S(1)}, bf16[64,1408]{1,0:T(8,128)(2,1)S(1)}, bf16[64,1408]{1,0:T(8,128)(2,1...) custom-call(f32[64,768]{1,0:T(8,128)S(1)} %get-tuple-element.43.gate_up_ref, ...), custom_call_target="tpu_custom_call" | custom-call | tf_op jit(solution)/shard_map/pallas_call | solution.py:27
  27.7 1.8 %collective-permute-start.7 = (bf16[32,640]{1,0:T(8,128)(2,1)S(1)}, bf16[32,640]{1,0:T(8,128)(2,1)S(1)}, u32[]{:S(2)}, u32[]{:S(2)}) collective-permute-start(bf16[32,640]{1,0:T(8,128)(2,1)S(1)} %get-tuple-element.51), channel_id=1, source_target_pairs={{0,16},{16,0},{1,17},{17,1},{2,18},{18,2},{3,19},{19,3},{4,20},{20... | collective-permute-start | bytes 122888 | tf_op jit(solution)/shard_map/ppermute | solution.py:234
  29.5 3.0 %collective-permute-start.11 = (bf16[64,1408]{1,0:T(8,128)(2,1)S(1)}, bf16[64,1408]{1,0:T(8,128)(2,1)S(1)}, u32[]{:S(2)}, u32[]{:S(2)}) collective-permute-start(bf16[64,1408]{1,0:T(8,128)(2,1)S(1)} %get-tuple-element.59), channel_id=1, source_target_pairs={{0,12},{4,8},{8,4},{12,0},{1,13},{5,9},{9,5},{13,1},{2,14},{6,10},... | collective-permute-start | bytes 540680 | tf_op jit(solution)/shard_map/ppermute | solution.py:231
  32.5 0.0 collective-permute-start.12
  32.5 0.8 %collective-permute-start.13 = (bf16[64,1408]{1,0:T(8,128)(2,1)S(1)}, bf16[64,1408]{1,0:T(8,128)(2,1)S(1)}, u32[]{:S(2)}, u32[]{:S(2)}) collective-permute-start(bf16[64,1408]{1,0:T(8,128)(2,1)S(1)} %get-tuple-element.61), channel_id=1, source_target_pairs={{0,4},{4,0},{8,12},{12,8},{1,5},{5,1},{9,13},{13,9},{2,6},{6,2},{1... | collective-permute-start | bytes 540680 | tf_op jit(solution)/shard_map/ppermute | solution.py:231
  33.3 0.0 collective-permute-done.7.swap_ref
  33.4 0.1 collective-permute-start.8
  33.4 1.6 %collective-permute-start.9 = (bf16[8,1152]{1,0:T(8,128)(2,1)S(1)}, bf16[8,1152]{1,0:T(8,128)(2,1)S(1)}, u32[]{:S(2)}, u32[]{:S(2)}) collective-permute-start(bf16[8,1152]{1,0:T(8,128)(2,1)S(1)} %get-tuple-element.54), channel_id=1, source_target_pairs={{0,2},{1,3},{2,0},{3,1},{4,6},{5,7},{6,4},{7,5},{8,10},{9,11},{10,... | collective-permute-start | bytes 55304 | tf_op jit(solution)/shard_map/ppermute | solution.py:303
  35.0 0.0 collective-permute-done.8.refs_1_
  35.0 0.9 %collective-permute-start.10 = (bf16[8,1152]{1,0:T(8,128)(2,1)S(1)}, bf16[8,1152]{1,0:T(8,128)(2,1)S(1)}, u32[]{:S(2)}, u32[]{:S(2)}) collective-permute-start(bf16[8,1152]{1,0:T(8,128)(2,1)S(1)} %get-tuple-element.55), channel_id=1, source_target_pairs={{0,3},{1,2},{2,1},{3,0},{4,7},{5,6},{6,5},{7,4},{8,11},{9,10},{10,... | collective-permute-start | bytes 55304 | tf_op jit(solution)/shard_map/ppermute | solution.py:303
  35.9 1.4 %collective-permute-done.9.refs_2_ = bf16[8,1152]{1,0:T(8,128)(2,1)S(1)} collective-permute-done((bf16[8,1152]{1,0:T(8,128)(2,1)S(1)}, bf16[8,1152]{1,0:T(8,128)(2,1)S(1)}, u32[]{:S(2)}, u32[]{:S(2)}) %collective-permute-start.9) | collective-permute-done | bytes 18464 | tf_op jit(solution)/shard_map/ppermute | solution.py:303
  37.3 0.9 %collective-permute-done.10.refs_3_ = bf16[8,1152]{1,0:T(8,128)(2,1)S(1)} collective-permute-done((bf16[8,1152]{1,0:T(8,128)(2,1)S(1)}, bf16[8,1152]{1,0:T(8,128)(2,1)S(1)}, u32[]{:S(2)}, u32[]{:S(2)}) %collective-permute-start.10) | collective-permute-done | bytes 18464 | tf_op jit(solution)/shard_map/ppermute | solution.py:303
  38.2 1.0 %shard_map.116 = (bf16[128,1024]{1,0:T(8,128)(2,1)}, bf16[8,128]{1,0:T(8,128)(2,1)}) custom-call(s32[8,128]{1,0:T(8,128)S(1)} %get-tuple-element.35.ids_ref, bf16[8,128]{1,0:T(8,128)(2,1)S(1)} %get-tuple-element.36.scales_ref, f32[32,128]{1,0:T(8,128)S(1)} %get-tuple-element.38.hits_ref, bf16[8,1152]{1,0:T(8,128)(2,1)S(1)} %get-tuple-element.52.refs_0_, ...), custom_call_target="tpu_custom_call" | custom-call | tf_op jit(solution)/shard_map/pallas_call | solution.py:27
  39.2 0.0 collective-permute-done.11.refs_1_
  39.2 0.3 collective-permute-done.12.refs_2_
  39.5 0.9 %collective-permute-done.13.refs_3_ = bf16[64,1408]{1,0:T(8,128)(2,1)S(1)} collective-permute-done((bf16[64,1408]{1,0:T(8,128)(2,1)S(1)}, bf16[64,1408]{1,0:T(8,128)(2,1)S(1)}, u32[]{:S(2)}, u32[]{:S(2)}) %collective-permute-start.13) | collective-permute-done | bytes 180256 | tf_op jit(solution)/shard_map/ppermute | solution.py:231
  40.4 1.0 %shard_map.117 = (f32[128,384]{1,0:T(8,128)}, f32[128,384]{1,0:T(8,128)}, f32[128,384]{1,0:T(8,128)}) custom-call(bf16[64,1408]{1,0:T(8,128)(2,1)S(1)} %get-tuple-element.58.refs_0_, bf16[64,1408]{1,0:T(8,128)(2,1)S(1)} %collective-permute-done.11.refs_1_, bf16[64,1408]{1,0:T(8,128)(2,1)S(1)} %collective-permute-done.12.refs_2_, ...), custom_call_target="tpu_custom_call" | custom-call | tf_op jit(solution)/shard_map/pallas_call | solution.py:27
  (1 shorter events, 0.0 us)
Async XLA Ops:
  2.0 16.4 %collective-permute-start.2 = (bf16[128,1152]{1,0:T(8,128)(2,1)S(1)}, bf16[128,1152]{1,0:T(8,128)(2,1)S(1)}, u32[]{:S(2)}, u32[]{:S(2)}) collective-permute-start(bf16[128,1152]{1,0:T(8,128)(2,1)S(1)} %get-tuple-element.42), channel_id=1, source_target_pairs={{0,8},{4,12},{8,0},{12,4},{1,9},{5,13},{9,1},{13,5},{2,10},{6,14},... | collective-permute-start | bytes 884744 | tf_op jit(solution)/shard_map/ppermute | solution.py:231
  5.1 13.3 %collective-permute-start.1 = (bf16[128,1152]{1,0:T(8,128)(2,1)S(1)}, bf16[128,1152]{1,0:T(8,128)(2,1)S(1)}, u32[]{:S(2)}, u32[]{:S(2)}) collective-permute-start(bf16[128,1152]{1,0:T(8,128)(2,1)S(1)} %get-tuple-element.42), channel_id=1, source_target_pairs={{0,4},{4,0},{8,12},{12,8},{1,5},{5,1},{9,13},{13,9},{2,6},{6,2},{1... | collective-permute-start | bytes 884744 | tf_op jit(solution)/shard_map/ppermute | solution.py:231
  6.6 11.8 %collective-permute-start.3 = (bf16[128,768]{1,0:T(8,128)(2,1)S(1)}, bf16[128,768]{1,0:T(8,128)(2,1)S(1)}, u32[]{:S(2)}, u32[]{:S(2)}) collective-permute-start(bf16[128,768]{1,0:T(8,128)(2,1)S(1)} %get-tuple-element.41.refs_0_), channel_id=1, source_target_pairs={{0,12},{4,8},{8,4},{12,0},{1,13},{5,9},{9,5},{13,1},{2,14},{6,10},... | collective-permute-start | bytes 589832 | tf_op jit(solution)/shard_map/ppermute | solution.py:231
  6.6 10.0 %collective-permute-start = (bf16[32,512]{1,0:T(8,128)(2,1)S(1)}, bf16[32,512]{1,0:T(8,128)(2,1)S(1)}, u32[]{:S(2)}, u32[]{:S(2)}) collective-permute-start(bf16[32,512]{1,0:T(8,128)(2,1)S(1)} %get-tuple-element.40), channel_id=1, source_target_pairs={{0,16},{16,0},{1,17},{17,1},{2,18},{18,2},{3,19},{19,3},{4,20},{20... | collective-permute-start | bytes 98312 | tf_op jit(solution)/shard_map/ppermute | solution.py:234
  10.5 10.4 %all-to-all-start = ((bf16[8,8,512]{2,1,0:T(8,128)(2,1)}), bf16[8,8,512]{2,1,0:T(8,128)(2,1)S(1)}, u32[]{:S(2)}, u32[]{:S(2)}) async-start(bf16[8,8,512]{2,1,0:T(8,128)(2,1)} %bitcast.9), calls=%async_computation | async-start | bytes 131072 | tf_op jit(solution)/shard_map/all_to_all | solution.py:238
  13.9 7.0 %collective-permute-start.5 = (bf16[128,384]{1,0:T(8,128)(2,1)S(1)}, bf16[128,384]{1,0:T(8,128)(2,1)S(1)}, u32[]{:S(2)}, u32[]{:S(2)}) collective-permute-start(bf16[128,384]{1,0:T(8,128)(2,1)S(1)} %get-tuple-element.46.refs_0_), channel_id=1, source_target_pairs={{0,12},{4,8},{8,4},{12,0},{1,13},{5,9},{9,5},{13,1},{2,14},{6,10},... | collective-permute-start | bytes 294920 | tf_op jit(solution)/shard_map/ppermute | solution.py:231
  18.6 8.6 %collective-permute-start.4 = (bf16[64,768]{1,0:T(8,128)(2,1)S(1)}, bf16[64,768]{1,0:T(8,128)(2,1)S(1)}, u32[]{:S(2)}, u32[]{:S(2)}) collective-permute-start(bf16[64,768]{1,0:T(8,128)(2,1)S(1)} %get-tuple-element.44), channel_id=1, source_target_pairs={{0,16},{16,0},{1,17},{17,1},{2,18},{18,2},{3,19},{19,3},{4,20},{20... | collective-permute-start | bytes 294920 | tf_op jit(solution)/shard_map/ppermute | solution.py:234
  21.1 6.1 %collective-permute-start.6 = (bf16[64,384]{1,0:T(8,128)(2,1)S(1)}, bf16[64,384]{1,0:T(8,128)(2,1)S(1)}, u32[]{:S(2)}, u32[]{:S(2)}) collective-permute-start(bf16[64,384]{1,0:T(8,128)(2,1)S(1)} %get-tuple-element.48), channel_id=1, source_target_pairs={{0,16},{16,0},{1,17},{17,1},{2,18},{18,2},{3,19},{19,3},{4,20},{20... | collective-permute-start | bytes 147464 | tf_op jit(solution)/shard_map/ppermute | solution.py:234
  27.7 5.6 %collective-permute-start.7 = (bf16[32,640]{1,0:T(8,128)(2,1)S(1)}, bf16[32,640]{1,0:T(8,128)(2,1)S(1)}, u32[]{:S(2)}, u32[]{:S(2)}) collective-permute-start(bf16[32,640]{1,0:T(8,128)(2,1)S(1)} %get-tuple-element.51), channel_id=1, source_target_pairs={{0,16},{16,0},{1,17},{17,1},{2,18},{18,2},{3,19},{19,3},{4,20},{20... | collective-permute-start | bytes 122888 | tf_op jit(solution)/shard_map/ppermute | solution.py:234
  29.5 9.7 %collective-permute-start.11 = (bf16[64,1408]{1,0:T(8,128)(2,1)S(1)}, bf16[64,1408]{1,0:T(8,128)(2,1)S(1)}, u32[]{:S(2)}, u32[]{:S(2)}) collective-permute-start(bf16[64,1408]{1,0:T(8,128)(2,1)S(1)} %get-tuple-element.59), channel_id=1, source_target_pairs={{0,12},{4,8},{8,4},{12,0},{1,13},{5,9},{9,5},{13,1},{2,14},{6,10},... | collective-permute-start | bytes 540680 | tf_op jit(solution)/shard_map/ppermute | solution.py:231
  32.5 6.9 %collective-permute-start.12 = (bf16[64,1408]{1,0:T(8,128)(2,1)S(1)}, bf16[64,1408]{1,0:T(8,128)(2,1)S(1)}, u32[]{:S(2)}, u32[]{:S(2)}) collective-permute-start(bf16[64,1408]{1,0:T(8,128)(2,1)S(1)} %get-tuple-element.60), channel_id=1, source_target_pairs={{0,8},{4,12},{8,0},{12,4},{1,9},{5,13},{9,1},{13,5},{2,10},{6,14},... | collective-permute-start | bytes 540680 | tf_op jit(solution)/shard_map/ppermute | solution.py:231
  32.5 7.8 %collective-permute-start.13 = (bf16[64,1408]{1,0:T(8,128)(2,1)S(1)}, bf16[64,1408]{1,0:T(8,128)(2,1)S(1)}, u32[]{:S(2)}, u32[]{:S(2)}) collective-permute-start(bf16[64,1408]{1,0:T(8,128)(2,1)S(1)} %get-tuple-element.61), channel_id=1, source_target_pairs={{0,4},{4,0},{8,12},{12,8},{1,5},{5,1},{9,13},{13,9},{2,6},{6,2},{1... | collective-permute-start | bytes 540680 | tf_op jit(solution)/shard_map/ppermute | solution.py:231
  33.4 1.7 %collective-permute-start.8 = (bf16[8,1152]{1,0:T(8,128)(2,1)S(1)}, bf16[8,1152]{1,0:T(8,128)(2,1)S(1)}, u32[]{:S(2)}, u32[]{:S(2)}) collective-permute-start(bf16[8,1152]{1,0:T(8,128)(2,1)S(1)} %get-tuple-element.53), channel_id=1, source_target_pairs={{0,1},{1,0},{2,3},{3,2},{4,5},{5,4},{6,7},{7,6},{8,9},{9,8},{10,11... | collective-permute-start | bytes 55304 | tf_op jit(solution)/shard_map/ppermute | solution.py:303
  33.4 3.8 %collective-permute-start.9 = (bf16[8,1152]{1,0:T(8,128)(2,1)S(1)}, bf16[8,1152]{1,0:T(8,128)(2,1)S(1)}, u32[]{:S(2)}, u32[]{:S(2)}) collective-permute-start(bf16[8,1152]{1,0:T(8,128)(2,1)S(1)} %get-tuple-element.54), channel_id=1, source_target_pairs={{0,2},{1,3},{2,0},{3,1},{4,6},{5,7},{6,4},{7,5},{8,10},{9,11},{10,... | collective-permute-start | bytes 55304 | tf_op jit(solution)/shard_map/ppermute | solution.py:303
  35.0 3.2 %collective-permute-start.10 = (bf16[8,1152]{1,0:T(8,128)(2,1)S(1)}, bf16[8,1152]{1,0:T(8,128)(2,1)S(1)}, u32[]{:S(2)}, u32[]{:S(2)}) collective-permute-start(bf16[8,1152]{1,0:T(8,128)(2,1)S(1)} %get-tuple-element.55), channel_id=1, source_target_pairs={{0,3},{1,2},{2,1},{3,0},{4,7},{5,6},{6,5},{7,4},{8,11},{9,10},{10,... | collective-permute-start | bytes 55304 | tf_op jit(solution)/shard_map/ppermute | solution.py:303
